TPU v7x, 512 devices: a whole 4x4x16 slice. The times are simulated.
512 devices in a mesh: seq: 4 (over z_lo), fsdp: 32 (over z_hi, y, core), dp: 4 (over x).
Axes of the slice: x: 4, y: 4, z: 16 (z_hi: 4, z_lo: 4; z = z_hi * 4 + z_lo), core: 2. Of those that a mesh axis runs over, the one named last changes fastest.
Arguments:
- query: bfloat16 [128, 768, 1024], P(('fsdp', 'dp'), 'seq'), may hold values from -6 to 6
- key: bfloat16 [128, 768, 1024], P(('fsdp', 'dp'), 'seq'), may hold values from -6 to 6
- value: bfloat16 [128, 768, 1024], P(('fsdp', 'dp'), 'seq'), may hold values from -4 to 4
- out_weight: bfloat16 [1024, 2048], P('fsdp'), may hold values from -0.1875 to 0.1875
- out_grad: bfloat16 [128, 768, 2048], P(('fsdp', 'dp'), 'seq'), may hold values from -5 to 5
- block_ids: int32 [8], P('seq'), may hold values from 0 to 7, as said below
Outputs:
- query_grad: bfloat16 [128, 768, 1024], P(('fsdp', 'dp'), 'seq')
- key_grad: bfloat16 [128, 768, 1024], P(('fsdp', 'dp'), 'seq')
- value_grad: bfloat16 [128, 768, 1024], P(('fsdp', 'dp'), 'seq')
- weight_grad: bfloat16 [1024, 2048], P('fsdp')
Inputs may be any that keep to these rules, and one draw needn't show every extreme that they name: `block_ids`: each number 0 to 7 appears once, and entries 2 i and 2 i + 1 always sum to 7.
All inputs are finite; a program needn't handle non-finite values.
Results may differ from a plain program's by a relative error of at most 0.027.
Values may be sent and summed in bfloat16 or wider, within the bound.
No kernel may reach another device: no remote copies, remote signals or barrier semaphores. Data moves between devices by JAX's collectives and lax.ppermute only.
A program may use at most 64 MiB of HBM per device.

v0:
```python
import math

import jax
import jax.numpy as jnp
from jax import lax
from jax.sharding import PartitionSpec as P

HEADS = 8
HD = 128


def positions_of(block_list, block_rows):
    offsets = jnp.arange(block_rows, dtype=jnp.int32)
    return (block_list[:, None] * block_rows + offsets[None, :]).reshape(-1)


def shards(query, key, value, out_weight, out_grad, block_ids):
    tokens_here = query.shape[1]
    width_heads = query.shape[2]
    block_rows = tokens_here // block_ids.shape[0]
    score_scale = 1.0 / math.sqrt(HD)
    all_blocks = lax.all_gather(block_ids, "seq", axis=0, tiled=True)
    query_pos = positions_of(block_ids, block_rows)
    every_pos = positions_of(all_blocks, block_rows)
    key_all, value_all = (
        lax.all_gather(key, "seq", axis=1, tiled=True),
        lax.all_gather(value, "seq", axis=1, tiled=True),
    )
    query_heads = query[0].reshape(tokens_here, HEADS, HD)
    key_heads = key_all[0].reshape(-1, HEADS, HD)
    value_heads = value_all[0].reshape(-1, HEADS, HD)
    scores = (
        jnp.einsum("thd,khd->htk", query_heads, key_heads, preferred_element_type=jnp.float32)
        * score_scale
    )
    allowed = every_pos[None, :] <= query_pos[:, None]
    scores = jnp.where(allowed[None], scores, -jnp.inf)
    row_top = jnp.max(scores, axis=2, keepdims=True)
    row_total = jnp.sum(jnp.exp(scores - row_top), axis=2, keepdims=True)
    log_total = row_top + jnp.log(row_total)
    weights = jnp.exp(scores - log_total)
    weights_low = weights.astype(jnp.bfloat16)
    attended = jnp.einsum(
        "htk,khd->thd", weights_low, value_heads, preferred_element_type=jnp.float32
    ).astype(jnp.bfloat16)
    grad_rows = out_grad[0]
    attn_grad = lax.dot_general(
        grad_rows,
        lax.all_gather(out_weight, "fsdp", axis=0, tiled=True),
        (((1,), (1,)), ((), ())),
        preferred_element_type=jnp.float32,
    ).astype(jnp.bfloat16)
    attended_flat = attended.reshape(tokens_here, width_heads)
    weight_shard = lax.psum_scatter(
        lax.dot_general(
            attended_flat, grad_rows, (((0,), (0,)), ((), ())), preferred_element_type=jnp.float32
        ).astype(jnp.bfloat16),
        "fsdp",
        scatter_dimension=0,
        tiled=True,
    ).astype(jnp.float32)
    token_count = tokens_here * lax.axis_size("seq") * lax.axis_size("fsdp") * lax.axis_size("dp")
    weight_grad = (lax.psum(weight_shard, ("seq", "dp")) * (1.0 / math.sqrt(token_count))).astype(
        jnp.bfloat16
    )
    grad_heads = attn_grad.reshape(tokens_here, HEADS, HD)
    row_delta = jnp.einsum("thd,thd->ht", grad_heads, attended, preferred_element_type=jnp.float32)
    prob_grad = jnp.einsum(
        "thd,khd->htk", grad_heads, value_heads, preferred_element_type=jnp.float32
    )
    score_grad = (weights * (prob_grad - row_delta[:, :, None])).astype(jnp.bfloat16)
    query_grad = (
        jnp.einsum("htk,khd->thd", score_grad, key_heads, preferred_element_type=jnp.float32)
        * score_scale
    ).astype(jnp.bfloat16)
    query_all, grad_all = (
        lax.all_gather(query, "seq", axis=1, tiled=True),
        lax.all_gather(attn_grad[None], "seq", axis=1, tiled=True),
    )
    totals_all, deltas_all = (
        lax.all_gather(log_total[:, :, 0][None], "seq", axis=2, tiled=True),
        lax.all_gather(row_delta[None], "seq", axis=2, tiled=True),
    )
    local_keys = key[0].reshape(tokens_here, HEADS, HD)
    local_values = value[0].reshape(tokens_here, HEADS, HD)
    gathered_queries = query_all[0].reshape(-1, HEADS, HD)
    gathered_grads = grad_all[0].reshape(-1, HEADS, HD)
    back_scores = (
        jnp.einsum("khd,qhd->hkq", local_keys, gathered_queries, preferred_element_type=jnp.float32)
        * score_scale
    )
    back_allowed = query_pos[:, None] <= every_pos[None, :]
    back_scores = jnp.where(back_allowed[None], back_scores, -jnp.inf)
    back_weights = jnp.exp(back_scores - totals_all[0][:, None, :])
    back_low = back_weights.astype(jnp.bfloat16)
    back_prob_grad = jnp.einsum(
        "qhd,khd->hkq", gathered_grads, local_values, preferred_element_type=jnp.float32
    )
    back_score_grad = (back_weights * (back_prob_grad - deltas_all[0][:, None, :])).astype(
        jnp.bfloat16
    )
    key_grad = (
        jnp.einsum(
            "hkq,qhd->khd", back_score_grad, gathered_queries, preferred_element_type=jnp.float32
        )
        * score_scale
    ).astype(jnp.bfloat16)
    value_grad = jnp.einsum(
        "hkq,qhd->khd", back_low, gathered_grads, preferred_element_type=jnp.float32
    ).astype(jnp.bfloat16)
    return (
        query_grad.reshape(tokens_here, width_heads)[None],
        key_grad.reshape(tokens_here, width_heads)[None],
        value_grad.reshape(tokens_here, width_heads)[None],
        weight_grad,
    )


def solution(mesh):
    in_specs = (
        P(("fsdp", "dp"), "seq", None),
        P(("fsdp", "dp"), "seq", None),
        P(("fsdp", "dp"), "seq", None),
        P("fsdp", None),
        P(("fsdp", "dp"), "seq", None),
        P("seq"),
    )
    out_specs = (
        P(("fsdp", "dp"), "seq", None),
        P(("fsdp", "dp"), "seq", None),
        P(("fsdp", "dp"), "seq", None),
        P("fsdp", None),
    )
    return jax.shard_map(shards, mesh=mesh, in_specs=in_specs, out_specs=out_specs, check_vma=False)
```

profile of v0, /device:TPU:16, one launch (start us, length us, event | category | flops | bytes accessed | tf_op | source)
XLA Modules:
  0.0 531.4 jit_solution(5790894048885190867)
XLA Ops:
  7.2 0.7 all-gather.13.cloned.1.call-update
  8.0 0.7 all-gather.11.cloned.1.call-update
  8.7 0.7 all-gather.15.cloned.1.call-update
  9.4 0.5 all-gather.17.cloned.1.call-update
  10.0 1.3 dynamic-slice
  12.0 0.9 dynamic-update-slice
  12.8 9.1 %all-reduce = s32[8]{0:T(128)S(1)} all-reduce(s32[8]{0:T(128)S(1)} %dynamic-update-slice), channel_id=1, replica_groups=mesh['seq'=4,'fsdp'=32,'dp'=4] {'seq'}, use_global_device_ids=true, to_apply=%add | all-reduce | flops 8 | bytes 64
  21.9 0.1 iota_add_fusion
  22.0 0.1 add.65
  22.1 0.7 broadcast_multiply_fusion
  22.8 0.1 iota_add_fusion.1
  22.8 0.1 add.69
  22.9 1.1 copy.64
  24.0 86.7 %all-gather.13.cloned.1.call-done = bf16[1024,2048]{1,0:T(8,128)(2,1)} async-done(((bf16[32,2048]{1,0:T(8,128)(2,1)}), bf16[1024,2048]{1,0:T(8,128)(2,1)}) %all-gather.13.cloned.1.call-update) | async-done | bytes 4194320 | tf_op jit(solution)/shard_map/all_gather | solution.py:49
  110.6 4.5 convolution_convert_fusion.1
  115.2 0.2 broadcast_compare_fusion
  115.4 39.8 %all-gather.11.cloned.1.call-done = bf16[1,768,1024]{2,1,0:T(8,128)(2,1)} async-done(((bf16[1,192,1024]{2,1,0:T(8,128)(2,1)}), bf16[1,768,1024]{2,1,0:T(8,128)(2,1)}) %all-gather.11.cloned.1.call-update) | async-done | bytes 1572880 | tf_op jit(solution)/shard_map/all_gather | solution.py:26
  155.2 1.7 copy.28
  157.0 46.7 %all-gather.15.cloned.1.call-done = bf16[1,768,1024]{2,1,0:T(8,128)(2,1)} async-done(((bf16[1,192,1024]{2,1,0:T(8,128)(2,1)}), bf16[1,768,1024]{2,1,0:T(8,128)(2,1)}) %all-gather.15.cloned.1.call-update) | async-done | bytes 1572880 | tf_op jit(solution)/shard_map/all_gather | solution.py:27
  203.7 2.6 copy.31
  206.3 1.0 fusion.3
  207.3 1.2 exponential_reduce_fusion
  208.6 0.1 copy.65
  208.6 0.1 bitcast_convert_fusion
  208.7 1.1 copy-done.3
  209.9 1.6 multiply_reduce_fusion
  211.6 3.4 convolution_convert_fusion
  215.0 0.8 copy.67
  215.9 13.1 %all-gather.3 = f32[4,192,8]{1,2,0:T(8,128)S(1)} all-gather(f32[1,192,8]{1,2,0:T(8,128)S(1)} %bitcast.115), channel_id=2, replica_groups=mesh['seq'=4,'fsdp'=32,'dp'=4] {'seq'}, dimensions={0}, use_global_device_ids=true | all-gather | bytes 30720 | tf_op jit(solution)/shard_map/all_gather | solution.py:81
  229.0 0.1 reshape.140
  229.1 22.9 %all-gather.17.cloned.1.call-done = bf16[1,768,1024]{2,1,0:T(8,128)(2,1)} async-done(((bf16[1,192,1024]{2,1,0:T(8,128)(2,1)}), bf16[1,768,1024]{2,1,0:T(8,128)(2,1)}) %all-gather.17.cloned.1.call-update) | async-done | bytes 1572880 | tf_op jit(solution)/shard_map/all_gather | solution.py:77
  252.0 1.7 copy.37
  253.7 2.9 fusion.72
  256.7 6.3 %fusion.56 = bf16[192,8,128]{2,0,1:T(8,128)(2,1)} fusion(bf16[768,8,128]{0,2,1:T(8,128)(2,1)} %bitcast.105, f32[8,192,768]{2,1,0:T(8,128)} %copy-done.1, f32[8,192]{1,0:T(8,128)S(1)} %get-tuple-element.8, f32[8,192]{1,0:T(8,128)S(1)} %log_add_fusion, pred[192,768]{1,0:T(8,128)(4,1)S(1)} %get-tuple-element.5, bf16[768,8,128]{0,2,1:T(8,128)(2,1)} %bitcast.106, ...), kind=kOutput, calls=%fused_computation.39 | convolution fusion | flops 611450880 | bytes 8810496 | tf_op jit(solution)/shard_map/htk,khd->thd/dot_general | solution.py:73
  262.9 1.3 copy.36
  264.2 0.9 broadcast_in_dim_reshape.6
  265.1 13.4 %all-gather.4 = f32[4,192,8]{1,2,0:T(8,128)S(1)} all-gather(f32[1,192,8]{1,2,0:T(8,128)S(1)} %bitcast.119), channel_id=4, replica_groups=mesh['seq'=4,'fsdp'=32,'dp'=4] {'seq'}, dimensions={0}, use_global_device_ids=true | all-gather | bytes 30720 | tf_op jit(solution)/shard_map/all_gather | solution.py:82
  278.5 0.1 reshape.142
  278.6 22.4 %all-gather.19.cloned.1.call-done = bf16[768,1024]{1,0:T(8,128)(2,1)} async-done(((bf16[192,1024]{1,0:T(8,128)(2,1)}), bf16[768,1024]{1,0:T(8,128)(2,1)}) %all-gather.19.cloned.1.call-update) | async-done | bytes 1572880 | tf_op jit(solution)/shard_map/all_gather | solution.py:78
  301.0 4.8 fusion.51
  305.8 0.3 copy.45
  306.1 0.9 broadcast_in_dim_reshape.14
  307.0 4.2 fusion.57
  311.3 0.3 copy.47
  311.5 0.9 broadcast_in_dim_reshape.15
  312.4 129.9 %reduce-scatter.2.cloned.1.call-done = bf16[32,2048]{1,0:T(8,128)(2,1)} async-done(((bf16[1024,2048]{1,0:T(8,128)(2,1)}), bf16[32,2048]{1,0:T(8,128)(2,1)}) %reduce-scatter.2.cloned.1.call-update) | async-done | bytes 131088 | tf_op jit(solution)/shard_map/reduce_scatter | solution.py:54
  442.3 81.5 %all-reduce.2 = f32[32,2048]{1,0:T(8,128)S(1)} all-reduce(bf16[32,2048]{1,0:T(8,128)(2,1)} %reduce-scatter.2.cloned.1.call-done), channel_id=1, replica_groups=mesh['seq'=4,'fsdp'=32,'dp'=4] {'seq','dp'}, use_global_device_ids=true, to_apply=%region_3.4 | all-reduce | flops 65536 | bytes 393216 | tf_op jit(solution)/shard_map/psum | solution.py:63
  523.9 0.7 multiply_convert_fusion.8
  (29 shorter events, 0.4 us)
Async XLA Ops:
  7.2 103.5 %copy-start = (bf16[1,192,2048]{2,1,0:T(8,128)(2,1)S(1)}, bf16[1,192,2048]{2,1,0:T(8,128)(2,1)}, u32[]{:S(2)}) copy-start(bf16[1,192,2048]{2,1,0:T(8,128)(2,1)} %param.10) | copy-start | bytes 2359300
  7.2 103.5 %all-gather.13.cloned.1.call-start = ((), (), s32[]{:S(2)}) async-start(), calls=%async_computation.2 | async-start | bytes 4325376 | tf_op jit(solution)/shard_map/all_gather | solution.py:49
  7.9 147.3 %all-gather.11.cloned.1.call-start = ((), (), s32[]{:S(2)}) async-start(), calls=%async_computation.1 | async-start | bytes 1966080 | tf_op jit(solution)/shard_map/all_gather | solution.py:26
  8.7 195.0 %all-gather.15.cloned.1.call-start = ((), (), s32[]{:S(2)}) async-start(), calls=%async_computation.3 | async-start | bytes 1966080 | tf_op jit(solution)/shard_map/all_gather | solution.py:27
  9.4 242.6 %all-gather.17.cloned.1.call-start = ((), (), s32[]{:S(2)}) async-start(), calls=%async_computation.4 | async-start | bytes 1966080 | tf_op jit(solution)/shard_map/all_gather | solution.py:77
  10.0 291.0 %all-gather.19.cloned.1.call-start = ((), (), s32[]{:S(2)}) async-start(), calls=%async_computation.6 | async-start | bytes 1966080 | tf_op jit(solution)/shard_map/all_gather | solution.py:78
  115.1 327.2 %reduce-scatter.2.cloned.1.call-start = ((), (), s32[]{:S(2)}) async-start(), calls=%async_computation.5 | async-start | bytes 4325376 | tf_op jit(solution)/shard_map/reduce_scatter | solution.py:54
  156.9 50.3 %copy-start.2 = (bf16[1,768,1024]{1,2,0:T(8,128)(2,1)}, bf16[1,768,1024]{1,2,0:T(8,128)(2,1)S(1)}, u32[]{:S(2)}) copy-start(bf16[1,768,1024]{1,2,0:T(8,128)(2,1)S(1)} %copy.28) | copy-start | bytes 4718596
  206.3 2.3 copy-start.6
  207.3 4.2 copy-start.1
  207.3 2.6 copy-start.3
  211.5 3.4 copy-start.4
  211.5 3.5 copy-start.5
  256.7 44.3 %copy-start.7 = (bf16[24,8,8,128]{3,2,1,0:T(8,128)(2,1)S(1)}, bf16[24,8,8,128]{3,2,1,0:T(8,128)(2,1)}, u32[]{:S(2)}) copy-start(bf16[24,8,8,128]{3,2,1,0:T(8,128)(2,1)} %copy.67) | copy-start | bytes 1179652
Sparse Core Ops, SparseCore 0:
  11.1 99.4 all-gather.12
  112.7 42.4 all-gather.10
  157.3 46.2 all-gather.14
  205.6 46.3 all-gather.16
  254.5 46.4 all-gather.18
  305.4 136.9 reduce-scatter.1
where the time goes:
time: 532 us; the launch traced here: 531 us
  waiting for transfers between devices  351 us (66%)
  blocking collectives  117 us (22%)
  matrix products  28.8 us (5%)
  local copies, waits for them, and re-layouts  16.2 us (3%)
  between operations  15 us (3%)
    reduce_scatter x1, waiting for transfers between devices, shards(): lax.psum_scatter(lax.dot_general(attended_flat, grad_rows, (((0,), (0,)),...  130 us
    all_gather x1, waiting for transfers between devices, shards(): lax.all_gather(out_weight, 'fsdp', axis=0, tiled=True)  86.7 us
    psum x1, blocking collectives, shards(): lax.psum(weight_shard, ('seq', 'dp')) * (1.0 / math.sqrt(token_count))  81.5 us
    all_gather x1, waiting for transfers between devices, shards(): lax.all_gather(value, 'seq', axis=1, tiled=True)  46.7 us
    all_gather x1, waiting for transfers between devices, shards(): lax.all_gather(key, 'seq', axis=1, tiled=True)  39.8 us
    all_gather x1, waiting for transfers between devices, shards(): lax.all_gather(query, 'seq', axis=1, tiled=True)  22.9 us
    all_gather x1, waiting for transfers between devices, shards(): lax.all_gather(attn_grad[None], 'seq', axis=1, tiled=True)  22.4 us
    all_gather x1, blocking collectives, shards(): lax.all_gather(row_delta[None], 'seq', axis=2, tiled=True)  13.4 us
  transfers between devices with their start and end apart: 6, of which 6 were waited for; matrix products, arithmetic and copies ran while one was open for 9% of the time, Pallas kernels for 0%

commit v1 on v0

v1 whole, which is shorter than its diff:
```python
import itertools
import math

import jax
import jax.numpy as jnp
from jax import lax
from jax.experimental import pallas as pl
from jax.experimental.pallas import tpu as pltpu
from jax.sharding import Mesh
from jax.sharding import PartitionSpec as P

HD = 128
BF16 = jnp.bfloat16
F32 = jnp.float32
SCALE = 1.0 / math.sqrt(HD)
VMEM = pl.BlockSpec(memory_space=pltpu.VMEM)
SMEM = pl.BlockSpec(memory_space=pltpu.SMEM)
NT = (((1,), (1,)), ((), ()))
NN = (((1,), (0,)), ((), ()))
TN = (((0,), (0,)), ((), ()))


def dot(a, b, dims):
    return lax.dot_general(a, b, dims, preferred_element_type=F32)


def call(kernel, outs, n_scalar, n_vector, name, flops, nbytes, scratch=(), exps=0):
    return pl.pallas_call(
        kernel,
        out_shape=outs,
        in_specs=[SMEM] * n_scalar + [VMEM] * n_vector,
        out_specs=jax.tree.map(lambda _: VMEM, outs),
        scratch_shapes=list(scratch),
        compiler_params=pltpu.CompilerParams(vmem_limit_bytes=40 * 1024 * 1024),
        cost_estimate=pl.CostEstimate(flops=flops, bytes_accessed=nbytes, transcendentals=exps),
        name=name,
    )


def arr(shape, dtype=BF16):
    return jax.ShapeDtypeStruct(shape, dtype)


def group_of(b):
    return 2 * (b % 2) + b // 2


def pack_kernel(where, q_ref, k_ref, v_ref, *outs):
    for k, out in enumerate(outs):
        at = pl.ds(pl.multiple_of(where[k] * 256, 256), 256)
        out[:, 0:256] = q_ref[:, at]
        out[:, 256:512] = k_ref[:, at]
        out[:, 512:768] = v_ref[:, at]


def unpack_kernel(where, r0, r1, r2, r3, dq, dk, dv):
    for k, ref in enumerate((r0, r1, r2, r3)):
        at = pl.ds(pl.multiple_of(where[k] * 256, 256), 256)
        dq[:, at] = ref[:, 0:256]
        dk[:, at] = ref[:, 256:512]
        dv[:, at] = ref[:, 512:768]


def columns_kernel(where, r0, r1, r2, r3, out):
    for k, ref in enumerate((r0, r1, r2, r3)):
        out[:, pl.ds(pl.multiple_of(where[k] * 512, 512), 512)] = ref[...]


def project_kernel(where, own_ref, mate_ref, w_here, w_there, keep, send, w_all):
    first, core = where[0], where[1]
    for k in range(4):
        for c, ref in ((0, w_here), (1, w_there)):
            at = lax.rem(core + c, 2)
            row = pl.multiple_of((where[2 + k] * 2 + at) * 32, 32)
            w_all[first, pl.ds(row, 32), :] = ref[k, 0:32, :]
            w_all[1 - first, pl.ds(row, 32), :] = ref[k, 32:64, :]
    for slot, out in ((1, send), (0, keep)):
        w = w_all[slot]
        out[0:192] = dot(own_ref[...], w, NT).astype(BF16)
        out[192:384] = dot(mate_ref[...], w, NT).astype(BF16)


def positions(ids, shape, dim, first, count):
    at = lax.broadcasted_iota(jnp.int32, shape, dim)
    pos = jnp.zeros(shape, jnp.int32)
    for j in range(count):
        here = (at >= 96 * j) & (at < 96 * (j + 1))
        pos = jnp.where(here, at + (ids[first + j] - j) * 96, pos)
    return pos


def forward_kernel(ids, x0, x1, x2, x3, o_ref, lse_ref, k_all, v_all):
    xs = (x0, x1, x2, x3)
    for i, x in enumerate(xs):
        k_all[192 * i : 192 * i + 192] = x[:, 256:512]
        v_all[192 * i : 192 * i + 192] = x[:, 512:768]
    key_pos = positions(ids, (1, 768), 1, 0, 8)
    for i, x in enumerate(xs):
        rows = slice(192 * i, 192 * i + 192)
        query_pos = positions(ids, (192, 1), 0, 2 * i, 2)
        allowed = key_pos <= query_pos
        for h in range(2):
            cols = slice(HD * h, HD * h + HD)
            s = dot(x[:, cols], k_all[:, cols], NT) * SCALE
            s = jnp.where(allowed, s, -jnp.inf)
            top = jnp.max(s, axis=1, keepdims=True)
            e = jnp.exp(s - top)
            total = jnp.sum(e, axis=1, keepdims=True)
            p = (e * (1.0 / total)).astype(BF16)
            o_ref[rows, cols] = dot(p, v_all[:, cols], NN).astype(BF16)
            lse_ref[rows, cols] = jnp.broadcast_to(top + jnp.log(total), (192, HD))


def backward_kernel(ids, x0, x1, x2, x3, g_near, g_far, o_ref, lse_ref, d0, d1, d2, d3, k_all, v_all, dk, dv):
    xs = (x0, x1, x2, x3)
    ds_ = (d0, d1, d2, d3)
    for i, x in enumerate(xs):
        k_all[192 * i : 192 * i + 192] = x[:, 256:512]
        v_all[192 * i : 192 * i + 192] = x[:, 512:768]
    key_pos = positions(ids, (1, 768), 1, 0, 8)
    for i, x in enumerate(xs):
        rows = slice(192 * i, 192 * i + 192)
        query_pos = positions(ids, (192, 1), 0, 2 * i, 2)
        allowed = key_pos <= query_pos
        grads = g_near if i < 2 else g_far
        grows = slice(192 * (i % 2), 192 * (i % 2) + 192)
        for h in range(2):
            cols = slice(HD * h, HD * h + HD)
            q = x[:, cols]
            g = grads[grows, cols]
            s = dot(q, k_all[:, cols], NT) * SCALE
            p = jnp.exp(jnp.where(allowed, s, -jnp.inf) - lse_ref[rows, HD * h : HD * h + 1])
            delta = jnp.sum(g.astype(F32) * o_ref[rows, cols].astype(F32), axis=1, keepdims=True)
            dp = dot(g, v_all[:, cols], NT)
            ds = (p * (dp - delta)).astype(BF16)
            ds_[i][:, cols] = (dot(ds, k_all[:, cols], NN) * SCALE).astype(BF16)
            pk = dot(ds, q, TN)
            pv = dot(p.astype(BF16), g, TN)
            if i == 0:
                dk[:, cols] = pk
                dv[:, cols] = pv
            else:
                dk[:, cols] += pk
                dv[:, cols] += pv
    for i, d in enumerate(ds_):
        rows = slice(192 * i, 192 * i + 192)
        d[:, 256:512] = (dk[rows] * SCALE).astype(BF16)
        d[:, 512:768] = dv[rows].astype(BF16)


def weight_kernel(where, o_here, o_there, own_ref, mate_ref, keep, send):
    core = where[0]
    for slot, o in ((0, o_here), (1, o_there)):
        for x in range(4):
            cols = slice(512 * x, 512 * x + 512)
            t = (
                dot(o[0:192], own_ref[:, cols], TN) + dot(o[192:384], mate_ref[:, cols], TN)
            ).astype(BF16)
            for y in range(4):
                t0 = t[64 * y : 64 * y + 32]
                t1 = t[64 * y + 32 : 64 * y + 64]
                keep[y, x, slot] = jnp.where(core == 0, t0, t1)
                send[y, x, slot] = jnp.where(core == 0, t1, t0)


def nearest(dests, source_of, n=16):
    pairs = []
    for row in range(4):
        takers = [d for d in dests if source_of(*d) == row]
        best = None
        for columns in itertools.permutations(range(4), len(takers)):
            steps = 0
            for (a, b), c in zip(takers, columns):
                gap = abs((4 * a + b) - (4 * row + c))
                steps += min(gap, n - gap) ** 2
            if best is None or steps < best[0]:
                best = (steps, columns)
        for (a, b), c in zip(takers, best[1]):
            pairs.append((c * 4 + row, b * 4 + a))
    return pairs


def swap(value, axis, mask, n):
    return lax.ppermute(value, axis, [(i, i ^ mask) for i in range(n)])


def shards(query, key, value, out_weight, out_grad, block_ids):
    b, a = lax.axis_index("seq"), lax.axis_index("zh")
    y, core, x = lax.axis_index("y"), lax.axis_index("c"), lax.axis_index("dp")
    half, pair = b % 2, b // 2
    places = [(i, j) for i in range(4) for j in range(4)]
    z = ("seq", "zh")

    first = lax.ppermute(
        out_weight, z, nearest([d for d in places if d[0] // 2 != d[1] % 2], lambda i, j: i ^ 2)
    )
    second = lax.ppermute(
        out_weight, z, nearest(places, lambda i, j: i ^ 1 if i // 2 == j % 2 else i ^ 3)
    )
    grads = out_grad[0]
    groups = jnp.stack([group_of(b ^ k) for k in range(4)]).astype(jnp.int32)
    packed = call(pack_kernel, [arr((192, 768))] * 4, 1, 3, "pack", 0, 2400000)(
        groups, query[0], key[0], value[0]
    )
    rows = [packed[0]] + [swap(packed[k], "seq", k, 4) for k in (1, 2, 3)]
    mate_grads = swap(grads, "seq", 1, 4)
    first = jnp.where(a // 2 == half, out_weight, first)
    piece = jnp.concatenate([first, second], axis=0)
    w_here = jnp.stack([piece] + [swap(piece, "y", k, 4) for k in (1, 2, 3)])
    w_there = swap(w_here, "c", 1, 2)
    all_ids = lax.all_gather(block_ids, "seq", axis=0, tiled=False)
    ids = jnp.concatenate([all_ids[b ^ k] for k in range(4)])

    slots = jnp.stack([(a % 2) ^ pair, core] + [y ^ k for k in range(4)]).astype(jnp.int32)
    g_near, g_send = call(
        project_kernel,
        [arr((384, 256))] * 2,
        1,
        4,
        "project",
        2 * 384 * 2048 * 512,
        4500000,
        [pltpu.VMEM((2, 256, 2048), BF16)],
    )(slots, grads, mate_grads, w_here, w_there)
    g_far = swap(g_send, "seq", 2, 4)
    kv = [pltpu.VMEM((768, 256), BF16)] * 2
    attended, lse = call(
        forward_kernel,
        [arr((768, 256)), arr((768, 256), F32)],
        1,
        4,
        "forward",
        4 * 2 * 768 * 768 * 128,
        2400000,
        kv,
        2 * 768 * 768,
    )(ids, *rows)
    o_there = swap(attended[384:768], "seq", 2, 4)
    back = call(
        backward_kernel,
        [arr((192, 768))] * 4,
        1,
        8,
        "backward",
        10 * 2 * 768 * 768 * 128,
        4000000,
        kv + [pltpu.VMEM((768, 256), F32)] * 2,
        2 * 768 * 768,
    )(ids, *rows, g_near, g_far, attended, lse)
    home = [back[0]] + [swap(back[k], "seq", k, 4) for k in (1, 2, 3)]
    query_grad, key_grad, value_grad = call(
        unpack_kernel, [arr((192, 1024))] * 3, 1, 4, "unpack", 0, 2400000
    )(groups, *home)

    keep, send = call(
        weight_kernel, [arr((4, 4, 2, 32, 512))] * 2, 1, 4, "weight", 2 * 384 * 2048 * 512, 4500000
    )(core.astype(jnp.int32)[None], attended[0:384], o_there, grads, mate_grads)
    taken = swap(send, "c", 1, 2)
    both = (keep.astype(F32) + taken.astype(F32)).astype(BF16).reshape(16, 2, 32, 512)
    parts = lax.all_to_all(both, ("y", "dp"), 0, 0, tiled=True)
    mine = jnp.sum(parts.astype(F32), axis=0).astype(BF16)
    turn = [(i * 4 + j, group_of(j) * 4 + group_of(i)) for i in range(4) for j in range(4)]
    turn2 = [(i * 4 + j, group_of(j) * 4 + (group_of(i) ^ 1)) for i in range(4) for j in range(4)]
    line = (lax.ppermute(mine[0], z, turn).astype(F32) + lax.ppermute(mine[1], z, turn2).astype(F32)).astype(BF16)
    near = [swap(line, "seq", k, 4).astype(F32) for k in (1, 2, 3)]
    total = (line.astype(F32) + near[0]) + (near[1] + near[2])
    quarter = (total * (1.0 / math.sqrt(192 * 512))).astype(BF16)
    quarters = [quarter] + [swap(quarter, "dp", k, 4) for k in (1, 2, 3)]
    columns = jnp.stack([x ^ k for k in range(4)]).astype(jnp.int32)
    weight_grad = call(columns_kernel, arr((32, 2048)), 1, 4, "columns", 0, 300000)(
        columns, *quarters
    )
    return query_grad[None], key_grad[None], value_grad[None], weight_grad


def solution(mesh):
    fine = Mesh(mesh.devices.reshape(4, 4, 4, 2, 4), ("seq", "zh", "y", "c", "dp"))
    tokens = P(("zh", "y", "c", "dp"), "seq", None)
    rows = P(("zh", "y", "c"), None)
    return jax.shard_map(
        shards,
        mesh=fine,
        in_specs=(tokens, tokens, tokens, rows, tokens, P("seq")),
        out_specs=(tokens, tokens, tokens, rows),
        check_vma=False,
    )
```

time: 532 us -> 191 us (0.36)
  the two profiles are of different devices: /device:TPU:16 before, /device:TPU:32 now
where the time goes in v1:
time: 191 us; the launch traced here: 190 us
  starting transfers between devices  97.8 us (51%)
  waiting for transfers between devices  35.5 us (19%)
  blocking collectives  25.6 us (13%)
  Pallas kernels  18 us (9%)
  local copies, waits for them, and re-layouts  7.91 us (4%)
  other arithmetic  3.27 us (2%)
  between operations  1.98 us (1%)
    ppermute x20, starting transfers between devices, swap(): return lax.ppermute(value, axis, [(i, i ^ mask) for i in range(n)])  67.2 us
    unnamed x1, blocking collectives  25.6 us
    ppermute x20, waiting for transfers between devices, swap(): return lax.ppermute(value, axis, [(i, i ^ mask) for i in range(n)])  18.5 us
    ppermute x1, starting transfers between devices, shards(): lax.ppermute(mine[0], z, turn).astype(F32)  11.7 us
    ppermute x1, starting transfers between devices, shards(): lax.ppermute(out_weight, z, nearest(places, lambda i, j: i ^ 1 if i // 2...  9.92 us
    all_to_all x1, waiting for transfers between devices, shards(): parts = lax.all_to_all(both, ('y', 'dp'), 0, 0, tiled=True)  8.44 us
    unnamed x39, local copies, waits for them, and re-layouts  7.69 us
    pallas_call x1, Pallas kernels, shards(): call(backward_kernel, [arr((192, 768))] * 4, 1, 8, 'backward', 10 * 2 * 7...  5.12 us
  transfers between devices with their start and end apart: 25, of which 9 were waited for; matrix products, arithmetic and copies ran while one was open for 3% of the time, Pallas kernels for 8%

profile of v1, /device:TPU:32, one launch (start us, length us, event | category | flops | bytes accessed | tf_op | source)
XLA Modules:
  0.0 190.1 jit_solution(9911320051025728589)
XLA Ops:
  0.8 1.0 copy-done.3
  3.9 1.5 pack.1
  5.4 7.4 %collective-permute-start = (bf16[192,768]{1,0:T(8,128)(2,1)}, bf16[192,768]{1,0:T(8,128)(2,1)S(1)}, u32[]{:S(2)}, u32[]{:S(2)}) collective-permute-start(bf16[192,768]{1,0:T(8,128)(2,1)} %get-tuple-element.22), channel_id=1, source_target_pairs={{0,128},{128,0},{256,384},{384,256},{1,129},{129,1},{257,385},{385... | collective-permute-start | bytes 884744 | tf_op jit(solution)/shard_map/ppermute | solution.py:184
  12.8 1.9 %collective-permute-start.1 = (bf16[192,768]{1,0:T(8,128)(2,1)}, bf16[192,768]{1,0:T(8,128)(2,1)S(1)}, u32[]{:S(2)}, u32[]{:S(2)}) collective-permute-start(bf16[192,768]{1,0:T(8,128)(2,1)} %get-tuple-element.23), channel_id=1, source_target_pairs={{0,256},{128,384},{256,0},{384,128},{1,257},{129,385},{257,1},{385... | collective-permute-start | bytes 884744 | tf_op jit(solution)/shard_map/ppermute | solution.py:184
  14.7 3.4 %collective-permute-start.2 = (bf16[192,768]{1,0:T(8,128)(2,1)S(1)}, bf16[192,768]{1,0:T(8,128)(2,1)S(1)}, u32[]{:S(2)}, u32[]{:S(2)}) collective-permute-start(bf16[192,768]{1,0:T(8,128)(2,1)S(1)} %get-tuple-element.24), channel_id=1, source_target_pairs={{0,384},{128,256},{256,128},{384,0},{1,385},{129,257},{257,129},{3... | collective-permute-start | bytes 884744 | tf_op jit(solution)/shard_map/ppermute | solution.py:184
  18.1 4.8 %collective-permute-start.3 = (bf16[192,2048]{1,0:T(8,128)(2,1)S(1)}, bf16[192,2048]{1,0:T(8,128)(2,1)S(1)}, u32[]{:S(2)}, u32[]{:S(2)}) collective-permute-start(bf16[192,2048]{1,0:T(8,128)(2,1)S(1)} %bitcast.40), channel_id=1, source_target_pairs={{0,128},{128,0},{256,384},{384,256},{1,129},{129,1},{257,385},{385... | collective-permute-start | bytes 2359304 | tf_op jit(solution)/shard_map/ppermute | solution.py:184
  22.9 1.3 dynamic-slice
  25.1 25.6 %all-reduce = s32[8]{0:T(128)S(1)} all-reduce(s32[8]{0:T(128)S(1)} %dynamic-update-slice), channel_id=2, replica_groups=mesh['seq'=4,'zh'=4,'y'=4,'c'=2,'dp'=4] {'seq'}, use_global_device_ids=true, to_apply=%add | all-reduce | flops 8 | bytes 64
  50.9 4.4 %forward.1 = (bf16[768,256]{1,0:T(8,128)(2,1)S(1)}, f32[768,256]{1,0:T(8,128)S(1)}) custom-call(s32[8]{0:T(128)S(1)} %pad_add_fusion.1.ids, bf16[192,768]{1,0:T(8,128)(2,1)S(1)} %get-tuple-element.21.x0, bf16[192,768]{1,0:T(8,128)(2,1)S(1)} %collective-permute-done.x1, bf16[192,768]{1,0:T(8,128)(2,1)S(1)} %collective-permute-done.1.x2, ...), custom_call_target="tpu_custom_call" | custom-call | flops 603979776 | bytes 2400000 | tf_op jit(solution)/shard_map/forward/pallas_call | solution.py:227
  56.3 3.0 %collective-permute-start.14 = (bf16[384,256]{1,0:T(8,128)(2,1)S(1)}, bf16[384,256]{1,0:T(8,128)(2,1)S(1)}, u32[]{:S(2)}, u32[]{:S(2)}) collective-permute-start(bf16[384,256]{1,0:T(8,128)(2,1)S(1)} %get-tuple-element.38), channel_id=1, source_target_pairs={{0,256},{128,384},{256,0},{384,128},{1,257},{129,385},{257,1},{385... | collective-permute-start | bytes 589832 | tf_op jit(solution)/shard_map/ppermute | solution.py:184
  59.4 1.3 collective-permute-start.4
  60.7 9.9 %collective-permute-start.5 = (bf16[32,2048]{1,0:T(8,128)(2,1)S(1)}, bf16[32,2048]{1,0:T(8,128)(2,1)S(1)}, u32[]{:S(2)}, u32[]{:S(2)}) collective-permute-start(bf16[32,2048]{1,0:T(8,128)(2,1)S(1)} %copy-done.16), channel_id=1, source_target_pairs={{256,32},{384,288},{0,96},{128,352},{32,0},{160,256},{288,64},{416... | collective-permute-start | bytes 393224 | tf_op jit(solution)/shard_map/ppermute | solution.py:197
  70.7 1.3 weight.1
  72.0 1.9 %collective-permute-start.15 = (bf16[4,4,2,32,512]{4,3,2,1,0:T(8,128)(2,1)S(1)}, bf16[4,4,2,32,512]{4,3,2,1,0:T(8,128)(2,1)S(1)}, u32[]{:S(2)}, u32[]{:S(2)}) collective-permute-start(bf16[4,4,2,32,512]{4,3,2,1,0:T(8,128)(2,1)S(1)} %get-tuple-element.37), channel_id=1, source_target_pairs={{0,4},{4,0},{1,5},{5,1},{2,6},{6,2},{3,7},{7,3},{8,12},{12,8},{9,1... | collective-permute-start | bytes 3145736 | tf_op jit(solution)/shard_map/ppermute | solution.py:184
  73.9 1.8 collective-permute-done.4
  75.7 4.1 %collective-permute-done.5 = bf16[32,2048]{1,0:T(8,128)(2,1)S(1)} collective-permute-done((bf16[32,2048]{1,0:T(8,128)(2,1)S(1)}, bf16[32,2048]{1,0:T(8,128)(2,1)S(1)}, u32[]{:S(2)}, u32[]{:S(2)}) %collective-permute-start.5) | collective-permute-done | bytes 131104 | tf_op jit(solution)/shard_map/ppermute | solution.py:197
  79.9 5.1 %collective-permute-start.7 = (bf16[64,2048]{1,0:T(8,128)(2,1)S(1)}, bf16[64,2048]{1,0:T(8,128)(2,1)S(1)}, u32[]{:S(2)}, u32[]{:S(2)}) collective-permute-start(bf16[64,2048]{1,0:T(8,128)(2,1)S(1)} %get-tuple-element.41), channel_id=1, source_target_pairs={{0,16},{8,24},{16,0},{24,8},{1,17},{9,25},{17,1},{25,9},{2,18},{10... | collective-permute-start | bytes 786440 | tf_op jit(solution)/shard_map/ppermute | solution.py:184
  85.0 2.6 %collective-permute-start.6 = (bf16[64,2048]{1,0:T(8,128)(2,1)S(1)}, bf16[64,2048]{1,0:T(8,128)(2,1)S(1)}, u32[]{:S(2)}, u32[]{:S(2)}) collective-permute-start(bf16[64,2048]{1,0:T(8,128)(2,1)S(1)} %get-tuple-element.41), channel_id=1, source_target_pairs={{0,8},{8,0},{16,24},{24,16},{1,9},{9,1},{17,25},{25,17},{2,10},{10... | collective-permute-start | bytes 786440 | tf_op jit(solution)/shard_map/ppermute | solution.py:184
  87.6 2.3 %collective-permute-start.8 = (bf16[64,2048]{1,0:T(8,128)(2,1)S(1)}, bf16[64,2048]{1,0:T(8,128)(2,1)S(1)}, u32[]{:S(2)}, u32[]{:S(2)}) collective-permute-start(bf16[64,2048]{1,0:T(8,128)(2,1)S(1)} %get-tuple-element.41), channel_id=1, source_target_pairs={{0,24},{8,16},{16,8},{24,0},{1,25},{9,17},{17,9},{25,1},{2,26},{10... | collective-permute-start | bytes 786440 | tf_op jit(solution)/shard_map/ppermute | solution.py:184
  89.9 1.8 collective-permute-done.7
  91.7 2.2 %collective-permute-done.6 = bf16[64,2048]{1,0:T(8,128)(2,1)S(1)} collective-permute-done((bf16[64,2048]{1,0:T(8,128)(2,1)S(1)}, bf16[64,2048]{1,0:T(8,128)(2,1)S(1)}, u32[]{:S(2)}, u32[]{:S(2)}) %collective-permute-start.6) | collective-permute-done | bytes 262176 | tf_op jit(solution)/shard_map/ppermute | solution.py:184
  93.9 3.2 %collective-permute-done.8 = bf16[64,2048]{1,0:T(8,128)(2,1)S(1)} collective-permute-done((bf16[64,2048]{1,0:T(8,128)(2,1)S(1)}, bf16[64,2048]{1,0:T(8,128)(2,1)S(1)}, u32[]{:S(2)}, u32[]{:S(2)}) %collective-permute-start.8) | collective-permute-done | bytes 262176 | tf_op jit(solution)/shard_map/ppermute | solution.py:184
  97.2 1.9 %collective-permute-start.9 = (bf16[4,64,2048]{2,1,0:T(8,128)(2,1)S(1)}, bf16[4,64,2048]{2,1,0:T(8,128)(2,1)S(1)}, u32[]{:S(2)}, u32[]{:S(2)}) collective-permute-start(bf16[4,64,2048]{2,1,0:T(8,128)(2,1)S(1)} %pad_maximum_fusion.w_here), channel_id=1, source_target_pairs={{0,4},{4,0},{1,5},{5,1},{2,6},{6,2},{3,7},{7,3},{8,12},{12,8},{9,1... | collective-permute-start | bytes 3145736 | tf_op jit(solution)/shard_map/ppermute | solution.py:184
  99.2 1.4 add_convert_fusion
  100.6 4.8 %all-to-all-start = ((bf16[16,2,32,512]{3,2,1,0:T(8,128)(2,1)}), bf16[16,2,32,512]{3,2,1,0:T(8,128)(2,1)}, u32[]{:S(2)}, u32[]{:S(2)}) async-start(bf16[16,2,32,512]{3,2,1,0:T(8,128)(2,1)} %bitcast.46), calls=%async_computation | async-start | bytes 2097152 | tf_op jit(solution)/shard_map/all_to_all | solution.py:260
  105.6 1.1 copy-done.2
  106.7 2.7 %project.1 = (bf16[384,256]{1,0:T(8,128)(2,1)S(1)}, bf16[384,256]{1,0:T(8,128)(2,1)}) custom-call(s32[6]{0:T(128)S(1)} %stack.77.where, bf16[192,2048]{1,0:T(8,128)(2,1)S(1)} %bitcast.42, bf16[192,2048]{1,0:T(8,128)(2,1)S(1)} %copy-done.2, bf16[4,64,2048]{2,1,0:T(8,128)(2,1)S(1)} %pad_maximum_fusion.w_here, ...), custom_call_target="tpu_custom_call" | custom-call | flops 805306368 | bytes 4500000 | tf_op jit(solution)/shard_map/project/pallas_call | solution.py:215
  109.4 6.3 %collective-permute-start.10 = (bf16[384,256]{1,0:T(8,128)(2,1)}, bf16[384,256]{1,0:T(8,128)(2,1)S(1)}, u32[]{:S(2)}, u32[]{:S(2)}) collective-permute-start(bf16[384,256]{1,0:T(8,128)(2,1)} %get-tuple-element.26), channel_id=1, source_target_pairs={{0,256},{128,384},{256,0},{384,128},{1,257},{129,385},{257,1},{385... | collective-permute-start | bytes 589832 | tf_op jit(solution)/shard_map/ppermute | solution.py:184
  115.7 8.4 %all-to-all-done = bf16[16,2,32,512]{3,2,1,0:T(8,128)(2,1)} async-done(((bf16[16,2,32,512]{3,2,1,0:T(8,128)(2,1)}), bf16[16,2,32,512]{3,2,1,0:T(8,128)(2,1)}, u32[]{:S(2)}, u32[]{:S(2)}) %all-to-all-start) | async-done | bytes 1048608 | tf_op jit(solution)/shard_map/all_to_all | solution.py:260
  124.2 1.4 reduce_sum.12
  125.6 11.7 %collective-permute-start.16 = (bf16[32,512]{1,0:T(8,128)(2,1)S(1)}, bf16[32,512]{1,0:T(8,128)(2,1)S(1)}, u32[]{:S(2)}, u32[]{:S(2)}) collective-permute-start(bf16[32,512]{1,0:T(8,128)(2,1)S(1)} %get-tuple-element.42), channel_id=1, source_target_pairs={{0,0},{32,256},{64,128},{96,384},{128,64},{160,320},{192,192},{224... | collective-permute-start | bytes 98312 | tf_op jit(solution)/shard_map/ppermute | solution.py:264
  137.2 2.9 %collective-permute-start.17 = (bf16[32,512]{1,0:T(8,128)(2,1)S(1)}, bf16[32,512]{1,0:T(8,128)(2,1)S(1)}, u32[]{:S(2)}, u32[]{:S(2)}) collective-permute-start(bf16[32,512]{1,0:T(8,128)(2,1)S(1)} %get-tuple-element.43), channel_id=1, source_target_pairs={{0,32},{32,288},{64,160},{96,416},{128,96},{160,352},{192,224},{22... | collective-permute-start | bytes 98312 | tf_op jit(solution)/shard_map/ppermute | solution.py:264
  140.2 1.1 copy-done.15
  141.3 5.1 %backward.1 = (bf16[192,768]{1,0:T(8,128)(2,1)S(1)}, bf16[192,768]{1,0:T(8,128)(2,1)S(1)}, bf16[192,768]{1,0:T(8,128)(2,1)S(1)}, bf16[192,768]{1,0:T(8,128)(2,1)S(1)}) custom-call(s32[8]{0:T(128)S(1)} %pad_add_fusion.1.ids, bf16[192,768]{1,0:T(8,128)(2,1)S(1)} %copy-done.7, bf16[192,768]{1,0:T(8,128)(2,1)S(1)} %copy-done.9, bf16[192,768]{1,0:T(8,128)(2,1)S(1)} %copy-done.11, ...), custom_call_target="tpu_custom_call" | custom-call | flops 1509949440 | bytes 4000000 | tf_op jit(solution)/shard_map/backward/pallas_call | solution.py:239
  146.4 1.9 %collective-permute-start.11 = (bf16[192,768]{1,0:T(8,128)(2,1)S(1)}, bf16[192,768]{1,0:T(8,128)(2,1)S(1)}, u32[]{:S(2)}, u32[]{:S(2)}) collective-permute-start(bf16[192,768]{1,0:T(8,128)(2,1)S(1)} %get-tuple-element.30), channel_id=1, source_target_pairs={{0,128},{128,0},{256,384},{384,256},{1,129},{129,1},{257,385},{385... | collective-permute-start | bytes 884744 | tf_op jit(solution)/shard_map/ppermute | solution.py:184
  148.3 2.7 %collective-permute-done.17 = bf16[32,512]{1,0:T(8,128)(2,1)S(1)} collective-permute-done((bf16[32,512]{1,0:T(8,128)(2,1)S(1)}, bf16[32,512]{1,0:T(8,128)(2,1)S(1)}, u32[]{:S(2)}, u32[]{:S(2)}) %collective-permute-start.17) | collective-permute-done | bytes 32800 | tf_op jit(solution)/shard_map/ppermute | solution.py:264
  151.0 1.9 %collective-permute-start.20 = (bf16[32,512]{1,0:T(8,128)(2,1)S(1)}, bf16[32,512]{1,0:T(8,128)(2,1)S(1)}, u32[]{:S(2)}, u32[]{:S(2)}) collective-permute-start(bf16[32,512]{1,0:T(8,128)(2,1)S(1)} %add_convert_fusion.1), channel_id=1, source_target_pairs={{0,384},{128,256},{256,128},{384,0},{1,385},{129,257},{257,129},{3... | collective-permute-start | bytes 98312 | tf_op jit(solution)/shard_map/ppermute | solution.py:184
  152.9 3.6 %collective-permute-start.19 = (bf16[32,512]{1,0:T(8,128)(2,1)S(1)}, bf16[32,512]{1,0:T(8,128)(2,1)S(1)}, u32[]{:S(2)}, u32[]{:S(2)}) collective-permute-start(bf16[32,512]{1,0:T(8,128)(2,1)S(1)} %add_convert_fusion.1), channel_id=1, source_target_pairs={{0,256},{128,384},{256,0},{384,128},{1,257},{129,385},{257,1},{385... | collective-permute-start | bytes 98312 | tf_op jit(solution)/shard_map/ppermute | solution.py:184
  156.6 3.7 %collective-permute-start.18 = (bf16[32,512]{1,0:T(8,128)(2,1)S(1)}, bf16[32,512]{1,0:T(8,128)(2,1)S(1)}, u32[]{:S(2)}, u32[]{:S(2)}) collective-permute-start(bf16[32,512]{1,0:T(8,128)(2,1)S(1)} %add_convert_fusion.1), channel_id=1, source_target_pairs={{0,128},{128,0},{256,384},{384,256},{1,129},{129,1},{257,385},{385... | collective-permute-start | bytes 98312 | tf_op jit(solution)/shard_map/ppermute | solution.py:184
  160.3 1.9 %collective-permute-start.12 = (bf16[192,768]{1,0:T(8,128)(2,1)S(1)}, bf16[192,768]{1,0:T(8,128)(2,1)S(1)}, u32[]{:S(2)}, u32[]{:S(2)}) collective-permute-start(bf16[192,768]{1,0:T(8,128)(2,1)S(1)} %get-tuple-element.31), channel_id=1, source_target_pairs={{0,256},{128,384},{256,0},{384,128},{1,257},{129,385},{257,1},{385... | collective-permute-start | bytes 884744 | tf_op jit(solution)/shard_map/ppermute | solution.py:184
  162.2 3.6 %collective-permute-start.13 = (bf16[192,768]{1,0:T(8,128)(2,1)S(1)}, bf16[192,768]{1,0:T(8,128)(2,1)S(1)}, u32[]{:S(2)}, u32[]{:S(2)}) collective-permute-start(bf16[192,768]{1,0:T(8,128)(2,1)S(1)} %get-tuple-element.32), channel_id=1, source_target_pairs={{0,384},{128,256},{256,128},{384,0},{1,385},{129,257},{257,129},{3... | collective-permute-start | bytes 884744 | tf_op jit(solution)/shard_map/ppermute | solution.py:184
  165.9 1.9 %collective-permute-start.23 = (bf16[32,512]{1,0:T(8,128)(2,1)S(1)}, bf16[32,512]{1,0:T(8,128)(2,1)S(1)}, u32[]{:S(2)}, u32[]{:S(2)}) collective-permute-start(bf16[32,512]{1,0:T(8,128)(2,1)S(1)} %multiply_convert_fusion.r0), channel_id=1, source_target_pairs={{0,3},{1,2},{2,1},{3,0},{4,7},{5,6},{6,5},{7,4},{8,11},{9,10},{10,... | collective-permute-start | bytes 98312 | tf_op jit(solution)/shard_map/ppermute | solution.py:184
  167.8 3.7 %collective-permute-start.22 = (bf16[32,512]{1,0:T(8,128)(2,1)S(1)}, bf16[32,512]{1,0:T(8,128)(2,1)S(1)}, u32[]{:S(2)}, u32[]{:S(2)}) collective-permute-start(bf16[32,512]{1,0:T(8,128)(2,1)S(1)} %multiply_convert_fusion.r0), channel_id=1, source_target_pairs={{0,2},{1,3},{2,0},{3,1},{4,6},{5,7},{6,4},{7,5},{8,10},{9,11},{10,... | collective-permute-start | bytes 98312 | tf_op jit(solution)/shard_map/ppermute | solution.py:184
  171.5 4.2 %collective-permute-start.21 = (bf16[32,512]{1,0:T(8,128)(2,1)S(1)}, bf16[32,512]{1,0:T(8,128)(2,1)S(1)}, u32[]{:S(2)}, u32[]{:S(2)}) collective-permute-start(bf16[32,512]{1,0:T(8,128)(2,1)S(1)} %multiply_convert_fusion.r0), channel_id=1, source_target_pairs={{0,1},{1,0},{2,3},{3,2},{4,5},{5,4},{6,7},{7,6},{8,9},{9,8},{10,11... | collective-permute-start | bytes 98312 | tf_op jit(solution)/shard_map/ppermute | solution.py:184
  175.8 3.7 %collective-permute-done.12.r2 = bf16[192,768]{1,0:T(8,128)(2,1)S(1)} collective-permute-done((bf16[192,768]{1,0:T(8,128)(2,1)S(1)}, bf16[192,768]{1,0:T(8,128)(2,1)S(1)}, u32[]{:S(2)}, u32[]{:S(2)}) %collective-permute-start.12) | collective-permute-done | bytes 294944 | tf_op jit(solution)/shard_map/ppermute | solution.py:184
  179.5 7.6 %collective-permute-done.13.r3 = bf16[192,768]{1,0:T(8,128)(2,1)S(1)} collective-permute-done((bf16[192,768]{1,0:T(8,128)(2,1)S(1)}, bf16[192,768]{1,0:T(8,128)(2,1)S(1)}, u32[]{:S(2)}, u32[]{:S(2)}) %collective-permute-start.13) | collective-permute-done | bytes 294944 | tf_op jit(solution)/shard_map/ppermute | solution.py:184
  187.1 1.7 unpack.1
  188.9 1.2 columns.1
  (64 shorter events, 3.9 us)
Async XLA Ops:
  0.6 17.4 %copy-start = (bf16[1,192,2048]{2,1,0:T(8,128)(2,1)S(1)}, bf16[1,192,2048]{2,1,0:T(8,128)(2,1)}, u32[]{:S(2)}) copy-start(bf16[1,192,2048]{2,1,0:T(8,128)(2,1)} %param.10) | copy-start | bytes 2359300
  0.8 1.0 copy-start.3
  1.9 1.0 copy-start.4
  2.9 1.0 copy-start.5
  3.9 21.0 %copy-start.17 = (s32[2]{0:T(128)S(1)}, s32[2]{0:T(128)}, u32[]{:S(2)}) copy-start(s32[2]{0:T(128)} %param.11) | copy-start | bytes 28
  5.4 50.0 %copy-start.6 = (bf16[192,768]{1,0:T(8,128)(2,1)}, bf16[192,768]{1,0:T(8,128)(2,1)S(1)}, u32[]{:S(2)}) copy-start(bf16[192,768]{1,0:T(8,128)(2,1)S(1)} %get-tuple-element.21.x0) | copy-start | bytes 884740
  5.4 45.5 %collective-permute-start = (bf16[192,768]{1,0:T(8,128)(2,1)}, bf16[192,768]{1,0:T(8,128)(2,1)S(1)}, u32[]{:S(2)}, u32[]{:S(2)}) collective-permute-start(bf16[192,768]{1,0:T(8,128)(2,1)} %get-tuple-element.22), channel_id=1, source_target_pairs={{0,128},{128,0},{256,384},{384,256},{1,129},{129,1},{257,385},{385... | collective-permute-start | bytes 884744 | tf_op jit(solution)/shard_map/ppermute | solution.py:184
  12.8 38.1 %collective-permute-start.1 = (bf16[192,768]{1,0:T(8,128)(2,1)}, bf16[192,768]{1,0:T(8,128)(2,1)S(1)}, u32[]{:S(2)}, u32[]{:S(2)}) collective-permute-start(bf16[192,768]{1,0:T(8,128)(2,1)} %get-tuple-element.23), channel_id=1, source_target_pairs={{0,256},{128,384},{256,0},{384,128},{1,257},{129,385},{257,1},{385... | collective-permute-start | bytes 884744 | tf_op jit(solution)/shard_map/ppermute | solution.py:184
  14.7 36.2 %collective-permute-start.2 = (bf16[192,768]{1,0:T(8,128)(2,1)S(1)}, bf16[192,768]{1,0:T(8,128)(2,1)S(1)}, u32[]{:S(2)}, u32[]{:S(2)}) collective-permute-start(bf16[192,768]{1,0:T(8,128)(2,1)S(1)} %get-tuple-element.24), channel_id=1, source_target_pairs={{0,384},{128,256},{256,128},{384,0},{1,385},{129,257},{257,129},{3... | collective-permute-start | bytes 884744 | tf_op jit(solution)/shard_map/ppermute | solution.py:184
  18.1 52.6 %collective-permute-start.3 = (bf16[192,2048]{1,0:T(8,128)(2,1)S(1)}, bf16[192,2048]{1,0:T(8,128)(2,1)S(1)}, u32[]{:S(2)}, u32[]{:S(2)}) collective-permute-start(bf16[192,2048]{1,0:T(8,128)(2,1)S(1)} %bitcast.40), channel_id=1, source_target_pairs={{0,128},{128,0},{256,384},{384,256},{1,129},{129,1},{257,385},{385... | collective-permute-start | bytes 2359304 | tf_op jit(solution)/shard_map/ppermute | solution.py:184
  50.9 4.5 %copy-start.8 = (bf16[192,768]{1,0:T(8,128)(2,1)}, bf16[192,768]{1,0:T(8,128)(2,1)S(1)}, u32[]{:S(2)}) copy-start(bf16[192,768]{1,0:T(8,128)(2,1)S(1)} %collective-permute-done.x1) | copy-start | bytes 884740
  50.9 4.5 %copy-start.10 = (bf16[192,768]{1,0:T(8,128)(2,1)}, bf16[192,768]{1,0:T(8,128)(2,1)S(1)}, u32[]{:S(2)}) copy-start(bf16[192,768]{1,0:T(8,128)(2,1)S(1)} %collective-permute-done.1.x2) | copy-start | bytes 884740
  50.9 4.5 %copy-start.12 = (bf16[192,768]{1,0:T(8,128)(2,1)}, bf16[192,768]{1,0:T(8,128)(2,1)S(1)}, u32[]{:S(2)}) copy-start(bf16[192,768]{1,0:T(8,128)(2,1)S(1)} %collective-permute-done.2.x3) | copy-start | bytes 884740
  50.9 8.4 %copy-start.16 = (bf16[32,2048]{1,0:T(8,128)(2,1)S(1)}, bf16[32,2048]{1,0:T(8,128)(2,1)}, u32[]{:S(2)}) copy-start(bf16[32,2048]{1,0:T(8,128)(2,1)} %param.9) | copy-start | bytes 393220
  55.4 0.9 copy-start.14
  56.3 14.3 %collective-permute-start.14 = (bf16[384,256]{1,0:T(8,128)(2,1)S(1)}, bf16[384,256]{1,0:T(8,128)(2,1)S(1)}, u32[]{:S(2)}, u32[]{:S(2)}) collective-permute-start(bf16[384,256]{1,0:T(8,128)(2,1)S(1)} %get-tuple-element.38), channel_id=1, source_target_pairs={{0,256},{128,384},{256,0},{384,128},{1,257},{129,385},{257,1},{385... | collective-permute-start | bytes 589832 | tf_op jit(solution)/shard_map/ppermute | solution.py:184
  59.4 16.3 %collective-permute-start.4 = (bf16[32,2048]{1,0:T(8,128)(2,1)S(1)}, bf16[32,2048]{1,0:T(8,128)(2,1)S(1)}, u32[]{:S(2)}, u32[]{:S(2)}) collective-permute-start(bf16[32,2048]{1,0:T(8,128)(2,1)S(1)} %copy-done.16), channel_id=1, source_target_pairs={{384,64},{0,320},{416,96},{32,352},{448,128},{64,384},{480,160},{9... | collective-permute-start | bytes 393224 | tf_op jit(solution)/shard_map/ppermute | solution.py:194
  60.7 19.2 %collective-permute-start.5 = (bf16[32,2048]{1,0:T(8,128)(2,1)S(1)}, bf16[32,2048]{1,0:T(8,128)(2,1)S(1)}, u32[]{:S(2)}, u32[]{:S(2)}) collective-permute-start(bf16[32,2048]{1,0:T(8,128)(2,1)S(1)} %copy-done.16), channel_id=1, source_target_pairs={{256,32},{384,288},{0,96},{128,352},{32,0},{160,256},{288,64},{416... | collective-permute-start | bytes 393224 | tf_op jit(solution)/shard_map/ppermute | solution.py:197
  70.6 1.3 copy-start.1
  72.0 27.2 %collective-permute-start.15 = (bf16[4,4,2,32,512]{4,3,2,1,0:T(8,128)(2,1)S(1)}, bf16[4,4,2,32,512]{4,3,2,1,0:T(8,128)(2,1)S(1)}, u32[]{:S(2)}, u32[]{:S(2)}) collective-permute-start(bf16[4,4,2,32,512]{4,3,2,1,0:T(8,128)(2,1)S(1)} %get-tuple-element.37), channel_id=1, source_target_pairs={{0,4},{4,0},{1,5},{5,1},{2,6},{6,2},{3,7},{7,3},{8,12},{12,8},{9,1... | collective-permute-start | bytes 3145736 | tf_op jit(solution)/shard_map/ppermute | solution.py:184
  79.9 11.8 %collective-permute-start.7 = (bf16[64,2048]{1,0:T(8,128)(2,1)S(1)}, bf16[64,2048]{1,0:T(8,128)(2,1)S(1)}, u32[]{:S(2)}, u32[]{:S(2)}) collective-permute-start(bf16[64,2048]{1,0:T(8,128)(2,1)S(1)} %get-tuple-element.41), channel_id=1, source_target_pairs={{0,16},{8,24},{16,0},{24,8},{1,17},{9,25},{17,1},{25,9},{2,18},{10... | collective-permute-start | bytes 786440 | tf_op jit(solution)/shard_map/ppermute | solution.py:184
  85.0 8.9 %collective-permute-start.6 = (bf16[64,2048]{1,0:T(8,128)(2,1)S(1)}, bf16[64,2048]{1,0:T(8,128)(2,1)S(1)}, u32[]{:S(2)}, u32[]{:S(2)}) collective-permute-start(bf16[64,2048]{1,0:T(8,128)(2,1)S(1)} %get-tuple-element.41), channel_id=1, source_target_pairs={{0,8},{8,0},{16,24},{24,16},{1,9},{9,1},{17,25},{25,17},{2,10},{10... | collective-permute-start | bytes 786440 | tf_op jit(solution)/shard_map/ppermute | solution.py:184
  87.6 9.5 %collective-permute-start.8 = (bf16[64,2048]{1,0:T(8,128)(2,1)S(1)}, bf16[64,2048]{1,0:T(8,128)(2,1)S(1)}, u32[]{:S(2)}, u32[]{:S(2)}) collective-permute-start(bf16[64,2048]{1,0:T(8,128)(2,1)S(1)} %get-tuple-element.41), channel_id=1, source_target_pairs={{0,24},{8,16},{16,8},{24,0},{1,25},{9,17},{17,9},{25,1},{2,26},{10... | collective-permute-start | bytes 786440 | tf_op jit(solution)/shard_map/ppermute | solution.py:184
  97.2 8.3 %collective-permute-start.9 = (bf16[4,64,2048]{2,1,0:T(8,128)(2,1)S(1)}, bf16[4,64,2048]{2,1,0:T(8,128)(2,1)S(1)}, u32[]{:S(2)}, u32[]{:S(2)}) collective-permute-start(bf16[4,64,2048]{2,1,0:T(8,128)(2,1)S(1)} %pad_maximum_fusion.w_here), channel_id=1, source_target_pairs={{0,4},{4,0},{1,5},{5,1},{2,6},{6,2},{3,7},{7,3},{8,12},{12,8},{9,1... | collective-permute-start | bytes 3145736 | tf_op jit(solution)/shard_map/ppermute | solution.py:184
  100.6 23.6 %all-to-all-start = ((bf16[16,2,32,512]{3,2,1,0:T(8,128)(2,1)}), bf16[16,2,32,512]{3,2,1,0:T(8,128)(2,1)}, u32[]{:S(2)}, u32[]{:S(2)}) async-start(bf16[16,2,32,512]{3,2,1,0:T(8,128)(2,1)} %bitcast.46), calls=%async_computation | async-start | bytes 2097152 | tf_op jit(solution)/shard_map/all_to_all | solution.py:260
  105.6 1.1 copy-start.2
  109.4 30.7 %copy-start.7 = (bf16[192,768]{1,0:T(8,128)(2,1)S(1)}, bf16[192,768]{1,0:T(8,128)(2,1)}, u32[]{:S(2)}) copy-start(bf16[192,768]{1,0:T(8,128)(2,1)} %copy-done.6) | copy-start | bytes 884740
  109.4 30.7 %copy-start.9 = (bf16[192,768]{1,0:T(8,128)(2,1)S(1)}, bf16[192,768]{1,0:T(8,128)(2,1)}, u32[]{:S(2)}) copy-start(bf16[192,768]{1,0:T(8,128)(2,1)} %copy-done.8) | copy-start | bytes 884740
  109.4 30.7 %copy-start.11 = (bf16[192,768]{1,0:T(8,128)(2,1)S(1)}, bf16[192,768]{1,0:T(8,128)(2,1)}, u32[]{:S(2)}) copy-start(bf16[192,768]{1,0:T(8,128)(2,1)} %copy-done.10) | copy-start | bytes 884740
  109.4 30.7 %copy-start.13 = (bf16[192,768]{1,0:T(8,128)(2,1)S(1)}, bf16[192,768]{1,0:T(8,128)(2,1)}, u32[]{:S(2)}) copy-start(bf16[192,768]{1,0:T(8,128)(2,1)} %copy-done.12) | copy-start | bytes 884740
  109.4 30.7 %collective-permute-start.10 = (bf16[384,256]{1,0:T(8,128)(2,1)}, bf16[384,256]{1,0:T(8,128)(2,1)S(1)}, u32[]{:S(2)}, u32[]{:S(2)}) collective-permute-start(bf16[384,256]{1,0:T(8,128)(2,1)} %get-tuple-element.26), channel_id=1, source_target_pairs={{0,256},{128,384},{256,0},{384,128},{1,257},{129,385},{257,1},{385... | collective-permute-start | bytes 589832 | tf_op jit(solution)/shard_map/ppermute | solution.py:184
  125.6 22.8 %collective-permute-start.16 = (bf16[32,512]{1,0:T(8,128)(2,1)S(1)}, bf16[32,512]{1,0:T(8,128)(2,1)S(1)}, u32[]{:S(2)}, u32[]{:S(2)}) collective-permute-start(bf16[32,512]{1,0:T(8,128)(2,1)S(1)} %get-tuple-element.42), channel_id=1, source_target_pairs={{0,0},{32,256},{64,128},{96,384},{128,64},{160,320},{192,192},{224... | collective-permute-start | bytes 98312 | tf_op jit(solution)/shard_map/ppermute | solution.py:264
  137.2 13.8 %collective-permute-start.17 = (bf16[32,512]{1,0:T(8,128)(2,1)S(1)}, bf16[32,512]{1,0:T(8,128)(2,1)S(1)}, u32[]{:S(2)}, u32[]{:S(2)}) collective-permute-start(bf16[32,512]{1,0:T(8,128)(2,1)S(1)} %get-tuple-element.43), channel_id=1, source_target_pairs={{0,32},{32,288},{64,160},{96,416},{128,96},{160,352},{192,224},{22... | collective-permute-start | bytes 98312 | tf_op jit(solution)/shard_map/ppermute | solution.py:264
  140.2 1.1 copy-start.15
  146.4 25.1 %collective-permute-start.11 = (bf16[192,768]{1,0:T(8,128)(2,1)S(1)}, bf16[192,768]{1,0:T(8,128)(2,1)S(1)}, u32[]{:S(2)}, u32[]{:S(2)}) collective-permute-start(bf16[192,768]{1,0:T(8,128)(2,1)S(1)} %get-tuple-element.30), channel_id=1, source_target_pairs={{0,128},{128,0},{256,384},{384,256},{1,129},{129,1},{257,385},{385... | collective-permute-start | bytes 884744 | tf_op jit(solution)/shard_map/ppermute | solution.py:184
  151.0 11.2 %collective-permute-start.20 = (bf16[32,512]{1,0:T(8,128)(2,1)S(1)}, bf16[32,512]{1,0:T(8,128)(2,1)S(1)}, u32[]{:S(2)}, u32[]{:S(2)}) collective-permute-start(bf16[32,512]{1,0:T(8,128)(2,1)S(1)} %add_convert_fusion.1), channel_id=1, source_target_pairs={{0,384},{128,256},{256,128},{384,0},{1,385},{129,257},{257,129},{3... | collective-permute-start | bytes 98312 | tf_op jit(solution)/shard_map/ppermute | solution.py:184
  152.9 12.9 %collective-permute-start.19 = (bf16[32,512]{1,0:T(8,128)(2,1)S(1)}, bf16[32,512]{1,0:T(8,128)(2,1)S(1)}, u32[]{:S(2)}, u32[]{:S(2)}) collective-permute-start(bf16[32,512]{1,0:T(8,128)(2,1)S(1)} %add_convert_fusion.1), channel_id=1, source_target_pairs={{0,256},{128,384},{256,0},{384,128},{1,257},{129,385},{257,1},{385... | collective-permute-start | bytes 98312 | tf_op jit(solution)/shard_map/ppermute | solution.py:184
  156.6 9.3 %collective-permute-start.18 = (bf16[32,512]{1,0:T(8,128)(2,1)S(1)}, bf16[32,512]{1,0:T(8,128)(2,1)S(1)}, u32[]{:S(2)}, u32[]{:S(2)}) collective-permute-start(bf16[32,512]{1,0:T(8,128)(2,1)S(1)} %add_convert_fusion.1), channel_id=1, source_target_pairs={{0,128},{128,0},{256,384},{384,256},{1,129},{129,1},{257,385},{385... | collective-permute-start | bytes 98312 | tf_op jit(solution)/shard_map/ppermute | solution.py:184
  160.3 19.2 %collective-permute-start.12 = (bf16[192,768]{1,0:T(8,128)(2,1)S(1)}, bf16[192,768]{1,0:T(8,128)(2,1)S(1)}, u32[]{:S(2)}, u32[]{:S(2)}) collective-permute-start(bf16[192,768]{1,0:T(8,128)(2,1)S(1)} %get-tuple-element.31), channel_id=1, source_target_pairs={{0,256},{128,384},{256,0},{384,128},{1,257},{129,385},{257,1},{385... | collective-permute-start | bytes 884744 | tf_op jit(solution)/shard_map/ppermute | solution.py:184
  162.2 24.9 %collective-permute-start.13 = (bf16[192,768]{1,0:T(8,128)(2,1)S(1)}, bf16[192,768]{1,0:T(8,128)(2,1)S(1)}, u32[]{:S(2)}, u32[]{:S(2)}) collective-permute-start(bf16[192,768]{1,0:T(8,128)(2,1)S(1)} %get-tuple-element.32), channel_id=1, source_target_pairs={{0,384},{128,256},{256,128},{384,0},{1,385},{129,257},{257,129},{3... | collective-permute-start | bytes 884744 | tf_op jit(solution)/shard_map/ppermute | solution.py:184
  165.9 23.0 %collective-permute-start.23 = (bf16[32,512]{1,0:T(8,128)(2,1)S(1)}, bf16[32,512]{1,0:T(8,128)(2,1)S(1)}, u32[]{:S(2)}, u32[]{:S(2)}) collective-permute-start(bf16[32,512]{1,0:T(8,128)(2,1)S(1)} %multiply_convert_fusion.r0), channel_id=1, source_target_pairs={{0,3},{1,2},{2,1},{3,0},{4,7},{5,6},{6,5},{7,4},{8,11},{9,10},{10,... | collective-permute-start | bytes 98312 | tf_op jit(solution)/shard_map/ppermute | solution.py:184
  167.8 21.0 %collective-permute-start.22 = (bf16[32,512]{1,0:T(8,128)(2,1)S(1)}, bf16[32,512]{1,0:T(8,128)(2,1)S(1)}, u32[]{:S(2)}, u32[]{:S(2)}) collective-permute-start(bf16[32,512]{1,0:T(8,128)(2,1)S(1)} %multiply_convert_fusion.r0), channel_id=1, source_target_pairs={{0,2},{1,3},{2,0},{3,1},{4,6},{5,7},{6,4},{7,5},{8,10},{9,11},{10,... | collective-permute-start | bytes 98312 | tf_op jit(solution)/shard_map/ppermute | solution.py:184
  171.5 17.3 %collective-permute-start.21 = (bf16[32,512]{1,0:T(8,128)(2,1)S(1)}, bf16[32,512]{1,0:T(8,128)(2,1)S(1)}, u32[]{:S(2)}, u32[]{:S(2)}) collective-permute-start(bf16[32,512]{1,0:T(8,128)(2,1)S(1)} %multiply_convert_fusion.r0), channel_id=1, source_target_pairs={{0,1},{1,0},{2,3},{3,2},{4,5},{5,4},{6,7},{7,6},{8,9},{9,8},{10,11... | collective-permute-start | bytes 98312 | tf_op jit(solution)/shard_map/ppermute | solution.py:184

commit v2 on v1

v2 whole, which is shorter than its diff:
```python
import itertools
import math

import jax
import jax.numpy as jnp
from jax import lax
from jax.experimental import pallas as pl
from jax.experimental.pallas import tpu as pltpu
from jax.sharding import Mesh
from jax.sharding import PartitionSpec as P

HD = 128
BF16 = jnp.bfloat16
F32 = jnp.float32
SCALE = 1.0 / math.sqrt(HD)
VMEM = pl.BlockSpec(memory_space=pltpu.VMEM)
SMEM = pl.BlockSpec(memory_space=pltpu.SMEM)
NT = (((1,), (1,)), ((), ()))
NN = (((1,), (0,)), ((), ()))
TN = (((0,), (0,)), ((), ()))


def dot(a, b, dims):
    return lax.dot_general(a, b, dims, preferred_element_type=F32)


def call(kernel, outs, n_scalar, n_vector, name, scratch=()):
    return pl.pallas_call(
        kernel,
        out_shape=outs,
        in_specs=[SMEM] * n_scalar + [VMEM] * n_vector,
        out_specs=jax.tree.map(lambda _: VMEM, outs),
        scratch_shapes=list(scratch),
        compiler_params=pltpu.CompilerParams(vmem_limit_bytes=40 * 1024 * 1024),
        cost_estimate=pl.CostEstimate(flops=1000, bytes_accessed=1000, transcendentals=0),
        name=name,
    )


def arr(shape, dtype=BF16):
    return jax.ShapeDtypeStruct(shape, dtype)


def group_of(b):
    return 2 * (b % 2) + b // 2


def pack_kernel(ids, q_ref, k_ref, v_ref, out):
    lane = lax.broadcasted_iota(jnp.int32, (8, 768), 1)
    block = jnp.where(lane < 384, ids[0], ids[1]).astype(F32).astype(BF16)
    for j in range(4):
        cols = slice(256 * group_of(j), 256 * group_of(j) + 256)
        out[j, 0:192, 0:256] = q_ref[:, cols]
        out[j, 0:192, 256:512] = k_ref[:, cols]
        out[j, 0:192, 512:768] = v_ref[:, cols]
        out[j, 192:200, :] = block


def unpack_kernel(home, dq, dk, dv):
    for j in range(4):
        cols = slice(256 * group_of(j), 256 * group_of(j) + 256)
        dq[:, cols] = home[j, :, 0:256]
        dk[:, cols] = home[j, :, 256:512]
        dv[:, cols] = home[j, :, 512:768]


def quarter_kernel(parts, out):
    t = [parts[j].astype(F32) for j in range(4)]
    total = ((t[0] + t[1]) + (t[2] + t[3])) * (1.0 / math.sqrt(192 * 512))
    for x in range(4):
        out[x] = total.astype(BF16)


def finish_kernel(parts, out):
    for x in range(4):
        out[:, 512 * x : 512 * x + 512] = parts[x]


def project_kernel(where, own_ref, mate_ref, w_here, w_there, keep, send, w_all):
    first, core = where[0], where[1]
    for k in range(4):
        for c, ref in ((0, w_here), (1, w_there)):
            row = pl.multiple_of((2 * where[2 + k] + lax.rem(core + c, 2)) * 32, 32)
            w_all[first, pl.ds(row, 32), :] = ref[k, 0:32, :]
            w_all[1 - first, pl.ds(row, 32), :] = ref[k, 32:64, :]
    for slot, out in ((1, send), (0, keep)):
        w = w_all[slot]
        out[0:192] = dot(own_ref[...], w, NT).astype(BF16)
        out[192:384] = dot(mate_ref[...], w, NT).astype(BF16)


def positions(x, shape, dim):
    at = lax.broadcasted_iota(jnp.int32, shape, dim)
    first = x[192:200, 0:128].astype(F32).astype(jnp.int32)[0:1, 0:1]
    second = x[192:200, 384:512].astype(F32).astype(jnp.int32)[0:1, 0:1]
    return jnp.where(at < 96, first * 96 + at, second * 96 + (at - 96))


def forward_kernel(where, x_all, near, far, lse_ref, k_all, v_all):
    xs = [x_all.at[where[0] ^ i] for i in range(4)]
    for i, x in enumerate(xs):
        k_all[192 * i : 192 * i + 192] = x[0:192, 256:512]
        v_all[192 * i : 192 * i + 192] = x[0:192, 512:768]
    key_pos = jnp.concatenate([positions(x, (1, 192), 1) for x in xs], axis=1)
    for i, x in enumerate(xs):
        rows = slice(192 * i, 192 * i + 192)
        here = slice(192 * (i % 2), 192 * (i % 2) + 192)
        allowed = key_pos <= positions(x, (192, 1), 0)
        for h in range(2):
            cols = slice(HD * h, HD * h + HD)
            s = dot(x[0:192, cols], k_all[:, cols], NT) * SCALE
            s = jnp.where(allowed, s, -jnp.inf)
            top = jnp.max(s, axis=1, keepdims=True)
            e = jnp.exp(s - top)
            total = jnp.sum(e, axis=1, keepdims=True)
            p = (e * (1.0 / total)).astype(BF16)
            out = near if i < 2 else far
            out[here, cols] = dot(p, v_all[:, cols], NN).astype(BF16)
            lse_ref[rows, cols] = jnp.broadcast_to(top + jnp.log(total), (192, HD))


def backward_kernel(
    where, x_all, g_near, g_far, o_near, o_far, lse_ref, home, k_all, v_all, dk, dv
):
    xs = [x_all.at[where[0] ^ i] for i in range(4)]
    outs = [home.at[where[0] ^ i] for i in range(4)]
    for i, x in enumerate(xs):
        k_all[192 * i : 192 * i + 192] = x[0:192, 256:512]
        v_all[192 * i : 192 * i + 192] = x[0:192, 512:768]
    key_pos = jnp.concatenate([positions(x, (1, 192), 1) for x in xs], axis=1)
    for i, x in enumerate(xs):
        rows = slice(192 * i, 192 * i + 192)
        here = slice(192 * (i % 2), 192 * (i % 2) + 192)
        grads, attended = (g_near, o_near) if i < 2 else (g_far, o_far)
        allowed = key_pos <= positions(x, (192, 1), 0)
        for h in range(2):
            cols = slice(HD * h, HD * h + HD)
            q = x[0:192, cols]
            g = grads[here, cols]
            s = dot(q, k_all[:, cols], NT) * SCALE
            p = jnp.exp(jnp.where(allowed, s, -jnp.inf) - lse_ref[rows, HD * h : HD * h + 1])
            delta = jnp.sum(g.astype(F32) * attended[here, cols].astype(F32), axis=1, keepdims=True)
            dp = dot(g, v_all[:, cols], NT)
            ds = (p * (dp - delta)).astype(BF16)
            outs[i][:, cols] = (dot(ds, k_all[:, cols], NN) * SCALE).astype(BF16)
            pk = dot(ds, q, TN)
            pv = dot(p.astype(BF16), g, TN)
            if i == 0:
                dk[:, cols] = pk
                dv[:, cols] = pv
            else:
                dk[:, cols] += pk
                dv[:, cols] += pv
    for i, out in enumerate(outs):
        rows = slice(192 * i, 192 * i + 192)
        out[:, 256:512] = (dk[rows] * SCALE).astype(BF16)
        out[:, 512:768] = dv[rows].astype(BF16)


def weight_kernel(where, o_here, o_there, own_ref, mate_ref, keep, send):
    core = where[0]
    for slot, o in ((0, o_here), (1, o_there)):
        for x in range(4):
            cols = slice(512 * x, 512 * x + 512)
            t = dot(o[0:192], own_ref[:, cols], TN) + dot(o[192:384], mate_ref[:, cols], TN)
            t = t.astype(BF16)
            for y in range(4):
                t0 = t[64 * y : 64 * y + 32]
                t1 = t[64 * y + 32 : 64 * y + 64]
                keep[y, x, slot] = jnp.where(core == 0, t0, t1)
                send[y, x, slot] = jnp.where(core == 0, t1, t0)


def sum_kernel(parts, own, other):
    for slot, out in ((0, own), (1, other)):
        t = [parts[j, slot].astype(F32) for j in range(16)]
        while len(t) > 1:
            t = [t[i] + t[i + 1] for i in range(0, len(t), 2)]
        out[...] = t[0].astype(BF16)


def nearest(dests, source_of, n=16):
    pairs = []
    for row in range(4):
        takers = [d for d in dests if source_of(*d) == row]
        best = None
        for columns in itertools.permutations(range(4), len(takers)):
            steps = 0
            for (a, b), c in zip(takers, columns):
                gap = abs((4 * a + b) - (4 * row + c))
                steps += min(gap, n - gap) ** 2
            if best is None or steps < best[0]:
                best = (steps, columns)
        for (a, b), c in zip(takers, best[1]):
            pairs.append((c * 4 + row, b * 4 + a))
    return pairs


def swap(value, axis, mask, n):
    return lax.ppermute(value, axis, [(i, i ^ mask) for i in range(n)])


def scalars(*values):
    return jnp.stack(values).astype(jnp.int32)


def exchange(value, axes):
    return lax.all_to_all(value, axes, 0, 0, tiled=True)


def shards(query, key, value, out_weight, out_grad, block_ids):
    b, a = lax.axis_index("seq"), lax.axis_index("zh")
    y, core = lax.axis_index("y"), lax.axis_index("c")
    half, pair = b & 1, b >> 1
    places = [(i, j) for i in range(4) for j in range(4)]
    z = ("seq", "zh")

    grads = out_grad[0]
    mate_grads = swap(grads, "seq", 1, 4)

    first = lax.ppermute(
        out_weight, z, nearest([d for d in places if d[0] // 2 != d[1] % 2], lambda i, j: i ^ 2)
    )
    second = lax.ppermute(
        out_weight, z, nearest(places, lambda i, j: i ^ 1 if i // 2 == j % 2 else i ^ 3)
    )
    packed = call(pack_kernel, arr((4, 200, 768)), 1, 3, "pack")(
        block_ids, query[0], key[0], value[0]
    )
    packed, mate_grads, first, second = lax.optimization_barrier(
        (packed, mate_grads, first, second)
    )
    rows = exchange(packed, "seq")
    first = jnp.where((a >> 1) == half, out_weight, first)
    piece = jnp.concatenate([first, second], axis=0)
    pieces = [piece] + [swap(piece, "y", k, 4) for k in (1, 2, 3)]
    w_here = jnp.stack(pieces)
    rows, w_here = lax.optimization_barrier((rows, w_here))
    w_there = swap(w_here, "c", 1, 2)

    g_near, g_send = call(
        project_kernel, [arr((384, 256))] * 2, 1, 4, "project", [pltpu.VMEM((2, 256, 2048), BF16)]
    )(scalars((a & 1) ^ pair, core, *(y ^ k for k in range(4))), grads, mate_grads, w_here, w_there)
    g_far = swap(g_send, "seq", 2, 4)
    kv = [pltpu.VMEM((768, 256), BF16)] * 2
    o_near, o_far, lse = call(
        forward_kernel, [arr((384, 256))] * 2 + [arr((768, 256), F32)], 1, 1, "forward", kv
    )(scalars(b), rows)
    o_there = swap(o_far, "seq", 2, 4)
    o_there, _ = lax.optimization_barrier((o_there, g_send))
    keep, send = call(weight_kernel, [arr((4, 4, 2, 32, 512))] * 2, 1, 4, "weight")(
        scalars(core), o_near, o_there, grads, mate_grads
    )
    send, g_far = lax.optimization_barrier((send, g_far))
    taken = swap(send, "c", 1, 2)
    back = call(
        backward_kernel,
        arr((4, 192, 768)),
        1,
        6,
        "backward",
        kv + [pltpu.VMEM((768, 256), F32)] * 2,
    )(scalars(b), rows, g_near, g_far, o_near, o_far, lse)
    home = exchange(back, "seq")
    both = (keep.astype(F32) + taken.astype(F32)).astype(BF16).reshape(16, 2, 32, 512)
    parts = exchange(both, ("y", "dp"))
    own, other = call(sum_kernel, [arr((32, 512))] * 2, 0, 1, "sum")(parts)
    turn = [(i * 4 + j, group_of(j) * 4 + group_of(i)) for i in range(4) for j in range(4)]
    turn2 = [(i * 4 + j, group_of(j) * 4 + (group_of(i) ^ 1)) for i in range(4) for j in range(4)]
    line = lax.ppermute(own, z, turn).astype(F32) + lax.ppermute(other, z, turn2).astype(F32)
    line, home = lax.optimization_barrier((line, home))
    spread = jnp.broadcast_to(line.astype(BF16)[None], (4, 32, 512))
    quarter = call(quarter_kernel, arr((4, 32, 512)), 0, 1, "quarter")(exchange(spread, "seq"))
    weight_grad = call(finish_kernel, arr((32, 2048)), 0, 1, "finish")(exchange(quarter, "dp"))
    query_grad, key_grad, value_grad = call(unpack_kernel, [arr((192, 1024))] * 3, 0, 1, "unpack")(
        home
    )
    return query_grad[None], key_grad[None], value_grad[None], weight_grad


def solution(mesh):
    fine = Mesh(mesh.devices.reshape(4, 4, 4, 2, 4), ("seq", "zh", "y", "c", "dp"))
    tokens = P(("zh", "y", "c", "dp"), "seq", None)
    rows = P(("zh", "y", "c"), None)
    return jax.shard_map(
        shards,
        mesh=fine,
        in_specs=(tokens, tokens, tokens, rows, tokens, P("seq")),
        out_specs=(tokens, tokens, tokens, rows),
        check_vma=False,
    )
```

time: 191 us -> 186 us (0.974)
  the two profiles are of different devices: /device:TPU:32 before, /device:TPU:128 now
where the time goes in v2:
time: 186 us; the launch traced here: 185 us
  starting transfers between devices  68.9 us (37%)
  waiting for transfers between devices  68.7 us (37%)
  Pallas kernels  19.1 us (10%)
  blocking collectives  17 us (9%)
  local copies, waits for them, and re-layouts  9.16 us (5%)
    all_to_all x4, waiting for transfers between devices, exchange(): return lax.all_to_all(value, axes, 0, 0, tiled=True)  28.4 us
    ppermute x8, starting transfers between devices, swap(): return lax.ppermute(value, axis, [(i, i ^ mask) for i in range(n)])  24.2 us
    all_to_all x4, starting transfers between devices, exchange(): return lax.all_to_all(value, axes, 0, 0, tiled=True)  20.2 us
    ppermute x8, waiting for transfers between devices, swap(): return lax.ppermute(value, axis, [(i, i ^ mask) for i in range(n)])  18.8 us
    all_to_all x1, blocking collectives, exchange(): return lax.all_to_all(value, axes, 0, 0, tiled=True)  17 us
    ppermute x1, waiting for transfers between devices, shards(): lax.ppermute(other, z, turn2).astype(F32)  16 us
    ppermute x1, starting transfers between devices, shards(): lax.ppermute(out_weight, z, nearest([d for d in places if d[0] // 2 != d[...  9.13 us
    unnamed x28, local copies, waits for them, and re-layouts  9.06 us
  transfers between devices with their start and end apart: 16, of which 12 were waited for; matrix products, arithmetic and copies ran while one was open for 0% of the time, Pallas kernels for 10%

profile of v2, /device:TPU:128, one launch (start us, length us, event | category | flops | bytes accessed | tf_op | source)
XLA Modules:
  0.0 185.3 jit_solution(15641887518328955546)
XLA Ops:
  0.6 3.8 %collective-permute-start = (bf16[192,2048]{1,0:T(8,128)(2,1)}, bf16[192,2048]{1,0:T(8,128)(2,1)S(1)}, u32[]{:S(2)}, u32[]{:S(2)}) collective-permute-start(bf16[192,2048]{1,0:T(8,128)(2,1)} %bitcast.20), channel_id=1, source_target_pairs={{0,128},{128,0},{256,384},{384,256},{1,129},{129,1},{257,385},{385... | collective-permute-start | bytes 2359304 | tf_op jit(solution)/shard_map/ppermute | solution.py:200
  4.5 9.1 %collective-permute-start.1 = (bf16[32,2048]{1,0:T(8,128)(2,1)}, bf16[32,2048]{1,0:T(8,128)(2,1)S(1)}, u32[]{:S(2)}, u32[]{:S(2)}) collective-permute-start(bf16[32,2048]{1,0:T(8,128)(2,1)} %param.9), channel_id=1, source_target_pairs={{384,64},{0,320},{416,96},{32,352},{448,128},{64,384},{480,160},{9... | collective-permute-start | bytes 393224 | tf_op jit(solution)/shard_map/ppermute | solution.py:221
  13.6 5.5 %collective-permute-start.2 = (bf16[32,2048]{1,0:T(8,128)(2,1)}, bf16[32,2048]{1,0:T(8,128)(2,1)S(1)}, u32[]{:S(2)}, u32[]{:S(2)}) collective-permute-start(bf16[32,2048]{1,0:T(8,128)(2,1)} %param.9), channel_id=1, source_target_pairs={{256,32},{384,288},{0,96},{128,352},{32,0},{160,256},{288,64},{416... | collective-permute-start | bytes 393224 | tf_op jit(solution)/shard_map/ppermute | solution.py:224
  19.1 1.0 copy-done.5
  20.1 1.0 copy-done.6
  21.1 1.0 copy-done.7
  22.1 0.7 copy-done.12
  22.7 1.7 pack.1
  24.4 5.6 %collective-permute-done.2 = bf16[32,2048]{1,0:T(8,128)(2,1)S(1)} collective-permute-done((bf16[32,2048]{1,0:T(8,128)(2,1)}, bf16[32,2048]{1,0:T(8,128)(2,1)S(1)}, u32[]{:S(2)}, u32[]{:S(2)}) %collective-permute-start.2) | collective-permute-done | bytes 131104 | tf_op jit(solution)/shard_map/ppermute | solution.py:224
  30.0 0.9 copy-done.1
  30.9 6.1 %all-to-all-start = ((bf16[4,200,768]{2,1,0:T(8,128)(2,1)}), bf16[4,200,768]{2,1,0:T(8,128)(2,1)S(1)}, u32[]{:S(2)}, u32[]{:S(2)}) async-start(bf16[4,200,768]{2,1,0:T(8,128)(2,1)} %pack.1), calls=%async_computation | async-start | bytes 2457600 | tf_op jit(solution)/shard_map/all_to_all | solution.py:208
  37.0 4.9 %collective-permute-start.5 = (bf16[64,2048]{1,0:T(8,128)(2,1)S(1)}, bf16[64,2048]{1,0:T(8,128)(2,1)S(1)}, u32[]{:S(2)}, u32[]{:S(2)}) collective-permute-start(bf16[64,2048]{1,0:T(8,128)(2,1)S(1)} %get-tuple-element.51), channel_id=1, source_target_pairs={{0,24},{8,16},{16,8},{24,0},{1,25},{9,17},{17,9},{25,1},{2,26},{10... | collective-permute-start | bytes 786440 | tf_op jit(solution)/shard_map/ppermute | solution.py:200
  42.0 2.5 %collective-permute-start.4 = (bf16[64,2048]{1,0:T(8,128)(2,1)S(1)}, bf16[64,2048]{1,0:T(8,128)(2,1)S(1)}, u32[]{:S(2)}, u32[]{:S(2)}) collective-permute-start(bf16[64,2048]{1,0:T(8,128)(2,1)S(1)} %get-tuple-element.51), channel_id=1, source_target_pairs={{0,16},{8,24},{16,0},{24,8},{1,17},{9,25},{17,1},{25,9},{2,18},{10... | collective-permute-start | bytes 786440 | tf_op jit(solution)/shard_map/ppermute | solution.py:200
  44.5 2.4 %collective-permute-start.3 = (bf16[64,2048]{1,0:T(8,128)(2,1)S(1)}, bf16[64,2048]{1,0:T(8,128)(2,1)S(1)}, u32[]{:S(2)}, u32[]{:S(2)}) collective-permute-start(bf16[64,2048]{1,0:T(8,128)(2,1)S(1)} %get-tuple-element.51), channel_id=1, source_target_pairs={{0,8},{8,0},{16,24},{24,16},{1,9},{9,1},{17,25},{25,17},{2,10},{10... | collective-permute-start | bytes 786440 | tf_op jit(solution)/shard_map/ppermute | solution.py:200
  46.9 5.1 %collective-permute-done.5 = bf16[64,2048]{1,0:T(8,128)(2,1)S(1)} collective-permute-done((bf16[64,2048]{1,0:T(8,128)(2,1)S(1)}, bf16[64,2048]{1,0:T(8,128)(2,1)S(1)}, u32[]{:S(2)}, u32[]{:S(2)}) %collective-permute-start.5) | collective-permute-done | bytes 262176 | tf_op jit(solution)/shard_map/ppermute | solution.py:200
  52.0 2.6 %collective-permute-done.4 = bf16[64,2048]{1,0:T(8,128)(2,1)S(1)} collective-permute-done((bf16[64,2048]{1,0:T(8,128)(2,1)S(1)}, bf16[64,2048]{1,0:T(8,128)(2,1)S(1)}, u32[]{:S(2)}, u32[]{:S(2)}) %collective-permute-start.4) | collective-permute-done | bytes 262176 | tf_op jit(solution)/shard_map/ppermute | solution.py:200
  54.6 0.7 collective-permute-done.3
  55.4 10.3 %all-to-all-done.x_all = bf16[4,200,768]{2,1,0:T(8,128)(2,1)S(1)} async-done(((bf16[4,200,768]{2,1,0:T(8,128)(2,1)}), bf16[4,200,768]{2,1,0:T(8,128)(2,1)S(1)}, u32[]{:S(2)}, u32[]{:S(2)}) %all-to-all-start) | async-done | bytes 1228832 | tf_op jit(solution)/shard_map/all_to_all | solution.py:208
  65.7 1.9 %collective-permute-start.7 = (bf16[4,64,2048]{2,1,0:T(8,128)(2,1)S(1)}, bf16[4,64,2048]{2,1,0:T(8,128)(2,1)}, u32[]{:S(2)}, u32[]{:S(2)}) collective-permute-start(bf16[4,64,2048]{2,1,0:T(8,128)(2,1)S(1)} %pad_maximum_fusion.w_here), channel_id=1, source_target_pairs={{0,4},{4,0},{1,5},{5,1},{2,6},{6,2},{3,7},{7,3},{8,12},{12,8},{9,1... | collective-permute-start | bytes 3145736 | tf_op jit(solution)/shard_map/ppermute | solution.py:200
  67.6 4.0 %forward.1 = (bf16[384,256]{1,0:T(8,128)(2,1)S(1)}, bf16[384,256]{1,0:T(8,128)(2,1)S(1)}, f32[768,256]{1,0:T(8,128)S(1)}) custom-call(s32[1]{0:T(128)} %bitcast.1.where, bf16[4,200,768]{2,1,0:T(8,128)(2,1)S(1)} %all-to-all-done.x_all), custom_call_target="tpu_custom_call" | custom-call | flops 1000 | bytes 1000 | tf_op jit(solution)/shard_map/forward/pallas_call | solution.py:246
  71.6 0.9 copy-done.3
  72.5 1.9 %collective-permute-start.6 = (bf16[384,256]{1,0:T(8,128)(2,1)S(1)}, bf16[384,256]{1,0:T(8,128)(2,1)}, u32[]{:S(2)}, u32[]{:S(2)}) collective-permute-start(bf16[384,256]{1,0:T(8,128)(2,1)S(1)} %get-tuple-element.32.o_far), channel_id=1, source_target_pairs={{0,256},{128,384},{256,0},{384,128},{1,257},{129,385},{257,1},{385... | collective-permute-start | bytes 589832 | tf_op jit(solution)/shard_map/ppermute | solution.py:200
  74.5 1.1 copy-done.2
  75.7 2.9 %project.1 = (bf16[384,256]{1,0:T(8,128)(2,1)S(1)}, bf16[384,256]{1,0:T(8,128)(2,1)S(1)}) custom-call(s32[6]{0:T(128)S(1)} %stack.53.where, bf16[192,2048]{1,0:T(8,128)(2,1)S(1)} %bitcast.21, bf16[192,2048]{1,0:T(8,128)(2,1)S(1)} %copy-done.2, bf16[4,64,2048]{2,1,0:T(8,128)(2,1)S(1)} %pad_maximum_fusion.w_here, ...), custom_call_target="tpu_custom_call" | custom-call | flops 1000 | bytes 1000 | tf_op jit(solution)/shard_map/project/pallas_call | solution.py:241
  78.6 0.7 copy-done.8
  79.2 4.8 %collective-permute-start.8 = (bf16[384,256]{1,0:T(8,128)(2,1)S(1)}, bf16[384,256]{1,0:T(8,128)(2,1)S(1)}, u32[]{:S(2)}, u32[]{:S(2)}) collective-permute-start(bf16[384,256]{1,0:T(8,128)(2,1)S(1)} %get-tuple-element.35), channel_id=1, source_target_pairs={{0,256},{128,384},{256,0},{384,128},{1,257},{129,385},{257,1},{385... | collective-permute-start | bytes 589832 | tf_op jit(solution)/shard_map/ppermute | solution.py:200
  84.0 1.8 collective-permute-done.6.o_there
  85.8 2.2 %weight.1 = (bf16[4,4,2,32,512]{4,3,2,1,0:T(8,128)(2,1)S(1)}, bf16[4,4,2,32,512]{4,3,2,1,0:T(8,128)(2,1)S(1)}) custom-call(s32[1]{0:T(128)} %bitcast.where, bf16[384,256]{1,0:T(8,128)(2,1)S(1)} %get-tuple-element.31.o_here.o_near, bf16[384,256]{1,0:T(8,128)(2,1)} %collective-permute-done.6.o_there, bf16[192,2048]{1,0:T(8,128)(2,1)S(1)} %bitcast.22, ...), custom_call_target="tpu_custom_call" | custom-call | flops 1000 | bytes 1000 | tf_op jit(solution)/shard_map/weight/pallas_call | solution.py:251
  88.0 6.1 %collective-permute-done.8.g_far = bf16[384,256]{1,0:T(8,128)(2,1)S(1)} collective-permute-done((bf16[384,256]{1,0:T(8,128)(2,1)S(1)}, bf16[384,256]{1,0:T(8,128)(2,1)S(1)}, u32[]{:S(2)}, u32[]{:S(2)}) %collective-permute-start.8) | collective-permute-done | bytes 196640 | tf_op jit(solution)/shard_map/ppermute | solution.py:200
  94.1 2.0 %collective-permute-start.9 = (bf16[4,4,2,32,512]{4,3,2,1,0:T(8,128)(2,1)S(1)}, bf16[4,4,2,32,512]{4,3,2,1,0:T(8,128)(2,1)S(1)}, u32[]{:S(2)}, u32[]{:S(2)}) collective-permute-start(bf16[4,4,2,32,512]{4,3,2,1,0:T(8,128)(2,1)S(1)} %get-tuple-element.39), channel_id=1, source_target_pairs={{0,4},{4,0},{1,5},{5,1},{2,6},{6,2},{3,7},{7,3},{8,12},{12,8},{9,1... | collective-permute-start | bytes 3145736 | tf_op jit(solution)/shard_map/ppermute | solution.py:200
  96.1 2.6 %collective-permute-done.9 = bf16[4,4,2,32,512]{4,3,2,1,0:T(8,128)(2,1)S(1)} collective-permute-done((bf16[4,4,2,32,512]{4,3,2,1,0:T(8,128)(2,1)S(1)}, bf16[4,4,2,32,512]{4,3,2,1,0:T(8,128)(2,1)S(1)}, u32[]{:S(2)}, u32[]{:S(2)}) %collective-permute-start.9) | collective-permute-done | bytes 1048608 | tf_op jit(solution)/shard_map/ppermute | solution.py:200
  98.6 1.4 add_convert_fusion
  100.0 7.1 %all-to-all-start.1 = ((bf16[16,2,32,512]{3,2,1,0:T(8,128)(2,1)}), bf16[16,2,32,512]{3,2,1,0:T(8,128)(2,1)S(1)}, u32[]{:S(2)}, u32[]{:S(2)}) async-start(bf16[16,2,32,512]{3,2,1,0:T(8,128)(2,1)} %bitcast.26), calls=%async_computation.1 | async-start | bytes 2097152 | tf_op jit(solution)/shard_map/all_to_all | solution.py:208
  107.2 0.9 copy-done.9
  108.1 0.9 copy-done.11
  109.1 5.7 %backward.1 = bf16[4,192,768]{2,1,0:T(8,128)(2,1)} custom-call(s32[1]{0:T(128)} %bitcast.1.where, bf16[4,200,768]{2,1,0:T(8,128)(2,1)S(1)} %all-to-all-done.x_all, bf16[384,256]{1,0:T(8,128)(2,1)S(1)} %copy-done.9, bf16[384,256]{1,0:T(8,128)(2,1)S(1)} %copy-done.11, bf16[384,256]{1,0:T(8,128)(2,1)S(1)} %get-tuple-element.31.o_here.o_near, ...), custom_call_target="tpu_custom_call" | custom-call | flops 1000 | bytes 1000 | tf_op jit(solution)/shard_map/backward/pallas_call | solution.py:256
  114.7 10.2 %all-to-all-done.1.parts = bf16[16,2,32,512]{3,2,1,0:T(8,128)(2,1)S(1)} async-done(((bf16[16,2,32,512]{3,2,1,0:T(8,128)(2,1)}), bf16[16,2,32,512]{3,2,1,0:T(8,128)(2,1)S(1)}, u32[]{:S(2)}, u32[]{:S(2)}) %all-to-all-start.1) | async-done | bytes 1048608 | tf_op jit(solution)/shard_map/all_to_all | solution.py:208
  125.0 3.6 %all-to-all-start.2 = ((bf16[4,192,768]{2,1,0:T(8,128)(2,1)}), bf16[4,192,768]{2,1,0:T(8,128)(2,1)S(1)}, u32[]{:S(2)}, u32[]{:S(2)}) async-start(bf16[4,192,768]{2,1,0:T(8,128)(2,1)} %backward.1), calls=%async_computation.2 | async-start | bytes 2359296 | tf_op jit(solution)/shard_map/all_to_all | solution.py:208
  128.7 4.8 %collective-permute-start.11 = (bf16[32,512]{1,0:T(8,128)(2,1)S(1)}, bf16[32,512]{1,0:T(8,128)(2,1)S(1)}, u32[]{:S(2)}, u32[]{:S(2)}) collective-permute-start(bf16[32,512]{1,0:T(8,128)(2,1)S(1)} %get-tuple-element.41), channel_id=1, source_target_pairs={{0,32},{32,288},{64,160},{96,416},{128,96},{160,352},{192,224},{22... | collective-permute-start | bytes 98312 | tf_op jit(solution)/shard_map/ppermute | solution.py:270
  133.6 5.0 %collective-permute-start.10 = (bf16[32,512]{1,0:T(8,128)(2,1)S(1)}, bf16[32,512]{1,0:T(8,128)(2,1)S(1)}, u32[]{:S(2)}, u32[]{:S(2)}) collective-permute-start(bf16[32,512]{1,0:T(8,128)(2,1)S(1)} %get-tuple-element.40), channel_id=1, source_target_pairs={{0,0},{32,256},{64,128},{96,384},{128,64},{160,320},{192,192},{224... | collective-permute-start | bytes 98312 | tf_op jit(solution)/shard_map/ppermute | solution.py:270
  138.6 16.0 %collective-permute-done.11 = bf16[32,512]{1,0:T(8,128)(2,1)S(1)} collective-permute-done((bf16[32,512]{1,0:T(8,128)(2,1)S(1)}, bf16[32,512]{1,0:T(8,128)(2,1)S(1)}, u32[]{:S(2)}, u32[]{:S(2)}) %collective-permute-start.11) | collective-permute-done | bytes 32800 | tf_op jit(solution)/shard_map/ppermute | solution.py:270
  154.6 3.0 %all-to-all-done.2.home = bf16[4,192,768]{2,1,0:T(8,128)(2,1)S(1)} async-done(((bf16[4,192,768]{2,1,0:T(8,128)(2,1)}), bf16[4,192,768]{2,1,0:T(8,128)(2,1)S(1)}, u32[]{:S(2)}, u32[]{:S(2)}) %all-to-all-start.2) | async-done | bytes 1179680 | tf_op jit(solution)/shard_map/all_to_all | solution.py:208
  157.6 17.0 %all_to_all.25.parts = bf16[4,32,512]{2,1,0:T(8,128)(2,1)S(1)} all-to-all(bf16[4,32,512]{2,1,0:T(8,128)(2,1)S(1)} %broadcast_in_dim.18), channel_id=1, replica_groups=mesh['seq'=4,'zh'=4,'y'=4,'c'=2,'dp'=4] {'seq'}, dimensions={0} | all-to-all | bytes 262144 | tf_op jit(solution)/shard_map/all_to_all | solution.py:208
  174.6 0.7 quarter.1
  175.3 3.3 %all-to-all-start.4 = ((bf16[4,32,512]{2,1,0:T(8,128)(2,1)}), bf16[4,32,512]{2,1,0:T(8,128)(2,1)S(1)}, u32[]{:S(2)}, u32[]{:S(2)}) async-start(bf16[4,32,512]{2,1,0:T(8,128)(2,1)} %quarter.1), calls=%async_computation.4 | async-start | bytes 262144 | tf_op jit(solution)/shard_map/all_to_all | solution.py:208
  178.6 1.2 unpack.1
  179.8 4.8 %all-to-all-done.4.parts = bf16[4,32,512]{2,1,0:T(8,128)(2,1)S(1)} async-done(((bf16[4,32,512]{2,1,0:T(8,128)(2,1)}), bf16[4,32,512]{2,1,0:T(8,128)(2,1)S(1)}, u32[]{:S(2)}, u32[]{:S(2)}) %all-to-all-start.4) | async-done | bytes 131104 | tf_op jit(solution)/shard_map/all_to_all | solution.py:208
  184.6 0.7 finish.1
  (29 shorter events, 0.5 us)
Async XLA Ops:
  0.6 29.4 %collective-permute-start = (bf16[192,2048]{1,0:T(8,128)(2,1)}, bf16[192,2048]{1,0:T(8,128)(2,1)S(1)}, u32[]{:S(2)}, u32[]{:S(2)}) collective-permute-start(bf16[192,2048]{1,0:T(8,128)(2,1)} %bitcast.20), channel_id=1, source_target_pairs={{0,128},{128,0},{256,384},{384,256},{1,129},{129,1},{257,385},{385... | collective-permute-start | bytes 2359304 | tf_op jit(solution)/shard_map/ppermute | solution.py:200
  4.5 19.9 %collective-permute-start.1 = (bf16[32,2048]{1,0:T(8,128)(2,1)}, bf16[32,2048]{1,0:T(8,128)(2,1)S(1)}, u32[]{:S(2)}, u32[]{:S(2)}) collective-permute-start(bf16[32,2048]{1,0:T(8,128)(2,1)} %param.9), channel_id=1, source_target_pairs={{384,64},{0,320},{416,96},{32,352},{448,128},{64,384},{480,160},{9... | collective-permute-start | bytes 393224 | tf_op jit(solution)/shard_map/ppermute | solution.py:221
  13.6 16.4 %collective-permute-start.2 = (bf16[32,2048]{1,0:T(8,128)(2,1)}, bf16[32,2048]{1,0:T(8,128)(2,1)S(1)}, u32[]{:S(2)}, u32[]{:S(2)}) collective-permute-start(bf16[32,2048]{1,0:T(8,128)(2,1)} %param.9), channel_id=1, source_target_pairs={{256,32},{384,288},{0,96},{128,352},{32,0},{160,256},{288,64},{416... | collective-permute-start | bytes 393224 | tf_op jit(solution)/shard_map/ppermute | solution.py:224
  19.1 1.0 copy-start.5
  20.1 1.0 copy-start.6
  21.1 1.0 copy-start.7
  22.1 0.7 copy-start.12
  24.4 12.6 %copy-start.13 = (bf16[32,2048]{1,0:T(8,128)(2,1)S(1)}, bf16[32,2048]{1,0:T(8,128)(2,1)}, u32[]{:S(2)}) copy-start(bf16[32,2048]{1,0:T(8,128)(2,1)} %param.9) | copy-start | bytes 393220
  30.0 0.9 copy-start.1
  30.9 34.8 %all-to-all-start = ((bf16[4,200,768]{2,1,0:T(8,128)(2,1)}), bf16[4,200,768]{2,1,0:T(8,128)(2,1)S(1)}, u32[]{:S(2)}, u32[]{:S(2)}) async-start(bf16[4,200,768]{2,1,0:T(8,128)(2,1)} %pack.1), calls=%async_computation | async-start | bytes 2457600 | tf_op jit(solution)/shard_map/all_to_all | solution.py:208
  37.0 15.0 %collective-permute-start.5 = (bf16[64,2048]{1,0:T(8,128)(2,1)S(1)}, bf16[64,2048]{1,0:T(8,128)(2,1)S(1)}, u32[]{:S(2)}, u32[]{:S(2)}) collective-permute-start(bf16[64,2048]{1,0:T(8,128)(2,1)S(1)} %get-tuple-element.51), channel_id=1, source_target_pairs={{0,24},{8,16},{16,8},{24,0},{1,25},{9,17},{17,9},{25,1},{2,26},{10... | collective-permute-start | bytes 786440 | tf_op jit(solution)/shard_map/ppermute | solution.py:200
  42.0 12.6 %collective-permute-start.4 = (bf16[64,2048]{1,0:T(8,128)(2,1)S(1)}, bf16[64,2048]{1,0:T(8,128)(2,1)S(1)}, u32[]{:S(2)}, u32[]{:S(2)}) collective-permute-start(bf16[64,2048]{1,0:T(8,128)(2,1)S(1)} %get-tuple-element.51), channel_id=1, source_target_pairs={{0,16},{8,24},{16,0},{24,8},{1,17},{9,25},{17,1},{25,9},{2,18},{10... | collective-permute-start | bytes 786440 | tf_op jit(solution)/shard_map/ppermute | solution.py:200
  44.5 10.8 %collective-permute-start.3 = (bf16[64,2048]{1,0:T(8,128)(2,1)S(1)}, bf16[64,2048]{1,0:T(8,128)(2,1)S(1)}, u32[]{:S(2)}, u32[]{:S(2)}) collective-permute-start(bf16[64,2048]{1,0:T(8,128)(2,1)S(1)} %get-tuple-element.51), channel_id=1, source_target_pairs={{0,8},{8,0},{16,24},{24,16},{1,9},{9,1},{17,25},{25,17},{2,10},{10... | collective-permute-start | bytes 786440 | tf_op jit(solution)/shard_map/ppermute | solution.py:200
  55.3 19.2 %copy-start = (bf16[1,192,2048]{2,1,0:T(8,128)(2,1)S(1)}, bf16[1,192,2048]{2,1,0:T(8,128)(2,1)}, u32[]{:S(2)}) copy-start(bf16[1,192,2048]{2,1,0:T(8,128)(2,1)} %param.10) | copy-start | bytes 2359300
  65.7 8.8 %collective-permute-start.7 = (bf16[4,64,2048]{2,1,0:T(8,128)(2,1)S(1)}, bf16[4,64,2048]{2,1,0:T(8,128)(2,1)}, u32[]{:S(2)}, u32[]{:S(2)}) collective-permute-start(bf16[4,64,2048]{2,1,0:T(8,128)(2,1)S(1)} %pad_maximum_fusion.w_here), channel_id=1, source_target_pairs={{0,4},{4,0},{1,5},{5,1},{2,6},{6,2},{3,7},{7,3},{8,12},{12,8},{9,1... | collective-permute-start | bytes 3145736 | tf_op jit(solution)/shard_map/ppermute | solution.py:200
  71.6 0.9 copy-start.3
  72.5 13.3 %collective-permute-start.6 = (bf16[384,256]{1,0:T(8,128)(2,1)S(1)}, bf16[384,256]{1,0:T(8,128)(2,1)}, u32[]{:S(2)}, u32[]{:S(2)}) collective-permute-start(bf16[384,256]{1,0:T(8,128)(2,1)S(1)} %get-tuple-element.32.o_far), channel_id=1, source_target_pairs={{0,256},{128,384},{256,0},{384,128},{1,257},{129,385},{257,1},{385... | collective-permute-start | bytes 589832 | tf_op jit(solution)/shard_map/ppermute | solution.py:200
  74.5 1.1 copy-start.2
  78.6 0.7 copy-start.8
  79.2 14.8 %collective-permute-start.8 = (bf16[384,256]{1,0:T(8,128)(2,1)S(1)}, bf16[384,256]{1,0:T(8,128)(2,1)S(1)}, u32[]{:S(2)}, u32[]{:S(2)}) collective-permute-start(bf16[384,256]{1,0:T(8,128)(2,1)S(1)} %get-tuple-element.35), channel_id=1, source_target_pairs={{0,256},{128,384},{256,0},{384,128},{1,257},{129,385},{257,1},{385... | collective-permute-start | bytes 589832 | tf_op jit(solution)/shard_map/ppermute | solution.py:200
  94.1 5.9 %copy-start.10 = (bf16[384,256]{1,0:T(8,128)(2,1)}, bf16[384,256]{1,0:T(8,128)(2,1)S(1)}, u32[]{:S(2)}) copy-start(bf16[384,256]{1,0:T(8,128)(2,1)S(1)} %collective-permute-done.8.g_far) | copy-start | bytes 589828
  94.1 4.5 %collective-permute-start.9 = (bf16[4,4,2,32,512]{4,3,2,1,0:T(8,128)(2,1)S(1)}, bf16[4,4,2,32,512]{4,3,2,1,0:T(8,128)(2,1)S(1)}, u32[]{:S(2)}, u32[]{:S(2)}) collective-permute-start(bf16[4,4,2,32,512]{4,3,2,1,0:T(8,128)(2,1)S(1)} %get-tuple-element.39), channel_id=1, source_target_pairs={{0,4},{4,0},{1,5},{5,1},{2,6},{6,2},{3,7},{7,3},{8,12},{12,8},{9,1... | collective-permute-start | bytes 3145736 | tf_op jit(solution)/shard_map/ppermute | solution.py:200
  100.0 7.2 %copy-start.4 = (f32[768,256]{1,0:T(8,128)S(1)}, f32[768,256]{1,0:T(8,128)}, u32[]{:S(2)}) copy-start(f32[768,256]{1,0:T(8,128)} %copy-done.3) | copy-start | bytes 2359300
  100.0 24.9 %all-to-all-start.1 = ((bf16[16,2,32,512]{3,2,1,0:T(8,128)(2,1)}), bf16[16,2,32,512]{3,2,1,0:T(8,128)(2,1)S(1)}, u32[]{:S(2)}, u32[]{:S(2)}) async-start(bf16[16,2,32,512]{3,2,1,0:T(8,128)(2,1)} %bitcast.26), calls=%async_computation.1 | async-start | bytes 2097152 | tf_op jit(solution)/shard_map/all_to_all | solution.py:208
  107.2 0.9 copy-start.9
  108.1 0.9 copy-start.11
  125.0 32.6 %all-to-all-start.2 = ((bf16[4,192,768]{2,1,0:T(8,128)(2,1)}), bf16[4,192,768]{2,1,0:T(8,128)(2,1)S(1)}, u32[]{:S(2)}, u32[]{:S(2)}) async-start(bf16[4,192,768]{2,1,0:T(8,128)(2,1)} %backward.1), calls=%async_computation.2 | async-start | bytes 2359296 | tf_op jit(solution)/shard_map/all_to_all | solution.py:208
  128.7 25.8 %collective-permute-start.11 = (bf16[32,512]{1,0:T(8,128)(2,1)S(1)}, bf16[32,512]{1,0:T(8,128)(2,1)S(1)}, u32[]{:S(2)}, u32[]{:S(2)}) collective-permute-start(bf16[32,512]{1,0:T(8,128)(2,1)S(1)} %get-tuple-element.41), channel_id=1, source_target_pairs={{0,32},{32,288},{64,160},{96,416},{128,96},{160,352},{192,224},{22... | collective-permute-start | bytes 98312 | tf_op jit(solution)/shard_map/ppermute | solution.py:270
  133.6 21.0 %collective-permute-start.10 = (bf16[32,512]{1,0:T(8,128)(2,1)S(1)}, bf16[32,512]{1,0:T(8,128)(2,1)S(1)}, u32[]{:S(2)}, u32[]{:S(2)}) collective-permute-start(bf16[32,512]{1,0:T(8,128)(2,1)S(1)} %get-tuple-element.40), channel_id=1, source_target_pairs={{0,0},{32,256},{64,128},{96,384},{128,64},{160,320},{192,192},{224... | collective-permute-start | bytes 98312 | tf_op jit(solution)/shard_map/ppermute | solution.py:270
  175.3 9.3 %all-to-all-start.4 = ((bf16[4,32,512]{2,1,0:T(8,128)(2,1)}), bf16[4,32,512]{2,1,0:T(8,128)(2,1)S(1)}, u32[]{:S(2)}, u32[]{:S(2)}) async-start(bf16[4,32,512]{2,1,0:T(8,128)(2,1)} %quarter.1), calls=%async_computation.4 | async-start | bytes 262144 | tf_op jit(solution)/shard_map/all_to_all | solution.py:208

commit v3 on v2

--- a/solution.py
+++ b/solution.py
@@ -66,14 +66,13 @@
 
 def quarter_kernel(parts, out):
     t = [parts[j].astype(F32) for j in range(4)]
-    total = ((t[0] + t[1]) + (t[2] + t[3])) * (1.0 / math.sqrt(192 * 512))
-    for x in range(4):
-        out[x] = total.astype(BF16)
-
-
-def finish_kernel(parts, out):
-    for x in range(4):
-        out[:, 512 * x : 512 * x + 512] = parts[x]
+    total = (t[0] + t[1]) + (t[2] + t[3])
+    out[...] = (total * (1.0 / math.sqrt(192 * 512))).astype(BF16)
+
+
+def finish_kernel(where, p0, p1, p2, p3, out):
+    for k, ref in enumerate((p0, p1, p2, p3)):
+        out[:, pl.ds(pl.multiple_of(where[k] * 512, 512), 512)] = ref[...]
 
 
 def project_kernel(where, own_ref, mate_ref, w_here, w_there, keep, send, w_all):
@@ -210,13 +209,12 @@
 
 def shards(query, key, value, out_weight, out_grad, block_ids):
     b, a = lax.axis_index("seq"), lax.axis_index("zh")
-    y, core = lax.axis_index("y"), lax.axis_index("c")
+    y, core, x = lax.axis_index("y"), lax.axis_index("c"), lax.axis_index("dp")
     half, pair = b & 1, b >> 1
     places = [(i, j) for i in range(4) for j in range(4)]
     z = ("seq", "zh")
 
     grads = out_grad[0]
-    mate_grads = swap(grads, "seq", 1, 4)
 
     first = lax.ppermute(
         out_weight, z, nearest([d for d in places if d[0] // 2 != d[1] % 2], lambda i, j: i ^ 2)
@@ -227,15 +225,13 @@
     packed = call(pack_kernel, arr((4, 200, 768)), 1, 3, "pack")(
         block_ids, query[0], key[0], value[0]
     )
-    packed, mate_grads, first, second = lax.optimization_barrier(
-        (packed, mate_grads, first, second)
-    )
     rows = exchange(packed, "seq")
+    grads, first, second = lax.optimization_barrier((grads, first, second))
+    mate_grads = swap(grads, "seq", 1, 4)
     first = jnp.where((a >> 1) == half, out_weight, first)
     piece = jnp.concatenate([first, second], axis=0)
     pieces = [piece] + [swap(piece, "y", k, 4) for k in (1, 2, 3)]
     w_here = jnp.stack(pieces)
-    rows, w_here = lax.optimization_barrier((rows, w_here))
     w_there = swap(w_here, "c", 1, 2)
 
     g_near, g_send = call(
@@ -247,11 +243,10 @@
         forward_kernel, [arr((384, 256))] * 2 + [arr((768, 256), F32)], 1, 1, "forward", kv
     )(scalars(b), rows)
     o_there = swap(o_far, "seq", 2, 4)
-    o_there, _ = lax.optimization_barrier((o_there, g_send))
+    o_there, _ = lax.optimization_barrier((o_there, pieces))
     keep, send = call(weight_kernel, [arr((4, 4, 2, 32, 512))] * 2, 1, 4, "weight")(
         scalars(core), o_near, o_there, grads, mate_grads
     )
-    send, g_far = lax.optimization_barrier((send, g_far))
     taken = swap(send, "c", 1, 2)
     back = call(
         backward_kernel,
@@ -261,17 +256,21 @@
         "backward",
         kv + [pltpu.VMEM((768, 256), F32)] * 2,
     )(scalars(b), rows, g_near, g_far, o_near, o_far, lse)
-    home = exchange(back, "seq")
     both = (keep.astype(F32) + taken.astype(F32)).astype(BF16).reshape(16, 2, 32, 512)
     parts = exchange(both, ("y", "dp"))
     own, other = call(sum_kernel, [arr((32, 512))] * 2, 0, 1, "sum")(parts)
+    own, other, g_far = lax.optimization_barrier((own, other, g_far))
     turn = [(i * 4 + j, group_of(j) * 4 + group_of(i)) for i in range(4) for j in range(4)]
     turn2 = [(i * 4 + j, group_of(j) * 4 + (group_of(i) ^ 1)) for i in range(4) for j in range(4)]
     line = lax.ppermute(own, z, turn).astype(F32) + lax.ppermute(other, z, turn2).astype(F32)
-    line, home = lax.optimization_barrier((line, home))
     spread = jnp.broadcast_to(line.astype(BF16)[None], (4, 32, 512))
-    quarter = call(quarter_kernel, arr((4, 32, 512)), 0, 1, "quarter")(exchange(spread, "seq"))
-    weight_grad = call(finish_kernel, arr((32, 2048)), 0, 1, "finish")(exchange(quarter, "dp"))
+    quarter = call(quarter_kernel, arr((32, 512)), 0, 1, "quarter")(exchange(spread, "seq"))
+    back, quarter = lax.optimization_barrier((back, quarter))
+    home = exchange(back, "seq")
+    quarters = [quarter] + [swap(quarter, "dp", k, 4) for k in (1, 2, 3)]
+    weight_grad = call(finish_kernel, arr((32, 2048)), 1, 4, "finish")(
+        scalars(*(x ^ k for k in range(4))), *quarters
+    )
     query_grad, key_grad, value_grad = call(unpack_kernel, [arr((192, 1024))] * 3, 0, 1, "unpack")(
         home
     )

time: 186 us -> 180 us (0.968)
  the two profiles are of different devices: /device:TPU:128 before, /device:TPU:2 now
where the time goes in v3:
time: 180 us; the launch traced here: 178 us
  starting transfers between devices  100 us (56%)
  waiting for transfers between devices  44.2 us (25%)
  Pallas kernels  18.6 us (10%)
  local copies, waits for them, and re-layouts  11 us (6%)
  other arithmetic  3.58 us (2%)
    ppermute x11, starting transfers between devices, swap(): return lax.ppermute(value, axis, [(i, i ^ mask) for i in range(n)])  39.5 us
    all_to_all x4, starting transfers between devices, exchange(): return lax.all_to_all(value, axes, 0, 0, tiled=True)  36.6 us
    all_to_all x4, waiting for transfers between devices, exchange(): return lax.all_to_all(value, axes, 0, 0, tiled=True)  20.9 us
    ppermute x1, starting transfers between devices, shards(): lax.ppermute(out_weight, z, nearest([d for d in places if d[0] // 2 != d[...  13.9 us
    ppermute x11, waiting for transfers between devices, swap(): return lax.ppermute(value, axis, [(i, i ^ mask) for i in range(n)])  13.3 us
    unnamed x36, local copies, waits for them, and re-layouts  10.3 us
    ppermute x1, starting transfers between devices, shards(): lax.ppermute(other, z, turn2).astype(F32)  6.37 us
    pallas_call x1, Pallas kernels, shards(): call(backward_kernel, arr((4, 192, 768)), 1, 6, 'backward', kv + [pltpu.V...  5.7 us
  transfers between devices with their start and end apart: 19, of which 11 were waited for; matrix products, arithmetic and copies ran while one was open for 2% of the time, Pallas kernels for 8%

profile of v3, /device:TPU:2, one launch (start us, length us, event | category | flops | bytes accessed | tf_op | source)
XLA Modules:
  0.0 178.4 jit_solution(13224867929470238951)
XLA Ops:
  0.6 1.0 copy-done.6
  1.6 1.0 copy-done.7
  2.6 1.0 copy-done.8
  4.3 1.7 pack.1
  6.0 6.0 %all-to-all-start = ((bf16[4,200,768]{2,1,0:T(8,128)(2,1)}), bf16[4,200,768]{2,1,0:T(8,128)(2,1)S(1)}, u32[]{:S(2)}, u32[]{:S(2)}) async-start(bf16[4,200,768]{2,1,0:T(8,128)(2,1)} %pack.1), calls=%async_computation | async-start | bytes 2457600 | tf_op jit(solution)/shard_map/all_to_all | solution.py:207
  12.0 13.9 %collective-permute-start = (bf16[32,2048]{1,0:T(8,128)(2,1)S(1)}, bf16[32,2048]{1,0:T(8,128)(2,1)S(1)}, u32[]{:S(2)}, u32[]{:S(2)}) collective-permute-start(bf16[32,2048]{1,0:T(8,128)(2,1)S(1)} %copy-done.17), channel_id=1, source_target_pairs={{384,64},{0,320},{416,96},{32,352},{448,128},{64,384},{480,160},{9... | collective-permute-start | bytes 393224 | tf_op jit(solution)/shard_map/ppermute | solution.py:219
  25.9 3.0 %collective-permute-start.1 = (bf16[32,2048]{1,0:T(8,128)(2,1)S(1)}, bf16[32,2048]{1,0:T(8,128)(2,1)S(1)}, u32[]{:S(2)}, u32[]{:S(2)}) collective-permute-start(bf16[32,2048]{1,0:T(8,128)(2,1)S(1)} %copy-done.17), channel_id=1, source_target_pairs={{256,32},{384,288},{0,96},{128,352},{32,0},{160,256},{288,64},{416... | collective-permute-start | bytes 393224 | tf_op jit(solution)/shard_map/ppermute | solution.py:222
  29.0 5.1 %collective-permute-done = bf16[32,2048]{1,0:T(8,128)(2,1)S(1)} collective-permute-done((bf16[32,2048]{1,0:T(8,128)(2,1)S(1)}, bf16[32,2048]{1,0:T(8,128)(2,1)S(1)}, u32[]{:S(2)}, u32[]{:S(2)}) %collective-permute-start) | collective-permute-done | bytes 131104 | tf_op jit(solution)/shard_map/ppermute | solution.py:219
  34.1 3.4 %collective-permute-done.1 = bf16[32,2048]{1,0:T(8,128)(2,1)S(1)} collective-permute-done((bf16[32,2048]{1,0:T(8,128)(2,1)S(1)}, bf16[32,2048]{1,0:T(8,128)(2,1)S(1)}, u32[]{:S(2)}, u32[]{:S(2)}) %collective-permute-start.1) | collective-permute-done | bytes 131104 | tf_op jit(solution)/shard_map/ppermute | solution.py:222
  37.5 11.6 %collective-permute-start.2 = (bf16[192,2048]{1,0:T(8,128)(2,1)S(1)}, bf16[192,2048]{1,0:T(8,128)(2,1)S(1)}, u32[]{:S(2)}, u32[]{:S(2)}) collective-permute-start(bf16[192,2048]{1,0:T(8,128)(2,1)S(1)} %bitcast.24), channel_id=1, source_target_pairs={{0,128},{128,0},{256,384},{384,256},{1,129},{129,1},{257,385},{385... | collective-permute-start | bytes 2359304 | tf_op jit(solution)/shard_map/ppermute | solution.py:199
  49.1 0.8 fusion
  50.0 4.9 %collective-permute-start.5 = (bf16[64,2048]{1,0:T(8,128)(2,1)}, bf16[64,2048]{1,0:T(8,128)(2,1)}, u32[]{:S(2)}, u32[]{:S(2)}) collective-permute-start(bf16[64,2048]{1,0:T(8,128)(2,1)} %get-tuple-element.45), channel_id=1, source_target_pairs={{0,24},{8,16},{16,8},{24,0},{1,25},{9,17},{17,9},{25,1},{2,26},{10... | collective-permute-start | bytes 786440 | tf_op jit(solution)/shard_map/ppermute | solution.py:199
  54.9 2.5 %collective-permute-start.4 = (bf16[64,2048]{1,0:T(8,128)(2,1)}, bf16[64,2048]{1,0:T(8,128)(2,1)}, u32[]{:S(2)}, u32[]{:S(2)}) collective-permute-start(bf16[64,2048]{1,0:T(8,128)(2,1)} %get-tuple-element.45), channel_id=1, source_target_pairs={{0,16},{8,24},{16,0},{24,8},{1,17},{9,25},{17,1},{25,9},{2,18},{10... | collective-permute-start | bytes 786440 | tf_op jit(solution)/shard_map/ppermute | solution.py:199
  57.5 2.4 %collective-permute-start.3 = (bf16[64,2048]{1,0:T(8,128)(2,1)}, bf16[64,2048]{1,0:T(8,128)(2,1)}, u32[]{:S(2)}, u32[]{:S(2)}) collective-permute-start(bf16[64,2048]{1,0:T(8,128)(2,1)} %get-tuple-element.45), channel_id=1, source_target_pairs={{0,8},{8,0},{16,24},{24,16},{1,9},{9,1},{17,25},{25,17},{2,10},{10... | collective-permute-start | bytes 786440 | tf_op jit(solution)/shard_map/ppermute | solution.py:199
  59.8 4.0 %forward.1 = (bf16[384,256]{1,0:T(8,128)(2,1)S(1)}, bf16[384,256]{1,0:T(8,128)(2,1)S(1)}, f32[768,256]{1,0:T(8,128)S(1)}) custom-call(s32[1]{0:T(128)} %bitcast.where, bf16[4,200,768]{2,1,0:T(8,128)(2,1)S(1)} %all-to-all-done.x_all), custom_call_target="tpu_custom_call" | custom-call | flops 1000 | bytes 1000 | tf_op jit(solution)/shard_map/forward/pallas_call | solution.py:242
  63.8 0.9 copy-done.4
  64.7 1.9 %collective-permute-start.8 = (bf16[384,256]{1,0:T(8,128)(2,1)S(1)}, bf16[384,256]{1,0:T(8,128)(2,1)S(1)}, u32[]{:S(2)}, u32[]{:S(2)}) collective-permute-start(bf16[384,256]{1,0:T(8,128)(2,1)S(1)} %get-tuple-element.30.o_far), channel_id=1, source_target_pairs={{0,256},{128,384},{256,0},{384,128},{1,257},{129,385},{257,1},{385... | collective-permute-start | bytes 589832 | tf_op jit(solution)/shard_map/ppermute | solution.py:199
  66.7 1.2 collective-permute-done.4
  68.5 7.6 %collective-permute-done.8.o_there = bf16[384,256]{1,0:T(8,128)(2,1)S(1)} collective-permute-done((bf16[384,256]{1,0:T(8,128)(2,1)S(1)}, bf16[384,256]{1,0:T(8,128)(2,1)S(1)}, u32[]{:S(2)}, u32[]{:S(2)}) %collective-permute-start.8) | collective-permute-done | bytes 196640 | tf_op jit(solution)/shard_map/ppermute | solution.py:199
  76.2 1.3 weight.1
  77.5 1.9 %collective-permute-start.9 = (bf16[4,4,2,32,512]{4,3,2,1,0:T(8,128)(2,1)S(1)}, bf16[4,4,2,32,512]{4,3,2,1,0:T(8,128)(2,1)S(1)}, u32[]{:S(2)}, u32[]{:S(2)}) collective-permute-start(bf16[4,4,2,32,512]{4,3,2,1,0:T(8,128)(2,1)S(1)} %get-tuple-element.34), channel_id=1, source_target_pairs={{0,4},{4,0},{1,5},{5,1},{2,6},{6,2},{3,7},{7,3},{8,12},{12,8},{9,1... | collective-permute-start | bytes 3145736 | tf_op jit(solution)/shard_map/ppermute | solution.py:199
  79.4 1.2 pad_maximum_fusion.w_here
  80.7 2.4 %collective-permute-start.6 = (bf16[4,64,2048]{2,1,0:T(8,128)(2,1)S(1)}, bf16[4,64,2048]{2,1,0:T(8,128)(2,1)}, u32[]{:S(2)}, u32[]{:S(2)}) collective-permute-start(bf16[4,64,2048]{2,1,0:T(8,128)(2,1)S(1)} %pad_maximum_fusion.w_here), channel_id=1, source_target_pairs={{0,4},{4,0},{1,5},{5,1},{2,6},{6,2},{3,7},{7,3},{8,12},{12,8},{9,1... | collective-permute-start | bytes 3145736 | tf_op jit(solution)/shard_map/ppermute | solution.py:199
  83.1 1.4 add_convert_fusion
  84.5 7.4 %all-to-all-start.1 = ((bf16[16,2,32,512]{3,2,1,0:T(8,128)(2,1)}), bf16[16,2,32,512]{3,2,1,0:T(8,128)(2,1)S(1)}, u32[]{:S(2)}, u32[]{:S(2)}) async-start(bf16[16,2,32,512]{3,2,1,0:T(8,128)(2,1)} %bitcast.30), calls=%async_computation.1 | async-start | bytes 2097152 | tf_op jit(solution)/shard_map/all_to_all | solution.py:207
  92.0 1.1 copy-done.1
  93.1 1.1 copy-done.3
  94.2 3.4 %project.1 = (bf16[384,256]{1,0:T(8,128)(2,1)S(1)}, bf16[384,256]{1,0:T(8,128)(2,1)}) custom-call(s32[6]{0:T(128)S(1)} %stack.63.where, bf16[192,2048]{1,0:T(8,128)(2,1)S(1)} %bitcast.26, bf16[192,2048]{1,0:T(8,128)(2,1)S(1)} %copy-done.3, bf16[4,64,2048]{2,1,0:T(8,128)(2,1)S(1)} %pad_maximum_fusion.w_here, bf16[4,64,2048]{2,1,0:T(8,128)(2,1)} %collective-permute-done.6.w_there), custom_call_target="tpu_custom_call" | custom-call | flops 1000 | bytes 1000 | tf_op jit(solution)/shard_map/project/pallas_call | solution.py:237
  97.7 0.7 copy-done.11
  98.3 2.0 %collective-permute-start.7 = (bf16[384,256]{1,0:T(8,128)(2,1)}, bf16[384,256]{1,0:T(8,128)(2,1)S(1)}, u32[]{:S(2)}, u32[]{:S(2)}) collective-permute-start(bf16[384,256]{1,0:T(8,128)(2,1)} %get-tuple-element.28), channel_id=1, source_target_pairs={{0,256},{128,384},{256,0},{384,128},{1,257},{129,385},{257,1},{385... | collective-permute-start | bytes 589832 | tf_op jit(solution)/shard_map/ppermute | solution.py:199
  100.4 7.5 %all-to-all-done.1.parts = bf16[16,2,32,512]{3,2,1,0:T(8,128)(2,1)S(1)} async-done(((bf16[16,2,32,512]{3,2,1,0:T(8,128)(2,1)}), bf16[16,2,32,512]{3,2,1,0:T(8,128)(2,1)S(1)}, u32[]{:S(2)}, u32[]{:S(2)}) %all-to-all-start.1) | async-done | bytes 1048608 | tf_op jit(solution)/shard_map/all_to_all | solution.py:207
  108.0 1.6 collective-permute-done.7.g_far
  110.3 6.4 %collective-permute-start.11 = (bf16[32,512]{1,0:T(8,128)(2,1)S(1)}, bf16[32,512]{1,0:T(8,128)(2,1)S(1)}, u32[]{:S(2)}, u32[]{:S(2)}) collective-permute-start(bf16[32,512]{1,0:T(8,128)(2,1)S(1)} %get-tuple-element.38), channel_id=1, source_target_pairs={{0,32},{32,288},{64,160},{96,416},{128,96},{160,352},{192,224},{22... | collective-permute-start | bytes 98312 | tf_op jit(solution)/shard_map/ppermute | solution.py:265
  116.6 1.6 collective-permute-done.11
  118.9 18.1 %all-to-all-start.2 = ((bf16[4,32,512]{2,1,0:T(8,128)(2,1)}), bf16[4,32,512]{2,1,0:T(8,128)(2,1)S(1)}, u32[]{:S(2)}, u32[]{:S(2)}) async-start(bf16[4,32,512]{2,1,0:T(8,128)(2,1)} %broadcast_in_dim.15), calls=%async_computation.2 | async-start | bytes 262144 | tf_op jit(solution)/shard_map/all_to_all | solution.py:207
  137.0 0.9 copy-done.10
  137.9 0.9 copy-done.12
  138.8 0.9 copy-done.14
  139.7 5.7 %backward.1 = bf16[4,192,768]{2,1,0:T(8,128)(2,1)} custom-call(s32[1]{0:T(128)} %bitcast.where, bf16[4,200,768]{2,1,0:T(8,128)(2,1)S(1)} %all-to-all-done.x_all, bf16[384,256]{1,0:T(8,128)(2,1)S(1)} %copy-done.12, bf16[384,256]{1,0:T(8,128)(2,1)S(1)} %copy-done.14, bf16[384,256]{1,0:T(8,128)(2,1)S(1)} %get-tuple-element.29.o_near.o_here, ...), custom_call_target="tpu_custom_call" | custom-call | flops 1000 | bytes 1000 | tf_op jit(solution)/shard_map/backward/pallas_call | solution.py:251
  145.5 5.1 %all-to-all-start.3 = ((bf16[4,192,768]{2,1,0:T(8,128)(2,1)}), bf16[4,192,768]{2,1,0:T(8,128)(2,1)S(1)}, u32[]{:S(2)}, u32[]{:S(2)}) async-start(bf16[4,192,768]{2,1,0:T(8,128)(2,1)} %backward.1), calls=%async_computation.3 | async-start | bytes 2359296 | tf_op jit(solution)/shard_map/all_to_all | solution.py:207
  150.6 3.4 %collective-permute-start.14 = (bf16[32,512]{1,0:T(8,128)(2,1)S(1)}, bf16[32,512]{1,0:T(8,128)(2,1)S(1)}, u32[]{:S(2)}, u32[]{:S(2)}) collective-permute-start(bf16[32,512]{1,0:T(8,128)(2,1)S(1)} %quarter.1.p0), channel_id=1, source_target_pairs={{0,3},{1,2},{2,1},{3,0},{4,7},{5,6},{6,5},{7,4},{8,11},{9,10},{10,... | collective-permute-start | bytes 98312 | tf_op jit(solution)/shard_map/ppermute | solution.py:199
  153.9 2.9 %collective-permute-start.13 = (bf16[32,512]{1,0:T(8,128)(2,1)S(1)}, bf16[32,512]{1,0:T(8,128)(2,1)S(1)}, u32[]{:S(2)}, u32[]{:S(2)}) collective-permute-start(bf16[32,512]{1,0:T(8,128)(2,1)S(1)} %quarter.1.p0), channel_id=1, source_target_pairs={{0,2},{1,3},{2,0},{3,1},{4,6},{5,7},{6,4},{7,5},{8,10},{9,11},{10,... | collective-permute-start | bytes 98312 | tf_op jit(solution)/shard_map/ppermute | solution.py:199
  156.8 3.5 %collective-permute-start.12 = (bf16[32,512]{1,0:T(8,128)(2,1)S(1)}, bf16[32,512]{1,0:T(8,128)(2,1)S(1)}, u32[]{:S(2)}, u32[]{:S(2)}) collective-permute-start(bf16[32,512]{1,0:T(8,128)(2,1)S(1)} %quarter.1.p0), channel_id=1, source_target_pairs={{0,1},{1,0},{2,3},{3,2},{4,5},{5,4},{6,7},{7,6},{8,9},{9,8},{10,11... | collective-permute-start | bytes 98312 | tf_op jit(solution)/shard_map/ppermute | solution.py:199
  160.5 0.8 collective-permute-done.13.p2
  161.2 1.4 collective-permute-done.12.p1
  162.7 1.2 finish.1
  163.9 13.4 %all-to-all-done.3.home = bf16[4,192,768]{2,1,0:T(8,128)(2,1)S(1)} async-done(((bf16[4,192,768]{2,1,0:T(8,128)(2,1)}), bf16[4,192,768]{2,1,0:T(8,128)(2,1)S(1)}, u32[]{:S(2)}, u32[]{:S(2)}) %all-to-all-start.3) | async-done | bytes 1179680 | tf_op jit(solution)/shard_map/all_to_all | solution.py:207
  177.3 1.2 unpack.1
  (43 shorter events, 3.0 us)
Async XLA Ops:
  0.6 1.0 copy-start.6
  1.6 1.0 copy-start.7
  2.6 1.0 copy-start.8
  3.6 0.7 copy-start.15
  6.0 6.0 %copy-start.17 = (bf16[32,2048]{1,0:T(8,128)(2,1)S(1)}, bf16[32,2048]{1,0:T(8,128)(2,1)}, u32[]{:S(2)}) copy-start(bf16[32,2048]{1,0:T(8,128)(2,1)} %param.9) | copy-start | bytes 393220
  6.0 31.5 %copy-start = (bf16[1,192,2048]{2,1,0:T(8,128)(2,1)S(1)}, bf16[1,192,2048]{2,1,0:T(8,128)(2,1)}, u32[]{:S(2)}) copy-start(bf16[1,192,2048]{2,1,0:T(8,128)(2,1)} %param.10) | copy-start | bytes 2359300
  6.0 53.9 %all-to-all-start = ((bf16[4,200,768]{2,1,0:T(8,128)(2,1)}), bf16[4,200,768]{2,1,0:T(8,128)(2,1)S(1)}, u32[]{:S(2)}, u32[]{:S(2)}) async-start(bf16[4,200,768]{2,1,0:T(8,128)(2,1)} %pack.1), calls=%async_computation | async-start | bytes 2457600 | tf_op jit(solution)/shard_map/all_to_all | solution.py:207
  12.0 22.1 %collective-permute-start = (bf16[32,2048]{1,0:T(8,128)(2,1)S(1)}, bf16[32,2048]{1,0:T(8,128)(2,1)S(1)}, u32[]{:S(2)}, u32[]{:S(2)}) collective-permute-start(bf16[32,2048]{1,0:T(8,128)(2,1)S(1)} %copy-done.17), channel_id=1, source_target_pairs={{384,64},{0,320},{416,96},{32,352},{448,128},{64,384},{480,160},{9... | collective-permute-start | bytes 393224 | tf_op jit(solution)/shard_map/ppermute | solution.py:219
  25.9 11.6 %collective-permute-start.1 = (bf16[32,2048]{1,0:T(8,128)(2,1)S(1)}, bf16[32,2048]{1,0:T(8,128)(2,1)S(1)}, u32[]{:S(2)}, u32[]{:S(2)}) collective-permute-start(bf16[32,2048]{1,0:T(8,128)(2,1)S(1)} %copy-done.17), channel_id=1, source_target_pairs={{256,32},{384,288},{0,96},{128,352},{32,0},{160,256},{288,64},{416... | collective-permute-start | bytes 393224 | tf_op jit(solution)/shard_map/ppermute | solution.py:222
  37.5 38.7 %collective-permute-start.2 = (bf16[192,2048]{1,0:T(8,128)(2,1)S(1)}, bf16[192,2048]{1,0:T(8,128)(2,1)S(1)}, u32[]{:S(2)}, u32[]{:S(2)}) collective-permute-start(bf16[192,2048]{1,0:T(8,128)(2,1)S(1)} %bitcast.24), channel_id=1, source_target_pairs={{0,128},{128,0},{256,384},{384,256},{1,129},{129,1},{257,385},{385... | collective-permute-start | bytes 2359304 | tf_op jit(solution)/shard_map/ppermute | solution.py:199
  50.0 16.7 %collective-permute-start.5 = (bf16[64,2048]{1,0:T(8,128)(2,1)}, bf16[64,2048]{1,0:T(8,128)(2,1)}, u32[]{:S(2)}, u32[]{:S(2)}) collective-permute-start(bf16[64,2048]{1,0:T(8,128)(2,1)} %get-tuple-element.45), channel_id=1, source_target_pairs={{0,24},{8,16},{16,8},{24,0},{1,25},{9,17},{17,9},{25,1},{2,26},{10... | collective-permute-start | bytes 786440 | tf_op jit(solution)/shard_map/ppermute | solution.py:199
  54.9 13.0 %collective-permute-start.4 = (bf16[64,2048]{1,0:T(8,128)(2,1)}, bf16[64,2048]{1,0:T(8,128)(2,1)}, u32[]{:S(2)}, u32[]{:S(2)}) collective-permute-start(bf16[64,2048]{1,0:T(8,128)(2,1)} %get-tuple-element.45), channel_id=1, source_target_pairs={{0,16},{8,24},{16,0},{24,8},{1,17},{9,25},{17,1},{25,9},{2,18},{10... | collective-permute-start | bytes 786440 | tf_op jit(solution)/shard_map/ppermute | solution.py:199
  57.5 11.1 %collective-permute-start.3 = (bf16[64,2048]{1,0:T(8,128)(2,1)}, bf16[64,2048]{1,0:T(8,128)(2,1)}, u32[]{:S(2)}, u32[]{:S(2)}) collective-permute-start(bf16[64,2048]{1,0:T(8,128)(2,1)} %get-tuple-element.45), channel_id=1, source_target_pairs={{0,8},{8,0},{16,24},{24,16},{1,9},{9,1},{17,25},{25,17},{2,10},{10... | collective-permute-start | bytes 786440 | tf_op jit(solution)/shard_map/ppermute | solution.py:199
  63.8 0.9 copy-start.4
  64.7 14.7 %copy-start.9 = (bf16[384,256]{1,0:T(8,128)(2,1)}, bf16[384,256]{1,0:T(8,128)(2,1)S(1)}, u32[]{:S(2)}) copy-start(bf16[384,256]{1,0:T(8,128)(2,1)S(1)} %get-tuple-element.30.o_far) | copy-start | bytes 589828
  64.7 11.4 %collective-permute-start.8 = (bf16[384,256]{1,0:T(8,128)(2,1)S(1)}, bf16[384,256]{1,0:T(8,128)(2,1)S(1)}, u32[]{:S(2)}, u32[]{:S(2)}) collective-permute-start(bf16[384,256]{1,0:T(8,128)(2,1)S(1)} %get-tuple-element.30.o_far), channel_id=1, source_target_pairs={{0,256},{128,384},{256,0},{384,128},{1,257},{129,385},{257,1},{385... | collective-permute-start | bytes 589832 | tf_op jit(solution)/shard_map/ppermute | solution.py:199
  66.6 12.8 %copy-start.16 = (bf16[1,64,2048]{2,1,0:T(8,128)(2,1)S(1)}, bf16[1,64,2048]{2,1,0:T(8,128)(2,1)}, u32[]{:S(2)}) copy-start(bf16[1,64,2048]{2,1,0:T(8,128)(2,1)} %get-tuple-element.44) | copy-start | bytes 786436
  76.2 3.2 %copy-start.2 = (bf16[192,2048]{1,0:T(8,128)(2,1)}, bf16[192,2048]{1,0:T(8,128)(2,1)S(1)}, u32[]{:S(2)}) copy-start(bf16[192,2048]{1,0:T(8,128)(2,1)S(1)} %collective-permute-done.2.mate_ref) | copy-start | bytes 2359300
  77.5 5.6 %collective-permute-start.9 = (bf16[4,4,2,32,512]{4,3,2,1,0:T(8,128)(2,1)S(1)}, bf16[4,4,2,32,512]{4,3,2,1,0:T(8,128)(2,1)S(1)}, u32[]{:S(2)}, u32[]{:S(2)}) collective-permute-start(bf16[4,4,2,32,512]{4,3,2,1,0:T(8,128)(2,1)S(1)} %get-tuple-element.34), channel_id=1, source_target_pairs={{0,4},{4,0},{1,5},{5,1},{2,6},{6,2},{3,7},{7,3},{8,12},{12,8},{9,1... | collective-permute-start | bytes 3145736 | tf_op jit(solution)/shard_map/ppermute | solution.py:199
  80.7 11.3 %collective-permute-start.6 = (bf16[4,64,2048]{2,1,0:T(8,128)(2,1)S(1)}, bf16[4,64,2048]{2,1,0:T(8,128)(2,1)}, u32[]{:S(2)}, u32[]{:S(2)}) collective-permute-start(bf16[4,64,2048]{2,1,0:T(8,128)(2,1)S(1)} %pad_maximum_fusion.w_here), channel_id=1, source_target_pairs={{0,4},{4,0},{1,5},{5,1},{2,6},{6,2},{3,7},{7,3},{8,12},{12,8},{9,1... | collective-permute-start | bytes 3145736 | tf_op jit(solution)/shard_map/ppermute | solution.py:199
  84.5 23.4 %all-to-all-start.1 = ((bf16[16,2,32,512]{3,2,1,0:T(8,128)(2,1)}), bf16[16,2,32,512]{3,2,1,0:T(8,128)(2,1)S(1)}, u32[]{:S(2)}, u32[]{:S(2)}) async-start(bf16[16,2,32,512]{3,2,1,0:T(8,128)(2,1)} %bitcast.30), calls=%async_computation.1 | async-start | bytes 2097152 | tf_op jit(solution)/shard_map/all_to_all | solution.py:207
  92.0 1.1 copy-start.1
  93.1 1.1 copy-start.3
  97.7 0.7 copy-start.11
  98.3 38.6 %copy-start.5 = (f32[768,256]{1,0:T(8,128)S(1)}, f32[768,256]{1,0:T(8,128)}, u32[]{:S(2)}) copy-start(f32[768,256]{1,0:T(8,128)} %copy-done.4) | copy-start | bytes 2359300
  98.3 11.2 %collective-permute-start.7 = (bf16[384,256]{1,0:T(8,128)(2,1)}, bf16[384,256]{1,0:T(8,128)(2,1)S(1)}, u32[]{:S(2)}, u32[]{:S(2)}) collective-permute-start(bf16[384,256]{1,0:T(8,128)(2,1)} %get-tuple-element.28), channel_id=1, source_target_pairs={{0,256},{128,384},{256,0},{384,128},{1,257},{129,385},{257,1},{385... | collective-permute-start | bytes 589832 | tf_op jit(solution)/shard_map/ppermute | solution.py:199
  109.6 9.3 %copy-start.13 = (bf16[384,256]{1,0:T(8,128)(2,1)}, bf16[384,256]{1,0:T(8,128)(2,1)S(1)}, u32[]{:S(2)}) copy-start(bf16[384,256]{1,0:T(8,128)(2,1)S(1)} %collective-permute-done.7.g_far) | copy-start | bytes 589828
  109.6 7.0 %collective-permute-start.10 = (bf16[32,512]{1,0:T(8,128)(2,1)S(1)}, bf16[32,512]{1,0:T(8,128)(2,1)S(1)}, u32[]{:S(2)}, u32[]{:S(2)}) collective-permute-start(bf16[32,512]{1,0:T(8,128)(2,1)S(1)} %get-tuple-element.37), channel_id=1, source_target_pairs={{0,0},{32,256},{64,128},{96,384},{128,64},{160,320},{192,192},{224... | collective-permute-start | bytes 98312 | tf_op jit(solution)/shard_map/ppermute | solution.py:265
  110.3 8.0 %collective-permute-start.11 = (bf16[32,512]{1,0:T(8,128)(2,1)S(1)}, bf16[32,512]{1,0:T(8,128)(2,1)S(1)}, u32[]{:S(2)}, u32[]{:S(2)}) collective-permute-start(bf16[32,512]{1,0:T(8,128)(2,1)S(1)} %get-tuple-element.38), channel_id=1, source_target_pairs={{0,32},{32,288},{64,160},{96,416},{128,96},{160,352},{192,224},{22... | collective-permute-start | bytes 98312 | tf_op jit(solution)/shard_map/ppermute | solution.py:265
  118.9 26.5 %all-to-all-start.2 = ((bf16[4,32,512]{2,1,0:T(8,128)(2,1)}), bf16[4,32,512]{2,1,0:T(8,128)(2,1)S(1)}, u32[]{:S(2)}, u32[]{:S(2)}) async-start(bf16[4,32,512]{2,1,0:T(8,128)(2,1)} %broadcast_in_dim.15), calls=%async_computation.2 | async-start | bytes 262144 | tf_op jit(solution)/shard_map/all_to_all | solution.py:207
  137.0 0.9 copy-start.10
  137.9 0.9 copy-start.12
  138.8 0.9 copy-start.14
  145.5 31.8 %all-to-all-start.3 = ((bf16[4,192,768]{2,1,0:T(8,128)(2,1)}), bf16[4,192,768]{2,1,0:T(8,128)(2,1)S(1)}, u32[]{:S(2)}, u32[]{:S(2)}) async-start(bf16[4,192,768]{2,1,0:T(8,128)(2,1)} %backward.1), calls=%async_computation.3 | async-start | bytes 2359296 | tf_op jit(solution)/shard_map/all_to_all | solution.py:207
  150.6 9.9 %collective-permute-start.14 = (bf16[32,512]{1,0:T(8,128)(2,1)S(1)}, bf16[32,512]{1,0:T(8,128)(2,1)S(1)}, u32[]{:S(2)}, u32[]{:S(2)}) collective-permute-start(bf16[32,512]{1,0:T(8,128)(2,1)S(1)} %quarter.1.p0), channel_id=1, source_target_pairs={{0,3},{1,2},{2,1},{3,0},{4,7},{5,6},{6,5},{7,4},{8,11},{9,10},{10,... | collective-permute-start | bytes 98312 | tf_op jit(solution)/shard_map/ppermute | solution.py:199
  153.9 7.3 %collective-permute-start.13 = (bf16[32,512]{1,0:T(8,128)(2,1)S(1)}, bf16[32,512]{1,0:T(8,128)(2,1)S(1)}, u32[]{:S(2)}, u32[]{:S(2)}) collective-permute-start(bf16[32,512]{1,0:T(8,128)(2,1)S(1)} %quarter.1.p0), channel_id=1, source_target_pairs={{0,2},{1,3},{2,0},{3,1},{4,6},{5,7},{6,4},{7,5},{8,10},{9,11},{10,... | collective-permute-start | bytes 98312 | tf_op jit(solution)/shard_map/ppermute | solution.py:199
  156.8 5.8 %collective-permute-start.12 = (bf16[32,512]{1,0:T(8,128)(2,1)S(1)}, bf16[32,512]{1,0:T(8,128)(2,1)S(1)}, u32[]{:S(2)}, u32[]{:S(2)}) collective-permute-start(bf16[32,512]{1,0:T(8,128)(2,1)S(1)} %quarter.1.p0), channel_id=1, source_target_pairs={{0,1},{1,0},{2,3},{3,2},{4,5},{5,4},{6,7},{7,6},{8,9},{9,8},{10,11... | collective-permute-start | bytes 98312 | tf_op jit(solution)/shard_map/ppermute | solution.py:199

commit v4 on v3

--- a/solution.py
+++ b/solution.py
@@ -64,8 +64,8 @@
         dv[:, cols] = home[j, :, 512:768]
 
 
-def quarter_kernel(parts, out):
-    t = [parts[j].astype(F32) for j in range(4)]
+def quarter_kernel(p0, p1, p2, p3, out):
+    t = [ref[...].astype(F32) for ref in (p0, p1, p2, p3)]
     total = (t[0] + t[1]) + (t[2] + t[3])
     out[...] = (total * (1.0 / math.sqrt(192 * 512))).astype(BF16)
 
@@ -259,14 +259,14 @@
     both = (keep.astype(F32) + taken.astype(F32)).astype(BF16).reshape(16, 2, 32, 512)
     parts = exchange(both, ("y", "dp"))
     own, other = call(sum_kernel, [arr((32, 512))] * 2, 0, 1, "sum")(parts)
-    own, other, g_far = lax.optimization_barrier((own, other, g_far))
     turn = [(i * 4 + j, group_of(j) * 4 + group_of(i)) for i in range(4) for j in range(4)]
     turn2 = [(i * 4 + j, group_of(j) * 4 + (group_of(i) ^ 1)) for i in range(4) for j in range(4)]
     line = lax.ppermute(own, z, turn).astype(F32) + lax.ppermute(other, z, turn2).astype(F32)
-    spread = jnp.broadcast_to(line.astype(BF16)[None], (4, 32, 512))
-    quarter = call(quarter_kernel, arr((32, 512)), 0, 1, "quarter")(exchange(spread, "seq"))
-    back, quarter = lax.optimization_barrier((back, quarter))
+    line = line.astype(BF16)
+    back, line = lax.optimization_barrier((back, line))
     home = exchange(back, "seq")
+    lines = [line] + [swap(line, "seq", k, 4) for k in (1, 2, 3)]
+    quarter = call(quarter_kernel, arr((32, 512)), 0, 4, "quarter")(*lines)
     quarters = [quarter] + [swap(quarter, "dp", k, 4) for k in (1, 2, 3)]
     weight_grad = call(finish_kernel, arr((32, 2048)), 1, 4, "finish")(
         scalars(*(x ^ k for k in range(4))), *quarters

time: 180 us -> 178 us (0.989)
  starting transfers between devices: 100 us -> 95.3 us
  waiting for transfers between devices: 44.2 us -> 47.3 us
    ppermute x11 -> x14, waiting for transfers between devices: 13.3 us -> 31.3 us  [swap(): return lax.ppermute(value, axis, [(i, i ^ mask) for i in range(n)])]
    all_to_all x4 -> x3, starting transfers between devices: 36.6 us -> 21.6 us  [exchange(): return lax.all_to_all(value, axes, 0, 0, tiled=True)]
    all_to_all x4 -> x3, waiting for transfers between devices: 20.9 us -> 7.5 us  [exchange(): return lax.all_to_all(value, axes, 0, 0, tiled=True)]
    ppermute x11 -> x14, starting transfers between devices: 39.5 us -> 49.7 us  [swap(): return lax.ppermute(value, axis, [(i, i ^ mask) for i in range(n)])]
  transfers between devices with their start and end apart: 19 -> 21, of which waited for: 11 -> 10; matrix products, arithmetic and copies ran while one was open for 2% -> 2% of each run, Pallas kernels for 8% -> 8%
where the time goes in v4:
time: 178 us; the launch traced here: 177 us
  starting transfers between devices  95.3 us (54%)
  waiting for transfers between devices  47.3 us (27%)
  Pallas kernels  18.6 us (10%)
  local copies, waits for them, and re-layouts  11 us (6%)
  other arithmetic  3.61 us (2%)
    ppermute x14, starting transfers between devices, swap(): return lax.ppermute(value, axis, [(i, i ^ mask) for i in range(n)])  49.7 us
    ppermute x14, waiting for transfers between devices, swap(): return lax.ppermute(value, axis, [(i, i ^ mask) for i in range(n)])  31.3 us
    all_to_all x3, starting transfers between devices, exchange(): return lax.all_to_all(value, axes, 0, 0, tiled=True)  21.6 us
    ppermute x1, starting transfers between devices, shards(): lax.ppermute(out_weight, z, nearest([d for d in places if d[0] // 2 != d[...  13.9 us
    unnamed x36, local copies, waits for them, and re-layouts  10.9 us
    all_to_all x3, waiting for transfers between devices, exchange(): return lax.all_to_all(value, axes, 0, 0, tiled=True)  7.5 us
    ppermute x1, starting transfers between devices, shards(): lax.ppermute(other, z, turn2).astype(F32)  6.45 us
    pallas_call x1, Pallas kernels, shards(): call(backward_kernel, arr((4, 192, 768)), 1, 6, 'backward', kv + [pltpu.V...  5.71 us
  transfers between devices with their start and end apart: 21, of which 10 were waited for; matrix products, arithmetic and copies ran while one was open for 2% of the time, Pallas kernels for 8%

profile of v4, /device:TPU:2, one launch (start us, length us, event | category | flops | bytes accessed | tf_op | source)
XLA Modules:
  0.0 176.8 jit_solution(16240292815483742581)
XLA Ops:
  0.6 1.0 copy-done.6
  1.6 1.0 copy-done.7
  2.6 1.0 copy-done.8
  4.3 1.7 pack.1
  6.0 6.0 %all-to-all-start = ((bf16[4,200,768]{2,1,0:T(8,128)(2,1)}), bf16[4,200,768]{2,1,0:T(8,128)(2,1)S(1)}, u32[]{:S(2)}, u32[]{:S(2)}) async-start(bf16[4,200,768]{2,1,0:T(8,128)(2,1)} %pack.1), calls=%async_computation | async-start | bytes 2457600 | tf_op jit(solution)/shard_map/all_to_all | solution.py:207
  12.0 13.9 %collective-permute-start = (bf16[32,2048]{1,0:T(8,128)(2,1)S(1)}, bf16[32,2048]{1,0:T(8,128)(2,1)S(1)}, u32[]{:S(2)}, u32[]{:S(2)}) collective-permute-start(bf16[32,2048]{1,0:T(8,128)(2,1)S(1)} %copy-done.17), channel_id=1, source_target_pairs={{384,64},{0,320},{416,96},{32,352},{448,128},{64,384},{480,160},{9... | collective-permute-start | bytes 393224 | tf_op jit(solution)/shard_map/ppermute | solution.py:219
  25.9 3.0 %collective-permute-start.1 = (bf16[32,2048]{1,0:T(8,128)(2,1)S(1)}, bf16[32,2048]{1,0:T(8,128)(2,1)S(1)}, u32[]{:S(2)}, u32[]{:S(2)}) collective-permute-start(bf16[32,2048]{1,0:T(8,128)(2,1)S(1)} %copy-done.17), channel_id=1, source_target_pairs={{256,32},{384,288},{0,96},{128,352},{32,0},{160,256},{288,64},{416... | collective-permute-start | bytes 393224 | tf_op jit(solution)/shard_map/ppermute | solution.py:222
  29.0 5.1 %collective-permute-done = bf16[32,2048]{1,0:T(8,128)(2,1)S(1)} collective-permute-done((bf16[32,2048]{1,0:T(8,128)(2,1)S(1)}, bf16[32,2048]{1,0:T(8,128)(2,1)S(1)}, u32[]{:S(2)}, u32[]{:S(2)}) %collective-permute-start) | collective-permute-done | bytes 131104 | tf_op jit(solution)/shard_map/ppermute | solution.py:219
  34.1 3.4 %collective-permute-done.1 = bf16[32,2048]{1,0:T(8,128)(2,1)S(1)} collective-permute-done((bf16[32,2048]{1,0:T(8,128)(2,1)S(1)}, bf16[32,2048]{1,0:T(8,128)(2,1)S(1)}, u32[]{:S(2)}, u32[]{:S(2)}) %collective-permute-start.1) | collective-permute-done | bytes 131104 | tf_op jit(solution)/shard_map/ppermute | solution.py:222
  37.5 11.6 %collective-permute-start.2 = (bf16[192,2048]{1,0:T(8,128)(2,1)S(1)}, bf16[192,2048]{1,0:T(8,128)(2,1)S(1)}, u32[]{:S(2)}, u32[]{:S(2)}) collective-permute-start(bf16[192,2048]{1,0:T(8,128)(2,1)S(1)} %bitcast.24), channel_id=1, source_target_pairs={{0,128},{128,0},{256,384},{384,256},{1,129},{129,1},{257,385},{385... | collective-permute-start | bytes 2359304 | tf_op jit(solution)/shard_map/ppermute | solution.py:199
  49.2 0.8 fusion
  50.0 4.9 %collective-permute-start.5 = (bf16[64,2048]{1,0:T(8,128)(2,1)}, bf16[64,2048]{1,0:T(8,128)(2,1)}, u32[]{:S(2)}, u32[]{:S(2)}) collective-permute-start(bf16[64,2048]{1,0:T(8,128)(2,1)} %get-tuple-element.41), channel_id=1, source_target_pairs={{0,24},{8,16},{16,8},{24,0},{1,25},{9,17},{17,9},{25,1},{2,26},{10... | collective-permute-start | bytes 786440 | tf_op jit(solution)/shard_map/ppermute | solution.py:199
  54.9 2.5 %collective-permute-start.4 = (bf16[64,2048]{1,0:T(8,128)(2,1)}, bf16[64,2048]{1,0:T(8,128)(2,1)}, u32[]{:S(2)}, u32[]{:S(2)}) collective-permute-start(bf16[64,2048]{1,0:T(8,128)(2,1)} %get-tuple-element.41), channel_id=1, source_target_pairs={{0,16},{8,24},{16,0},{24,8},{1,17},{9,25},{17,1},{25,9},{2,18},{10... | collective-permute-start | bytes 786440 | tf_op jit(solution)/shard_map/ppermute | solution.py:199
  57.5 2.4 %collective-permute-start.3 = (bf16[64,2048]{1,0:T(8,128)(2,1)}, bf16[64,2048]{1,0:T(8,128)(2,1)}, u32[]{:S(2)}, u32[]{:S(2)}) collective-permute-start(bf16[64,2048]{1,0:T(8,128)(2,1)} %get-tuple-element.41), channel_id=1, source_target_pairs={{0,8},{8,0},{16,24},{24,16},{1,9},{9,1},{17,25},{25,17},{2,10},{10... | collective-permute-start | bytes 786440 | tf_op jit(solution)/shard_map/ppermute | solution.py:199
  59.8 4.0 %forward.1 = (bf16[384,256]{1,0:T(8,128)(2,1)S(1)}, bf16[384,256]{1,0:T(8,128)(2,1)S(1)}, f32[768,256]{1,0:T(8,128)S(1)}) custom-call(s32[1]{0:T(128)} %bitcast.where, bf16[4,200,768]{2,1,0:T(8,128)(2,1)S(1)} %all-to-all-done.x_all), custom_call_target="tpu_custom_call" | custom-call | flops 1000 | bytes 1000 | tf_op jit(solution)/shard_map/forward/pallas_call | solution.py:242
  63.8 0.9 copy-done.4
  64.7 1.9 %collective-permute-start.8 = (bf16[384,256]{1,0:T(8,128)(2,1)S(1)}, bf16[384,256]{1,0:T(8,128)(2,1)S(1)}, u32[]{:S(2)}, u32[]{:S(2)}) collective-permute-start(bf16[384,256]{1,0:T(8,128)(2,1)S(1)} %get-tuple-element.28.o_far), channel_id=1, source_target_pairs={{0,256},{128,384},{256,0},{384,128},{1,257},{129,385},{257,1},{385... | collective-permute-start | bytes 589832 | tf_op jit(solution)/shard_map/ppermute | solution.py:199
  66.7 1.2 collective-permute-done.4
  68.5 7.6 %collective-permute-done.8.o_there = bf16[384,256]{1,0:T(8,128)(2,1)S(1)} collective-permute-done((bf16[384,256]{1,0:T(8,128)(2,1)S(1)}, bf16[384,256]{1,0:T(8,128)(2,1)S(1)}, u32[]{:S(2)}, u32[]{:S(2)}) %collective-permute-start.8) | collective-permute-done | bytes 196640 | tf_op jit(solution)/shard_map/ppermute | solution.py:199
  76.2 1.3 weight.1
  77.5 1.9 %collective-permute-start.9 = (bf16[4,4,2,32,512]{4,3,2,1,0:T(8,128)(2,1)S(1)}, bf16[4,4,2,32,512]{4,3,2,1,0:T(8,128)(2,1)S(1)}, u32[]{:S(2)}, u32[]{:S(2)}) collective-permute-start(bf16[4,4,2,32,512]{4,3,2,1,0:T(8,128)(2,1)S(1)} %get-tuple-element.32), channel_id=1, source_target_pairs={{0,4},{4,0},{1,5},{5,1},{2,6},{6,2},{3,7},{7,3},{8,12},{12,8},{9,1... | collective-permute-start | bytes 3145736 | tf_op jit(solution)/shard_map/ppermute | solution.py:199
  79.4 1.2 pad_maximum_fusion.w_here
  80.7 2.4 %collective-permute-start.6 = (bf16[4,64,2048]{2,1,0:T(8,128)(2,1)S(1)}, bf16[4,64,2048]{2,1,0:T(8,128)(2,1)}, u32[]{:S(2)}, u32[]{:S(2)}) collective-permute-start(bf16[4,64,2048]{2,1,0:T(8,128)(2,1)S(1)} %pad_maximum_fusion.w_here), channel_id=1, source_target_pairs={{0,4},{4,0},{1,5},{5,1},{2,6},{6,2},{3,7},{7,3},{8,12},{12,8},{9,1... | collective-permute-start | bytes 3145736 | tf_op jit(solution)/shard_map/ppermute | solution.py:199
  83.1 1.4 add_convert_fusion
  84.5 7.4 %all-to-all-start.1 = ((bf16[16,2,32,512]{3,2,1,0:T(8,128)(2,1)}), bf16[16,2,32,512]{3,2,1,0:T(8,128)(2,1)S(1)}, u32[]{:S(2)}, u32[]{:S(2)}) async-start(bf16[16,2,32,512]{3,2,1,0:T(8,128)(2,1)} %bitcast.30), calls=%async_computation.1 | async-start | bytes 2097152 | tf_op jit(solution)/shard_map/all_to_all | solution.py:207
  92.0 1.1 copy-done.1
  93.2 1.1 copy-done.3
  94.3 3.4 %project.1 = (bf16[384,256]{1,0:T(8,128)(2,1)S(1)}, bf16[384,256]{1,0:T(8,128)(2,1)}) custom-call(s32[6]{0:T(128)S(1)} %stack.63.where, bf16[192,2048]{1,0:T(8,128)(2,1)S(1)} %bitcast.26, bf16[192,2048]{1,0:T(8,128)(2,1)S(1)} %copy-done.3, bf16[4,64,2048]{2,1,0:T(8,128)(2,1)S(1)} %pad_maximum_fusion.w_here, bf16[4,64,2048]{2,1,0:T(8,128)(2,1)} %collective-permute-done.6.w_there), custom_call_target="tpu_custom_call" | custom-call | flops 1000 | bytes 1000 | tf_op jit(solution)/shard_map/project/pallas_call | solution.py:237
  98.4 2.0 %collective-permute-start.7 = (bf16[384,256]{1,0:T(8,128)(2,1)}, bf16[384,256]{1,0:T(8,128)(2,1)S(1)}, u32[]{:S(2)}, u32[]{:S(2)}) collective-permute-start(bf16[384,256]{1,0:T(8,128)(2,1)} %get-tuple-element.26), channel_id=1, source_target_pairs={{0,256},{128,384},{256,0},{384,128},{1,257},{129,385},{257,1},{385... | collective-permute-start | bytes 589832 | tf_op jit(solution)/shard_map/ppermute | solution.py:199
  100.4 7.5 %all-to-all-done.1.parts = bf16[16,2,32,512]{3,2,1,0:T(8,128)(2,1)S(1)} async-done(((bf16[16,2,32,512]{3,2,1,0:T(8,128)(2,1)}), bf16[16,2,32,512]{3,2,1,0:T(8,128)(2,1)S(1)}, u32[]{:S(2)}, u32[]{:S(2)}) %all-to-all-start.1) | async-done | bytes 1048608 | tf_op jit(solution)/shard_map/all_to_all | solution.py:207
  108.7 6.4 %collective-permute-start.11 = (bf16[32,512]{1,0:T(8,128)(2,1)S(1)}, bf16[32,512]{1,0:T(8,128)(2,1)S(1)}, u32[]{:S(2)}, u32[]{:S(2)}) collective-permute-start(bf16[32,512]{1,0:T(8,128)(2,1)S(1)} %get-tuple-element.34), channel_id=1, source_target_pairs={{0,32},{32,288},{64,160},{96,416},{128,96},{160,352},{192,224},{22... | collective-permute-start | bytes 98312 | tf_op jit(solution)/shard_map/ppermute | solution.py:264
  115.9 0.9 copy-done.10
  116.8 0.9 copy-done.12
  117.7 0.9 copy-done.14
  118.6 5.7 %backward.1 = bf16[4,192,768]{2,1,0:T(8,128)(2,1)} custom-call(s32[1]{0:T(128)} %bitcast.where, bf16[4,200,768]{2,1,0:T(8,128)(2,1)S(1)} %all-to-all-done.x_all, bf16[384,256]{1,0:T(8,128)(2,1)S(1)} %copy-done.12, bf16[384,256]{1,0:T(8,128)(2,1)S(1)} %copy-done.14, bf16[384,256]{1,0:T(8,128)(2,1)S(1)} %get-tuple-element.27.o_near.o_here, ...), custom_call_target="tpu_custom_call" | custom-call | flops 1000 | bytes 1000 | tf_op jit(solution)/shard_map/backward/pallas_call | solution.py:251
  124.4 8.2 %all-to-all-start.2 = ((bf16[4,192,768]{2,1,0:T(8,128)(2,1)}), bf16[4,192,768]{2,1,0:T(8,128)(2,1)S(1)}, u32[]{:S(2)}, u32[]{:S(2)}) async-start(bf16[4,192,768]{2,1,0:T(8,128)(2,1)} %backward.1), calls=%async_computation.2 | async-start | bytes 2359296 | tf_op jit(solution)/shard_map/all_to_all | solution.py:207
  132.6 5.7 %collective-permute-start.14 = (bf16[32,512]{1,0:T(8,128)(2,1)S(1)}, bf16[32,512]{1,0:T(8,128)(2,1)S(1)}, u32[]{:S(2)}, u32[]{:S(2)}) collective-permute-start(bf16[32,512]{1,0:T(8,128)(2,1)S(1)} %add_convert_fusion.1.p0), channel_id=1, source_target_pairs={{0,384},{128,256},{256,128},{384,0},{1,385},{129,257},{257,129},{3... | collective-permute-start | bytes 98312 | tf_op jit(solution)/shard_map/ppermute | solution.py:199
  138.3 1.9 %collective-permute-start.13 = (bf16[32,512]{1,0:T(8,128)(2,1)S(1)}, bf16[32,512]{1,0:T(8,128)(2,1)S(1)}, u32[]{:S(2)}, u32[]{:S(2)}) collective-permute-start(bf16[32,512]{1,0:T(8,128)(2,1)S(1)} %add_convert_fusion.1.p0), channel_id=1, source_target_pairs={{0,256},{128,384},{256,0},{384,128},{1,257},{129,385},{257,1},{385... | collective-permute-start | bytes 98312 | tf_op jit(solution)/shard_map/ppermute | solution.py:199
  140.2 2.5 %collective-permute-start.12 = (bf16[32,512]{1,0:T(8,128)(2,1)S(1)}, bf16[32,512]{1,0:T(8,128)(2,1)S(1)}, u32[]{:S(2)}, u32[]{:S(2)}) collective-permute-start(bf16[32,512]{1,0:T(8,128)(2,1)S(1)} %add_convert_fusion.1.p0), channel_id=1, source_target_pairs={{0,128},{128,0},{256,384},{384,256},{1,129},{129,1},{257,385},{385... | collective-permute-start | bytes 98312 | tf_op jit(solution)/shard_map/ppermute | solution.py:199
  142.7 11.9 %collective-permute-done.14.p3 = bf16[32,512]{1,0:T(8,128)(2,1)S(1)} collective-permute-done((bf16[32,512]{1,0:T(8,128)(2,1)S(1)}, bf16[32,512]{1,0:T(8,128)(2,1)S(1)}, u32[]{:S(2)}, u32[]{:S(2)}) %collective-permute-start.14) | collective-permute-done | bytes 32800 | tf_op jit(solution)/shard_map/ppermute | solution.py:199
  154.6 6.6 %collective-permute-done.13.p2 = bf16[32,512]{1,0:T(8,128)(2,1)S(1)} collective-permute-done((bf16[32,512]{1,0:T(8,128)(2,1)S(1)}, bf16[32,512]{1,0:T(8,128)(2,1)S(1)}, u32[]{:S(2)}, u32[]{:S(2)}) %collective-permute-start.13) | collective-permute-done | bytes 32800 | tf_op jit(solution)/shard_map/ppermute | solution.py:199
  161.3 3.5 %collective-permute-start.17 = (bf16[32,512]{1,0:T(8,128)(2,1)S(1)}, bf16[32,512]{1,0:T(8,128)(2,1)S(1)}, u32[]{:S(2)}, u32[]{:S(2)}) collective-permute-start(bf16[32,512]{1,0:T(8,128)(2,1)S(1)} %quarter.1.p0), channel_id=1, source_target_pairs={{0,3},{1,2},{2,1},{3,0},{4,7},{5,6},{6,5},{7,4},{8,11},{9,10},{10,... | collective-permute-start | bytes 98312 | tf_op jit(solution)/shard_map/ppermute | solution.py:199
  164.8 3.8 %collective-permute-start.16 = (bf16[32,512]{1,0:T(8,128)(2,1)S(1)}, bf16[32,512]{1,0:T(8,128)(2,1)S(1)}, u32[]{:S(2)}, u32[]{:S(2)}) collective-permute-start(bf16[32,512]{1,0:T(8,128)(2,1)S(1)} %quarter.1.p0), channel_id=1, source_target_pairs={{0,2},{1,3},{2,0},{3,1},{4,6},{5,7},{6,4},{7,5},{8,10},{9,11},{10,... | collective-permute-start | bytes 98312 | tf_op jit(solution)/shard_map/ppermute | solution.py:199
  168.6 2.5 %collective-permute-start.15 = (bf16[32,512]{1,0:T(8,128)(2,1)S(1)}, bf16[32,512]{1,0:T(8,128)(2,1)S(1)}, u32[]{:S(2)}, u32[]{:S(2)}) collective-permute-start(bf16[32,512]{1,0:T(8,128)(2,1)S(1)} %quarter.1.p0), channel_id=1, source_target_pairs={{0,1},{1,0},{2,3},{3,2},{4,5},{5,4},{6,7},{7,6},{8,9},{9,8},{10,11... | collective-permute-start | bytes 98312 | tf_op jit(solution)/shard_map/ppermute | solution.py:199
  171.2 1.0 collective-permute-done.16.p2
  172.2 2.3 %collective-permute-done.15.p1 = bf16[32,512]{1,0:T(8,128)(2,1)S(1)} collective-permute-done((bf16[32,512]{1,0:T(8,128)(2,1)S(1)}, bf16[32,512]{1,0:T(8,128)(2,1)S(1)}, u32[]{:S(2)}, u32[]{:S(2)}) %collective-permute-start.15) | collective-permute-done | bytes 32800 | tf_op jit(solution)/shard_map/ppermute | solution.py:199
  174.4 1.2 finish.1
  175.7 1.2 unpack.1
  (46 shorter events, 3.7 us)
Async XLA Ops:
  0.6 1.0 copy-start.6
  1.6 1.0 copy-start.7
  2.6 1.0 copy-start.8
  3.6 0.7 copy-start.15
  6.0 6.0 %copy-start.17 = (bf16[32,2048]{1,0:T(8,128)(2,1)S(1)}, bf16[32,2048]{1,0:T(8,128)(2,1)}, u32[]{:S(2)}) copy-start(bf16[32,2048]{1,0:T(8,128)(2,1)} %param.9) | copy-start | bytes 393220
  6.0 31.5 %copy-start = (bf16[1,192,2048]{2,1,0:T(8,128)(2,1)S(1)}, bf16[1,192,2048]{2,1,0:T(8,128)(2,1)}, u32[]{:S(2)}) copy-start(bf16[1,192,2048]{2,1,0:T(8,128)(2,1)} %param.10) | copy-start | bytes 2359300
  6.0 53.9 %all-to-all-start = ((bf16[4,200,768]{2,1,0:T(8,128)(2,1)}), bf16[4,200,768]{2,1,0:T(8,128)(2,1)S(1)}, u32[]{:S(2)}, u32[]{:S(2)}) async-start(bf16[4,200,768]{2,1,0:T(8,128)(2,1)} %pack.1), calls=%async_computation | async-start | bytes 2457600 | tf_op jit(solution)/shard_map/all_to_all | solution.py:207
  12.0 22.1 %collective-permute-start = (bf16[32,2048]{1,0:T(8,128)(2,1)S(1)}, bf16[32,2048]{1,0:T(8,128)(2,1)S(1)}, u32[]{:S(2)}, u32[]{:S(2)}) collective-permute-start(bf16[32,2048]{1,0:T(8,128)(2,1)S(1)} %copy-done.17), channel_id=1, source_target_pairs={{384,64},{0,320},{416,96},{32,352},{448,128},{64,384},{480,160},{9... | collective-permute-start | bytes 393224 | tf_op jit(solution)/shard_map/ppermute | solution.py:219
  25.9 11.6 %collective-permute-start.1 = (bf16[32,2048]{1,0:T(8,128)(2,1)S(1)}, bf16[32,2048]{1,0:T(8,128)(2,1)S(1)}, u32[]{:S(2)}, u32[]{:S(2)}) collective-permute-start(bf16[32,2048]{1,0:T(8,128)(2,1)S(1)} %copy-done.17), channel_id=1, source_target_pairs={{256,32},{384,288},{0,96},{128,352},{32,0},{160,256},{288,64},{416... | collective-permute-start | bytes 393224 | tf_op jit(solution)/shard_map/ppermute | solution.py:222
  37.5 38.7 %collective-permute-start.2 = (bf16[192,2048]{1,0:T(8,128)(2,1)S(1)}, bf16[192,2048]{1,0:T(8,128)(2,1)S(1)}, u32[]{:S(2)}, u32[]{:S(2)}) collective-permute-start(bf16[192,2048]{1,0:T(8,128)(2,1)S(1)} %bitcast.24), channel_id=1, source_target_pairs={{0,128},{128,0},{256,384},{384,256},{1,129},{129,1},{257,385},{385... | collective-permute-start | bytes 2359304 | tf_op jit(solution)/shard_map/ppermute | solution.py:199
  50.0 16.7 %collective-permute-start.5 = (bf16[64,2048]{1,0:T(8,128)(2,1)}, bf16[64,2048]{1,0:T(8,128)(2,1)}, u32[]{:S(2)}, u32[]{:S(2)}) collective-permute-start(bf16[64,2048]{1,0:T(8,128)(2,1)} %get-tuple-element.41), channel_id=1, source_target_pairs={{0,24},{8,16},{16,8},{24,0},{1,25},{9,17},{17,9},{25,1},{2,26},{10... | collective-permute-start | bytes 786440 | tf_op jit(solution)/shard_map/ppermute | solution.py:199
  54.9 13.0 %collective-permute-start.4 = (bf16[64,2048]{1,0:T(8,128)(2,1)}, bf16[64,2048]{1,0:T(8,128)(2,1)}, u32[]{:S(2)}, u32[]{:S(2)}) collective-permute-start(bf16[64,2048]{1,0:T(8,128)(2,1)} %get-tuple-element.41), channel_id=1, source_target_pairs={{0,16},{8,24},{16,0},{24,8},{1,17},{9,25},{17,1},{25,9},{2,18},{10... | collective-permute-start | bytes 786440 | tf_op jit(solution)/shard_map/ppermute | solution.py:199
  57.5 11.1 %collective-permute-start.3 = (bf16[64,2048]{1,0:T(8,128)(2,1)}, bf16[64,2048]{1,0:T(8,128)(2,1)}, u32[]{:S(2)}, u32[]{:S(2)}) collective-permute-start(bf16[64,2048]{1,0:T(8,128)(2,1)} %get-tuple-element.41), channel_id=1, source_target_pairs={{0,8},{8,0},{16,24},{24,16},{1,9},{9,1},{17,25},{25,17},{2,10},{10... | collective-permute-start | bytes 786440 | tf_op jit(solution)/shard_map/ppermute | solution.py:199
  63.8 0.9 copy-start.4
  64.7 14.7 %copy-start.9 = (bf16[384,256]{1,0:T(8,128)(2,1)}, bf16[384,256]{1,0:T(8,128)(2,1)S(1)}, u32[]{:S(2)}) copy-start(bf16[384,256]{1,0:T(8,128)(2,1)S(1)} %get-tuple-element.28.o_far) | copy-start | bytes 589828
  64.7 11.4 %collective-permute-start.8 = (bf16[384,256]{1,0:T(8,128)(2,1)S(1)}, bf16[384,256]{1,0:T(8,128)(2,1)S(1)}, u32[]{:S(2)}, u32[]{:S(2)}) collective-permute-start(bf16[384,256]{1,0:T(8,128)(2,1)S(1)} %get-tuple-element.28.o_far), channel_id=1, source_target_pairs={{0,256},{128,384},{256,0},{384,128},{1,257},{129,385},{257,1},{385... | collective-permute-start | bytes 589832 | tf_op jit(solution)/shard_map/ppermute | solution.py:199
  66.6 12.8 %copy-start.16 = (bf16[1,64,2048]{2,1,0:T(8,128)(2,1)S(1)}, bf16[1,64,2048]{2,1,0:T(8,128)(2,1)}, u32[]{:S(2)}) copy-start(bf16[1,64,2048]{2,1,0:T(8,128)(2,1)} %get-tuple-element.40) | copy-start | bytes 786436
  76.2 3.3 %copy-start.2 = (bf16[192,2048]{1,0:T(8,128)(2,1)}, bf16[192,2048]{1,0:T(8,128)(2,1)S(1)}, u32[]{:S(2)}) copy-start(bf16[192,2048]{1,0:T(8,128)(2,1)S(1)} %collective-permute-done.2.mate_ref) | copy-start | bytes 2359300
  77.5 5.6 %collective-permute-start.9 = (bf16[4,4,2,32,512]{4,3,2,1,0:T(8,128)(2,1)S(1)}, bf16[4,4,2,32,512]{4,3,2,1,0:T(8,128)(2,1)S(1)}, u32[]{:S(2)}, u32[]{:S(2)}) collective-permute-start(bf16[4,4,2,32,512]{4,3,2,1,0:T(8,128)(2,1)S(1)} %get-tuple-element.32), channel_id=1, source_target_pairs={{0,4},{4,0},{1,5},{5,1},{2,6},{6,2},{3,7},{7,3},{8,12},{12,8},{9,1... | collective-permute-start | bytes 3145736 | tf_op jit(solution)/shard_map/ppermute | solution.py:199
  80.7 11.3 %collective-permute-start.6 = (bf16[4,64,2048]{2,1,0:T(8,128)(2,1)S(1)}, bf16[4,64,2048]{2,1,0:T(8,128)(2,1)}, u32[]{:S(2)}, u32[]{:S(2)}) collective-permute-start(bf16[4,64,2048]{2,1,0:T(8,128)(2,1)S(1)} %pad_maximum_fusion.w_here), channel_id=1, source_target_pairs={{0,4},{4,0},{1,5},{5,1},{2,6},{6,2},{3,7},{7,3},{8,12},{12,8},{9,1... | collective-permute-start | bytes 3145736 | tf_op jit(solution)/shard_map/ppermute | solution.py:199
  84.5 23.4 %all-to-all-start.1 = ((bf16[16,2,32,512]{3,2,1,0:T(8,128)(2,1)}), bf16[16,2,32,512]{3,2,1,0:T(8,128)(2,1)S(1)}, u32[]{:S(2)}, u32[]{:S(2)}) async-start(bf16[16,2,32,512]{3,2,1,0:T(8,128)(2,1)} %bitcast.30), calls=%async_computation.1 | async-start | bytes 2097152 | tf_op jit(solution)/shard_map/all_to_all | solution.py:207
  92.0 1.1 copy-start.1
  93.1 1.1 copy-start.3
  97.7 0.7 copy-start.11
  98.3 17.5 %copy-start.5 = (f32[768,256]{1,0:T(8,128)S(1)}, f32[768,256]{1,0:T(8,128)}, u32[]{:S(2)}) copy-start(f32[768,256]{1,0:T(8,128)} %copy-done.4) | copy-start | bytes 2359300
  98.4 16.8 %collective-permute-start.7 = (bf16[384,256]{1,0:T(8,128)(2,1)}, bf16[384,256]{1,0:T(8,128)(2,1)S(1)}, u32[]{:S(2)}, u32[]{:S(2)}) collective-permute-start(bf16[384,256]{1,0:T(8,128)(2,1)} %get-tuple-element.26), channel_id=1, source_target_pairs={{0,256},{128,384},{256,0},{384,128},{1,257},{129,385},{257,1},{385... | collective-permute-start | bytes 589832 | tf_op jit(solution)/shard_map/ppermute | solution.py:199
  108.0 16.3 %collective-permute-start.10 = (bf16[32,512]{1,0:T(8,128)(2,1)S(1)}, bf16[32,512]{1,0:T(8,128)(2,1)S(1)}, u32[]{:S(2)}, u32[]{:S(2)}) collective-permute-start(bf16[32,512]{1,0:T(8,128)(2,1)S(1)} %get-tuple-element.33), channel_id=1, source_target_pairs={{0,0},{32,256},{64,128},{96,384},{128,64},{160,320},{192,192},{224... | collective-permute-start | bytes 98312 | tf_op jit(solution)/shard_map/ppermute | solution.py:264
  108.7 15.6 %collective-permute-start.11 = (bf16[32,512]{1,0:T(8,128)(2,1)S(1)}, bf16[32,512]{1,0:T(8,128)(2,1)S(1)}, u32[]{:S(2)}, u32[]{:S(2)}) collective-permute-start(bf16[32,512]{1,0:T(8,128)(2,1)S(1)} %get-tuple-element.34), channel_id=1, source_target_pairs={{0,32},{32,288},{64,160},{96,416},{128,96},{160,352},{192,224},{22... | collective-permute-start | bytes 98312 | tf_op jit(solution)/shard_map/ppermute | solution.py:264
  115.2 0.7 copy-start.13
  115.9 0.9 copy-start.10
  116.8 0.9 copy-start.12
  117.7 0.9 copy-start.14
  124.4 51.3 %all-to-all-start.2 = ((bf16[4,192,768]{2,1,0:T(8,128)(2,1)}), bf16[4,192,768]{2,1,0:T(8,128)(2,1)S(1)}, u32[]{:S(2)}, u32[]{:S(2)}) async-start(bf16[4,192,768]{2,1,0:T(8,128)(2,1)} %backward.1), calls=%async_computation.2 | async-start | bytes 2359296 | tf_op jit(solution)/shard_map/all_to_all | solution.py:207
  132.6 22.0 %collective-permute-start.14 = (bf16[32,512]{1,0:T(8,128)(2,1)S(1)}, bf16[32,512]{1,0:T(8,128)(2,1)S(1)}, u32[]{:S(2)}, u32[]{:S(2)}) collective-permute-start(bf16[32,512]{1,0:T(8,128)(2,1)S(1)} %add_convert_fusion.1.p0), channel_id=1, source_target_pairs={{0,384},{128,256},{256,128},{384,0},{1,385},{129,257},{257,129},{3... | collective-permute-start | bytes 98312 | tf_op jit(solution)/shard_map/ppermute | solution.py:199
  138.3 22.9 %collective-permute-start.13 = (bf16[32,512]{1,0:T(8,128)(2,1)S(1)}, bf16[32,512]{1,0:T(8,128)(2,1)S(1)}, u32[]{:S(2)}, u32[]{:S(2)}) collective-permute-start(bf16[32,512]{1,0:T(8,128)(2,1)S(1)} %add_convert_fusion.1.p0), channel_id=1, source_target_pairs={{0,256},{128,384},{256,0},{384,128},{1,257},{129,385},{257,1},{385... | collective-permute-start | bytes 98312 | tf_op jit(solution)/shard_map/ppermute | solution.py:199
  140.2 21.0 %collective-permute-start.12 = (bf16[32,512]{1,0:T(8,128)(2,1)S(1)}, bf16[32,512]{1,0:T(8,128)(2,1)S(1)}, u32[]{:S(2)}, u32[]{:S(2)}) collective-permute-start(bf16[32,512]{1,0:T(8,128)(2,1)S(1)} %add_convert_fusion.1.p0), channel_id=1, source_target_pairs={{0,128},{128,0},{256,384},{384,256},{1,129},{129,1},{257,385},{385... | collective-permute-start | bytes 98312 | tf_op jit(solution)/shard_map/ppermute | solution.py:199
  161.3 9.9 %collective-permute-start.17 = (bf16[32,512]{1,0:T(8,128)(2,1)S(1)}, bf16[32,512]{1,0:T(8,128)(2,1)S(1)}, u32[]{:S(2)}, u32[]{:S(2)}) collective-permute-start(bf16[32,512]{1,0:T(8,128)(2,1)S(1)} %quarter.1.p0), channel_id=1, source_target_pairs={{0,3},{1,2},{2,1},{3,0},{4,7},{5,6},{6,5},{7,4},{8,11},{9,10},{10,... | collective-permute-start | bytes 98312 | tf_op jit(solution)/shard_map/ppermute | solution.py:199
  164.8 7.4 %collective-permute-start.16 = (bf16[32,512]{1,0:T(8,128)(2,1)S(1)}, bf16[32,512]{1,0:T(8,128)(2,1)S(1)}, u32[]{:S(2)}, u32[]{:S(2)}) collective-permute-start(bf16[32,512]{1,0:T(8,128)(2,1)S(1)} %quarter.1.p0), channel_id=1, source_target_pairs={{0,2},{1,3},{2,0},{3,1},{4,6},{5,7},{6,4},{7,5},{8,10},{9,11},{10,... | collective-permute-start | bytes 98312 | tf_op jit(solution)/shard_map/ppermute | solution.py:199
  168.6 5.8 %collective-permute-start.15 = (bf16[32,512]{1,0:T(8,128)(2,1)S(1)}, bf16[32,512]{1,0:T(8,128)(2,1)S(1)}, u32[]{:S(2)}, u32[]{:S(2)}) collective-permute-start(bf16[32,512]{1,0:T(8,128)(2,1)S(1)} %quarter.1.p0), channel_id=1, source_target_pairs={{0,1},{1,0},{2,3},{3,2},{4,5},{5,4},{6,7},{7,6},{8,9},{9,8},{10,11... | collective-permute-start | bytes 98312 | tf_op jit(solution)/shard_map/ppermute | solution.py:199

commit v5 on v2

--- a/solution.py
+++ b/solution.py
@@ -45,15 +45,22 @@
     return 2 * (b % 2) + b // 2
 
 
-def pack_kernel(ids, q_ref, k_ref, v_ref, out):
+def pack_kernel(ids, q_ref, k_ref, v_ref, out, block, sems):
+    copies = []
+    for j in range(4):
+        cols = pl.ds(256 * group_of(j), 256)
+        for n, ref in enumerate((q_ref, k_ref, v_ref)):
+            to = out.at[j, pl.ds(0, 192), pl.ds(256 * n, 256)]
+            copies.append(pltpu.make_async_copy(ref.at[:, cols], to, sems.at[4 * j + n]))
+            copies[-1].start()
     lane = lax.broadcasted_iota(jnp.int32, (8, 768), 1)
-    block = jnp.where(lane < 384, ids[0], ids[1]).astype(F32).astype(BF16)
+    block[...] = jnp.where(lane < 384, ids[0], ids[1]).astype(F32).astype(BF16)
     for j in range(4):
-        cols = slice(256 * group_of(j), 256 * group_of(j) + 256)
-        out[j, 0:192, 0:256] = q_ref[:, cols]
-        out[j, 0:192, 256:512] = k_ref[:, cols]
-        out[j, 0:192, 512:768] = v_ref[:, cols]
-        out[j, 192:200, :] = block
+        to = out.at[j, pl.ds(192, 8), :]
+        copies.append(pltpu.make_async_copy(block, to, sems.at[4 * j + 3]))
+        copies[-1].start()
+    for copy in copies:
+        copy.wait()
 
 
 def unpack_kernel(home, dq, dk, dv):
@@ -76,13 +83,13 @@
         out[:, 512 * x : 512 * x + 512] = parts[x]
 
 
-def project_kernel(where, own_ref, mate_ref, w_here, w_there, keep, send, w_all):
+def project_kernel(where, own_ref, mate_ref, w0, w1, w2, w3, keep, send, w_all):
     first, core = where[0], where[1]
-    for k in range(4):
-        for c, ref in ((0, w_here), (1, w_there)):
+    for k, ref in enumerate((w0, w1, w2, w3)):
+        for c in range(2):
             row = pl.multiple_of((2 * where[2 + k] + lax.rem(core + c, 2)) * 32, 32)
-            w_all[first, pl.ds(row, 32), :] = ref[k, 0:32, :]
-            w_all[1 - first, pl.ds(row, 32), :] = ref[k, 32:64, :]
+            w_all[first, pl.ds(row, 32), :] = ref[c, 0:32, :]
+            w_all[1 - first, pl.ds(row, 32), :] = ref[c, 32:64, :]
     for slot, out in ((1, send), (0, keep)):
         w = w_all[slot]
         out[0:192] = dot(own_ref[...], w, NT).astype(BF16)
@@ -216,7 +223,6 @@
     z = ("seq", "zh")
 
     grads = out_grad[0]
-    mate_grads = swap(grads, "seq", 1, 4)
 
     first = lax.ppermute(
         out_weight, z, nearest([d for d in places if d[0] // 2 != d[1] % 2], lambda i, j: i ^ 2)
@@ -224,34 +230,38 @@
     second = lax.ppermute(
         out_weight, z, nearest(places, lambda i, j: i ^ 1 if i // 2 == j % 2 else i ^ 3)
     )
-    packed = call(pack_kernel, arr((4, 200, 768)), 1, 3, "pack")(
-        block_ids, query[0], key[0], value[0]
-    )
-    packed, mate_grads, first, second = lax.optimization_barrier(
-        (packed, mate_grads, first, second)
-    )
+    anywhere = pl.BlockSpec(memory_space=pl.ANY)
+    packed = pl.pallas_call(
+        pack_kernel,
+        out_shape=arr((4, 200, 768)),
+        in_specs=[SMEM] + [anywhere] * 3,
+        out_specs=anywhere,
+        scratch_shapes=[pltpu.VMEM((8, 768), BF16), pltpu.SemaphoreType.DMA((16,))],
+        compiler_params=pltpu.CompilerParams(vmem_limit_bytes=60 * 1024 * 1024),
+        cost_estimate=pl.CostEstimate(flops=1000, bytes_accessed=1000, transcendentals=0),
+        name="pack",
+    )(block_ids, query[0], key[0], value[0])
     rows = exchange(packed, "seq")
+    grads, first, second = lax.optimization_barrier((grads, first, second))
+    mate_grads = swap(grads, "seq", 1, 4)
     first = jnp.where((a >> 1) == half, out_weight, first)
     piece = jnp.concatenate([first, second], axis=0)
-    pieces = [piece] + [swap(piece, "y", k, 4) for k in (1, 2, 3)]
-    w_here = jnp.stack(pieces)
-    rows, w_here = lax.optimization_barrier((rows, w_here))
-    w_there = swap(w_here, "c", 1, 2)
+    both_cores = jnp.stack([piece, swap(piece, "c", 1, 2)])
+    pieces = [both_cores] + [swap(both_cores, "y", k, 4) for k in (1, 2, 3)]
 
     g_near, g_send = call(
-        project_kernel, [arr((384, 256))] * 2, 1, 4, "project", [pltpu.VMEM((2, 256, 2048), BF16)]
-    )(scalars((a & 1) ^ pair, core, *(y ^ k for k in range(4))), grads, mate_grads, w_here, w_there)
+        project_kernel, [arr((384, 256))] * 2, 1, 6, "project", [pltpu.VMEM((2, 256, 2048), BF16)]
+    )(scalars((a & 1) ^ pair, core, *(y ^ k for k in range(4))), grads, mate_grads, *pieces)
     g_far = swap(g_send, "seq", 2, 4)
     kv = [pltpu.VMEM((768, 256), BF16)] * 2
     o_near, o_far, lse = call(
         forward_kernel, [arr((384, 256))] * 2 + [arr((768, 256), F32)], 1, 1, "forward", kv
     )(scalars(b), rows)
     o_there = swap(o_far, "seq", 2, 4)
-    o_there, _ = lax.optimization_barrier((o_there, g_send))
+    o_there, _ = lax.optimization_barrier((o_there, pieces))
     keep, send = call(weight_kernel, [arr((4, 4, 2, 32, 512))] * 2, 1, 4, "weight")(
         scalars(core), o_near, o_there, grads, mate_grads
     )
-    send, g_far = lax.optimization_barrier((send, g_far))
     taken = swap(send, "c", 1, 2)
     back = call(
         backward_kernel,
@@ -263,6 +273,7 @@
     )(scalars(b), rows, g_near, g_far, o_near, o_far, lse)
     home = exchange(back, "seq")
     both = (keep.astype(F32) + taken.astype(F32)).astype(BF16).reshape(16, 2, 32, 512)
+    both, g_send = lax.optimization_barrier((both, g_send))
     parts = exchange(both, ("y", "dp"))
     own, other = call(sum_kernel, [arr((32, 512))] * 2, 0, 1, "sum")(parts)
     turn = [(i * 4 + j, group_of(j) * 4 + group_of(i)) for i in range(4) for j in range(4)]

time: 186 us -> 211 us (1.13)
  Pallas kernels: 19.1 us -> 57.9 us
  waiting for transfers between devices: 68.7 us -> 55.1 us
  local copies, waits for them, and re-layouts: 9.16 us -> 2.01 us
  blocking collectives: 17 us -> 20 us
  starting transfers between devices: 68.9 us -> 71.6 us
    pallas_call x2, Pallas kernels: 4.55 us -> 40.8 us  [the longest x1 37.6 us: shards(): pl.pallas_call(pack_kernel, out_shape=arr((4, 200, 768)), in_specs=[SMEM]...]
    all_to_all x4, waiting for transfers between devices: 28.4 us -> 4.83 us  [exchange(): return lax.all_to_all(value, axes, 0, 0, tiled=True)]
    ppermute x1, waiting for transfers between devices: 0.01 us -> 10.6 us  [shards(): lax.ppermute(own, z, turn).astype(F32)]
    ppermute x1, waiting for transfers between devices: 16 us -> 6.77 us  [shards(): lax.ppermute(other, z, turn2).astype(F32)]
    unnamed x28 -> x18, local copies, waits for them, and re-layouts: 9.06 us -> 1.92 us
    ppermute x1, starting transfers between devices: 5.02 us -> 11.5 us  [shards(): lax.ppermute(own, z, turn).astype(F32)]
    ppermute x1, waiting for transfers between devices: 5.6 us -> 10.6 us  [shards(): lax.ppermute(out_weight, z, nearest(places, lambda i, j: i ^ 1 if i // 2...]
    ppermute x8, waiting for transfers between devices: 18.8 us -> 22.3 us  [swap(): return lax.ppermute(value, axis, [(i, i ^ mask) for i in range(n)])]
  transfers between devices with their start and end apart: 16 -> 16, of which waited for: 12 -> 7; matrix products, arithmetic and copies ran while one was open for 0% -> 0% of each run, Pallas kernels for 10% -> 7%
where the time goes in v5:
time: 211 us; the launch traced here: 210 us
  starting transfers between devices  71.6 us (34%)
  Pallas kernels  57.9 us (27%)
  waiting for transfers between devices  55.1 us (26%)
  blocking collectives  20 us (9%)
  other arithmetic  2.88 us (1%)
    pallas_call x1, Pallas kernels, shards(): pl.pallas_call(pack_kernel, out_shape=arr((4, 200, 768)), in_specs=[SMEM]...  37.6 us
    ppermute x8, starting transfers between devices, swap(): return lax.ppermute(value, axis, [(i, i ^ mask) for i in range(n)])  23.4 us
    ppermute x8, waiting for transfers between devices, swap(): return lax.ppermute(value, axis, [(i, i ^ mask) for i in range(n)])  22.3 us
    all_to_all x4, starting transfers between devices, exchange(): return lax.all_to_all(value, axes, 0, 0, tiled=True)  20.3 us
    all_to_all x1, blocking collectives, exchange(): return lax.all_to_all(value, axes, 0, 0, tiled=True)  20 us
    ppermute x1, starting transfers between devices, shards(): lax.ppermute(own, z, turn).astype(F32)  11.5 us
    ppermute x1, waiting for transfers between devices, shards(): lax.ppermute(out_weight, z, nearest(places, lambda i, j: i ^ 1 if i // 2...  10.6 us
    ppermute x1, waiting for transfers between devices, shards(): lax.ppermute(own, z, turn).astype(F32)  10.6 us
  transfers between devices with their start and end apart: 16, of which 7 were waited for; matrix products, arithmetic and copies ran while one was open for 0% of the time, Pallas kernels for 7%

profile of v5, /device:TPU:128, one launch (start us, length us, event | category | flops | bytes accessed | tf_op | source)
XLA Modules:
  0.0 210.4 jit_solution(15244075737143454521)
XLA Ops:
  0.6 37.6 %pack.1 = bf16[4,200,768]{2,1,0:T(8,128)(2,1)} custom-call(s32[2]{0:T(128)} %ids.1, bf16[192,1024]{1,0:T(8,128)(2,1)} %bitcast.22, bf16[192,1024]{1,0:T(8,128)(2,1)} %bitcast.23, bf16[192,1024]{1,0:T(8,128)(2,1)} %bitcast.24), custom_call_target="tpu_custom_call" | custom-call | flops 1000 | bytes 1000 | tf_op jit(solution)/shard_map/pack/pallas_call | solution.py:234
  38.3 0.0 copy-start.8
  38.3 0.0 copy-start
  38.3 6.0 %all-to-all-start = ((bf16[4,200,768]{2,1,0:T(8,128)(2,1)}), bf16[4,200,768]{2,1,0:T(8,128)(2,1)S(1)}, u32[]{:S(2)}, u32[]{:S(2)}) async-start(bf16[4,200,768]{2,1,0:T(8,128)(2,1)} %pack.1), calls=%async_computation | async-start | bytes 2457600 | tf_op jit(solution)/shard_map/all_to_all | solution.py:215
  44.4 9.1 %collective-permute-start.1 = (bf16[32,2048]{1,0:T(8,128)(2,1)S(1)}, bf16[32,2048]{1,0:T(8,128)(2,1)S(1)}, u32[]{:S(2)}, u32[]{:S(2)}) collective-permute-start(bf16[32,2048]{1,0:T(8,128)(2,1)S(1)} %copy-done.8), channel_id=1, source_target_pairs={{384,64},{0,320},{416,96},{32,352},{448,128},{64,384},{480,160},{9... | collective-permute-start | bytes 393224 | tf_op jit(solution)/shard_map/ppermute | solution.py:227
  53.4 5.5 %collective-permute-start.2 = (bf16[32,2048]{1,0:T(8,128)(2,1)S(1)}, bf16[32,2048]{1,0:T(8,128)(2,1)S(1)}, u32[]{:S(2)}, u32[]{:S(2)}) collective-permute-start(bf16[32,2048]{1,0:T(8,128)(2,1)S(1)} %copy-done.8), channel_id=1, source_target_pairs={{256,32},{384,288},{0,96},{128,352},{32,0},{160,256},{288,64},{416... | collective-permute-start | bytes 393224 | tf_op jit(solution)/shard_map/ppermute | solution.py:230
  58.9 0.0 collective-permute-done.1
  58.9 10.6 %collective-permute-done.2 = bf16[32,2048]{1,0:T(8,128)(2,1)S(1)} collective-permute-done((bf16[32,2048]{1,0:T(8,128)(2,1)S(1)}, bf16[32,2048]{1,0:T(8,128)(2,1)S(1)}, u32[]{:S(2)}, u32[]{:S(2)}) %collective-permute-start.2) | collective-permute-done | bytes 131104 | tf_op jit(solution)/shard_map/ppermute | solution.py:230
  69.6 1.9 collective-permute-start.3
  71.5 1.9 collective-permute-start.7
  73.5 0.0 collective-permute-done.3
  73.5 0.1 pad_maximum_fusion.w0
  73.5 4.1 %collective-permute-start.6 = (bf16[2,64,2048]{2,1,0:T(8,128)(2,1)S(1)}, bf16[2,64,2048]{2,1,0:T(8,128)(2,1)}, u32[]{:S(2)}, u32[]{:S(2)}) collective-permute-start(bf16[2,64,2048]{2,1,0:T(8,128)(2,1)S(1)} %pad_maximum_fusion.w0), channel_id=1, source_target_pairs={{0,24},{8,16},{16,8},{24,0},{1,25},{9,17},{17,9},{25,1},{2,26},{10... | collective-permute-start | bytes 1572872 | tf_op jit(solution)/shard_map/ppermute | solution.py:207
  77.7 2.5 %collective-permute-start.5 = (bf16[2,64,2048]{2,1,0:T(8,128)(2,1)S(1)}, bf16[2,64,2048]{2,1,0:T(8,128)(2,1)}, u32[]{:S(2)}, u32[]{:S(2)}) collective-permute-start(bf16[2,64,2048]{2,1,0:T(8,128)(2,1)S(1)} %pad_maximum_fusion.w0), channel_id=1, source_target_pairs={{0,16},{8,24},{16,0},{24,8},{1,17},{9,25},{17,1},{25,9},{2,18},{10... | collective-permute-start | bytes 1572872 | tf_op jit(solution)/shard_map/ppermute | solution.py:207
  80.2 3.1 %collective-permute-start.4 = (bf16[2,64,2048]{2,1,0:T(8,128)(2,1)S(1)}, bf16[2,64,2048]{2,1,0:T(8,128)(2,1)}, u32[]{:S(2)}, u32[]{:S(2)}) collective-permute-start(bf16[2,64,2048]{2,1,0:T(8,128)(2,1)S(1)} %pad_maximum_fusion.w0), channel_id=1, source_target_pairs={{0,8},{8,0},{16,24},{24,16},{1,9},{9,1},{17,25},{25,17},{2,10},{10... | collective-permute-start | bytes 1572872 | tf_op jit(solution)/shard_map/ppermute | solution.py:207
  83.4 4.7 %forward.1 = (bf16[384,256]{1,0:T(8,128)(2,1)S(1)}, bf16[384,256]{1,0:T(8,128)(2,1)}, f32[768,256]{1,0:T(8,128)S(1)}) custom-call(s32[1]{0:T(128)} %bitcast.1.where, bf16[4,200,768]{2,1,0:T(8,128)(2,1)S(1)} %all-to-all-done.x_all), custom_call_target="tpu_custom_call" | custom-call | flops 1000 | bytes 1000 | tf_op jit(solution)/shard_map/forward/pallas_call | solution.py:257
  88.1 0.9 copy-done.3
  89.0 3.6 %collective-permute-start = (bf16[384,256]{1,0:T(8,128)(2,1)}, bf16[384,256]{1,0:T(8,128)(2,1)}, u32[]{:S(2)}, u32[]{:S(2)}) collective-permute-start(bf16[384,256]{1,0:T(8,128)(2,1)} %get-tuple-element.24.o_far), channel_id=1, source_target_pairs={{0,256},{128,384},{256,0},{384,128},{1,257},{129,385},{257,1},{385... | collective-permute-start | bytes 589832 | tf_op jit(solution)/shard_map/ppermute | solution.py:207
  92.6 9.7 %collective-permute-done.6.w3 = bf16[2,64,2048]{2,1,0:T(8,128)(2,1)} collective-permute-done((bf16[2,64,2048]{2,1,0:T(8,128)(2,1)S(1)}, bf16[2,64,2048]{2,1,0:T(8,128)(2,1)}, u32[]{:S(2)}, u32[]{:S(2)}) %collective-permute-start.6) | collective-permute-done | bytes 524320 | tf_op jit(solution)/shard_map/ppermute | solution.py:207
  102.3 0.0 collective-permute-done.5.w2
  102.3 2.5 %collective-permute-done.4.w1 = bf16[2,64,2048]{2,1,0:T(8,128)(2,1)} collective-permute-done((bf16[2,64,2048]{2,1,0:T(8,128)(2,1)S(1)}, bf16[2,64,2048]{2,1,0:T(8,128)(2,1)}, u32[]{:S(2)}, u32[]{:S(2)}) %collective-permute-start.4) | collective-permute-done | bytes 524320 | tf_op jit(solution)/shard_map/ppermute | solution.py:207
  104.8 0.0 collective-permute-done.7.mate_ref
  104.8 3.2 %weight.1 = (bf16[4,4,2,32,512]{4,3,2,1,0:T(8,128)(2,1)S(1)}, bf16[4,4,2,32,512]{4,3,2,1,0:T(8,128)(2,1)}) custom-call(s32[1]{0:T(128)} %bitcast.where, bf16[384,256]{1,0:T(8,128)(2,1)S(1)} %get-tuple-element.23.o_here.o_near, bf16[384,256]{1,0:T(8,128)(2,1)} %collective-permute-done.o_there, bf16[192,2048]{1,0:T(8,128)(2,1)S(1)} %bitcast.19, ...), custom_call_target="tpu_custom_call" | custom-call | flops 1000 | bytes 1000 | tf_op jit(solution)/shard_map/weight/pallas_call | solution.py:262
  108.1 1.0 copy-done.1
  109.1 1.9 collective-permute-start.8
  111.0 0.1 stack.45.where
  111.1 3.1 %project.1 = (bf16[384,256]{1,0:T(8,128)(2,1)S(1)}, bf16[384,256]{1,0:T(8,128)(2,1)S(1)}) custom-call(s32[6]{0:T(128)S(1)} %stack.45.where, bf16[192,2048]{1,0:T(8,128)(2,1)S(1)} %bitcast.20, bf16[192,2048]{1,0:T(8,128)(2,1)S(1)} %collective-permute-done.7.mate_ref, bf16[2,64,2048]{2,1,0:T(8,128)(2,1)S(1)} %pad_maximum_fusion.w0, ...), custom_call_target="tpu_custom_call" | custom-call | flops 1000 | bytes 1000 | tf_op jit(solution)/shard_map/project/pallas_call | solution.py:252
  114.2 0.0 copy-start.5
  114.2 0.0 copy-start.7
  114.3 2.8 %add_convert_fusion = bf16[4,4,2,32,512]{4,3,2,1,0:T(8,128)(2,1)} fusion(bf16[4,4,2,32,512]{4,3,2,1,0:T(8,128)(2,1)} %collective-permute-done.8, bf16[4,4,2,32,512]{4,3,2,1,0:T(8,128)(2,1)S(1)} %copy-done.2), kind=kLoop, calls=%fused_computation | loop fusion | flops 2097152 | bytes 3145728 | tf_op jit(solution)/shard_map/convert_element_type | solution.py:275
  117.0 6.3 %all-to-all-start.1 = ((bf16[16,2,32,512]{3,2,1,0:T(8,128)(2,1)}), bf16[16,2,32,512]{3,2,1,0:T(8,128)(2,1)S(1)}, u32[]{:S(2)}, u32[]{:S(2)}) async-start(bf16[16,2,32,512]{3,2,1,0:T(8,128)(2,1)} %bitcast.21), calls=%async_computation.1 | async-start | bytes 2097152 | tf_op jit(solution)/shard_map/all_to_all | solution.py:215
  123.4 4.2 %collective-permute-start.11 = (bf16[384,256]{1,0:T(8,128)(2,1)}, bf16[384,256]{1,0:T(8,128)(2,1)S(1)}, u32[]{:S(2)}, u32[]{:S(2)}) collective-permute-start(bf16[384,256]{1,0:T(8,128)(2,1)} %copy-done.7), channel_id=1, source_target_pairs={{0,256},{128,384},{256,0},{384,128},{1,257},{129,385},{257,1},{385... | collective-permute-start | bytes 589832 | tf_op jit(solution)/shard_map/ppermute | solution.py:207
  127.6 10.0 %collective-permute-done.11.g_far = bf16[384,256]{1,0:T(8,128)(2,1)S(1)} collective-permute-done((bf16[384,256]{1,0:T(8,128)(2,1)}, bf16[384,256]{1,0:T(8,128)(2,1)S(1)}, u32[]{:S(2)}, u32[]{:S(2)}) %collective-permute-start.11) | collective-permute-done | bytes 196640 | tf_op jit(solution)/shard_map/ppermute | solution.py:207
  137.6 6.6 %backward.1 = bf16[4,192,768]{2,1,0:T(8,128)(2,1)} custom-call(s32[1]{0:T(128)} %bitcast.1.where, bf16[4,200,768]{2,1,0:T(8,128)(2,1)S(1)} %all-to-all-done.x_all, bf16[384,256]{1,0:T(8,128)(2,1)S(1)} %copy-done.6, bf16[384,256]{1,0:T(8,128)(2,1)S(1)} %collective-permute-done.11.g_far, bf16[384,256]{1,0:T(8,128)(2,1)S(1)} %get-tuple-element.23.o_here.o_near, ...), custom_call_target="tpu_custom_call" | custom-call | flops 1000 | bytes 1000 | tf_op jit(solution)/shard_map/backward/pallas_call | solution.py:266
  144.2 0.0 all-to-all-done.1.parts
  144.2 3.5 %all-to-all-start.2 = ((bf16[4,192,768]{2,1,0:T(8,128)(2,1)}), bf16[4,192,768]{2,1,0:T(8,128)(2,1)S(1)}, u32[]{:S(2)}, u32[]{:S(2)}) async-start(bf16[4,192,768]{2,1,0:T(8,128)(2,1)} %backward.1), calls=%async_computation.2 | async-start | bytes 2359296 | tf_op jit(solution)/shard_map/all_to_all | solution.py:215
  147.8 0.1 sum.1
  147.9 11.5 %collective-permute-start.9 = (bf16[32,512]{1,0:T(8,128)(2,1)S(1)}, bf16[32,512]{1,0:T(8,128)(2,1)S(1)}, u32[]{:S(2)}, u32[]{:S(2)}) collective-permute-start(bf16[32,512]{1,0:T(8,128)(2,1)S(1)} %get-tuple-element.33), channel_id=1, source_target_pairs={{0,0},{32,256},{64,128},{96,384},{128,64},{160,320},{192,192},{224... | collective-permute-start | bytes 98312 | tf_op jit(solution)/shard_map/ppermute | solution.py:281
  159.4 1.9 collective-permute-start.10
  161.4 10.6 %collective-permute-done.9 = bf16[32,512]{1,0:T(8,128)(2,1)S(1)} collective-permute-done((bf16[32,512]{1,0:T(8,128)(2,1)S(1)}, bf16[32,512]{1,0:T(8,128)(2,1)S(1)}, u32[]{:S(2)}, u32[]{:S(2)}) %collective-permute-start.9) | collective-permute-done | bytes 32800 | tf_op jit(solution)/shard_map/ppermute | solution.py:281
  171.9 6.8 %collective-permute-done.10 = bf16[32,512]{1,0:T(8,128)(2,1)S(1)} collective-permute-done((bf16[32,512]{1,0:T(8,128)(2,1)S(1)}, bf16[32,512]{1,0:T(8,128)(2,1)S(1)}, u32[]{:S(2)}, u32[]{:S(2)}) %collective-permute-start.10) | collective-permute-done | bytes 32800 | tf_op jit(solution)/shard_map/ppermute | solution.py:281
  178.7 0.0 all-to-all-done.2.home
  178.7 20.0 %all_to_all.25.parts = bf16[4,32,512]{2,1,0:T(8,128)(2,1)S(1)} all-to-all(bf16[4,32,512]{2,1,0:T(8,128)(2,1)S(1)} %broadcast_in_dim.18), channel_id=1, replica_groups=mesh['seq'=4,'zh'=4,'y'=4,'c'=2,'dp'=4] {'seq'}, dimensions={0} | all-to-all | bytes 262144 | tf_op jit(solution)/shard_map/all_to_all | solution.py:215
  198.7 0.7 quarter.1
  199.4 4.4 %all-to-all-start.4 = ((bf16[4,32,512]{2,1,0:T(8,128)(2,1)}), bf16[4,32,512]{2,1,0:T(8,128)(2,1)S(1)}, u32[]{:S(2)}, u32[]{:S(2)}) async-start(bf16[4,32,512]{2,1,0:T(8,128)(2,1)} %quarter.1), calls=%async_computation.4 | async-start | bytes 262144 | tf_op jit(solution)/shard_map/all_to_all | solution.py:215
  203.8 1.2 unpack.1
  204.9 4.8 %all-to-all-done.4.parts = bf16[4,32,512]{2,1,0:T(8,128)(2,1)S(1)} async-done(((bf16[4,32,512]{2,1,0:T(8,128)(2,1)}), bf16[4,32,512]{2,1,0:T(8,128)(2,1)S(1)}, u32[]{:S(2)}, u32[]{:S(2)}) %all-to-all-start.4) | async-done | bytes 131104 | tf_op jit(solution)/shard_map/all_to_all | solution.py:215
  209.7 0.7 finish.1
  (19 shorter events, 0.1 us)
Async XLA Ops:
  38.3 6.1 %copy-start.8 = (bf16[32,2048]{1,0:T(8,128)(2,1)S(1)}, bf16[32,2048]{1,0:T(8,128)(2,1)}, u32[]{:S(2)}) copy-start(bf16[32,2048]{1,0:T(8,128)(2,1)} %param.9) | copy-start | bytes 393220
  38.3 33.2 %copy-start = (bf16[1,192,2048]{2,1,0:T(8,128)(2,1)S(1)}, bf16[1,192,2048]{2,1,0:T(8,128)(2,1)}, u32[]{:S(2)}) copy-start(bf16[1,192,2048]{2,1,0:T(8,128)(2,1)} %param.10) | copy-start | bytes 2359300
  38.3 45.1 %all-to-all-start = ((bf16[4,200,768]{2,1,0:T(8,128)(2,1)}), bf16[4,200,768]{2,1,0:T(8,128)(2,1)S(1)}, u32[]{:S(2)}, u32[]{:S(2)}) async-start(bf16[4,200,768]{2,1,0:T(8,128)(2,1)} %pack.1), calls=%async_computation | async-start | bytes 2457600 | tf_op jit(solution)/shard_map/all_to_all | solution.py:215
  44.4 14.6 %collective-permute-start.1 = (bf16[32,2048]{1,0:T(8,128)(2,1)S(1)}, bf16[32,2048]{1,0:T(8,128)(2,1)S(1)}, u32[]{:S(2)}, u32[]{:S(2)}) collective-permute-start(bf16[32,2048]{1,0:T(8,128)(2,1)S(1)} %copy-done.8), channel_id=1, source_target_pairs={{384,64},{0,320},{416,96},{32,352},{448,128},{64,384},{480,160},{9... | collective-permute-start | bytes 393224 | tf_op jit(solution)/shard_map/ppermute | solution.py:227
  53.4 16.1 %collective-permute-start.2 = (bf16[32,2048]{1,0:T(8,128)(2,1)S(1)}, bf16[32,2048]{1,0:T(8,128)(2,1)S(1)}, u32[]{:S(2)}, u32[]{:S(2)}) collective-permute-start(bf16[32,2048]{1,0:T(8,128)(2,1)S(1)} %copy-done.8), channel_id=1, source_target_pairs={{256,32},{384,288},{0,96},{128,352},{32,0},{160,256},{288,64},{416... | collective-permute-start | bytes 393224 | tf_op jit(solution)/shard_map/ppermute | solution.py:230
  69.6 3.9 %collective-permute-start.3 = (bf16[64,2048]{1,0:T(8,128)(2,1)S(1)}, bf16[64,2048]{1,0:T(8,128)(2,1)S(1)}, u32[]{:S(2)}, u32[]{:S(2)}) collective-permute-start(bf16[64,2048]{1,0:T(8,128)(2,1)S(1)} %get-tuple-element.43), channel_id=1, source_target_pairs={{0,4},{4,0},{1,5},{5,1},{2,6},{6,2},{3,7},{7,3},{8,12},{12,8},{9,1... | collective-permute-start | bytes 786440 | tf_op jit(solution)/shard_map/ppermute | solution.py:207
  71.5 33.3 %collective-permute-start.7 = (bf16[192,2048]{1,0:T(8,128)(2,1)S(1)}, bf16[192,2048]{1,0:T(8,128)(2,1)S(1)}, u32[]{:S(2)}, u32[]{:S(2)}) collective-permute-start(bf16[192,2048]{1,0:T(8,128)(2,1)S(1)} %bitcast.18), channel_id=1, source_target_pairs={{0,128},{128,0},{256,384},{384,256},{1,129},{129,1},{257,385},{385... | collective-permute-start | bytes 2359304 | tf_op jit(solution)/shard_map/ppermute | solution.py:207
  73.5 28.8 %collective-permute-start.6 = (bf16[2,64,2048]{2,1,0:T(8,128)(2,1)S(1)}, bf16[2,64,2048]{2,1,0:T(8,128)(2,1)}, u32[]{:S(2)}, u32[]{:S(2)}) collective-permute-start(bf16[2,64,2048]{2,1,0:T(8,128)(2,1)S(1)} %pad_maximum_fusion.w0), channel_id=1, source_target_pairs={{0,24},{8,16},{16,8},{24,0},{1,25},{9,17},{17,9},{25,1},{2,26},{10... | collective-permute-start | bytes 1572872 | tf_op jit(solution)/shard_map/ppermute | solution.py:207
  77.7 24.6 %collective-permute-start.5 = (bf16[2,64,2048]{2,1,0:T(8,128)(2,1)S(1)}, bf16[2,64,2048]{2,1,0:T(8,128)(2,1)}, u32[]{:S(2)}, u32[]{:S(2)}) collective-permute-start(bf16[2,64,2048]{2,1,0:T(8,128)(2,1)S(1)} %pad_maximum_fusion.w0), channel_id=1, source_target_pairs={{0,16},{8,24},{16,0},{24,8},{1,17},{9,25},{17,1},{25,9},{2,18},{10... | collective-permute-start | bytes 1572872 | tf_op jit(solution)/shard_map/ppermute | solution.py:207
  80.2 24.6 %collective-permute-start.4 = (bf16[2,64,2048]{2,1,0:T(8,128)(2,1)S(1)}, bf16[2,64,2048]{2,1,0:T(8,128)(2,1)}, u32[]{:S(2)}, u32[]{:S(2)}) collective-permute-start(bf16[2,64,2048]{2,1,0:T(8,128)(2,1)S(1)} %pad_maximum_fusion.w0), channel_id=1, source_target_pairs={{0,8},{8,0},{16,24},{24,16},{1,9},{9,1},{17,25},{25,17},{2,10},{10... | collective-permute-start | bytes 1572872 | tf_op jit(solution)/shard_map/ppermute | solution.py:207
  88.1 0.9 copy-start.3
  89.0 15.9 %collective-permute-start = (bf16[384,256]{1,0:T(8,128)(2,1)}, bf16[384,256]{1,0:T(8,128)(2,1)}, u32[]{:S(2)}, u32[]{:S(2)}) collective-permute-start(bf16[384,256]{1,0:T(8,128)(2,1)} %get-tuple-element.24.o_far), channel_id=1, source_target_pairs={{0,256},{128,384},{256,0},{384,128},{1,257},{129,385},{257,1},{385... | collective-permute-start | bytes 589832 | tf_op jit(solution)/shard_map/ppermute | solution.py:207
  108.1 1.0 copy-start.1
  109.1 5.2 %collective-permute-start.8 = (bf16[4,4,2,32,512]{4,3,2,1,0:T(8,128)(2,1)}, bf16[4,4,2,32,512]{4,3,2,1,0:T(8,128)(2,1)}, u32[]{:S(2)}, u32[]{:S(2)}) collective-permute-start(bf16[4,4,2,32,512]{4,3,2,1,0:T(8,128)(2,1)} %get-tuple-element.30), channel_id=1, source_target_pairs={{0,4},{4,0},{1,5},{5,1},{2,6},{6,2},{3,7},{7,3},{8,12},{12,8},{9,1... | collective-permute-start | bytes 3145736 | tf_op jit(solution)/shard_map/ppermute | solution.py:207
  111.1 3.2 %copy-start.2 = (bf16[4,4,2,32,512]{4,3,2,1,0:T(8,128)(2,1)S(1)}, bf16[4,4,2,32,512]{4,3,2,1,0:T(8,128)(2,1)}, u32[]{:S(2)}) copy-start(bf16[4,4,2,32,512]{4,3,2,1,0:T(8,128)(2,1)} %copy-done.1) | copy-start | bytes 3145732
  114.2 2.8 %copy-start.5 = (bf16[384,256]{1,0:T(8,128)(2,1)}, bf16[384,256]{1,0:T(8,128)(2,1)S(1)}, u32[]{:S(2)}) copy-start(bf16[384,256]{1,0:T(8,128)(2,1)S(1)} %get-tuple-element.35.g_near) | copy-start | bytes 589828
  114.2 2.8 %copy-start.7 = (bf16[384,256]{1,0:T(8,128)(2,1)}, bf16[384,256]{1,0:T(8,128)(2,1)S(1)}, u32[]{:S(2)}) copy-start(bf16[384,256]{1,0:T(8,128)(2,1)S(1)} %get-tuple-element.31) | copy-start | bytes 589828
  117.0 20.6 %copy-start.4 = (f32[768,256]{1,0:T(8,128)S(1)}, f32[768,256]{1,0:T(8,128)}, u32[]{:S(2)}) copy-start(f32[768,256]{1,0:T(8,128)} %copy-done.3) | copy-start | bytes 2359300
  117.0 20.6 %copy-start.6 = (bf16[384,256]{1,0:T(8,128)(2,1)S(1)}, bf16[384,256]{1,0:T(8,128)(2,1)}, u32[]{:S(2)}) copy-start(bf16[384,256]{1,0:T(8,128)(2,1)} %copy-done.5) | copy-start | bytes 589828
  117.0 27.2 %all-to-all-start.1 = ((bf16[16,2,32,512]{3,2,1,0:T(8,128)(2,1)}), bf16[16,2,32,512]{3,2,1,0:T(8,128)(2,1)S(1)}, u32[]{:S(2)}, u32[]{:S(2)}) async-start(bf16[16,2,32,512]{3,2,1,0:T(8,128)(2,1)} %bitcast.21), calls=%async_computation.1 | async-start | bytes 2097152 | tf_op jit(solution)/shard_map/all_to_all | solution.py:215
  123.4 14.2 %collective-permute-start.11 = (bf16[384,256]{1,0:T(8,128)(2,1)}, bf16[384,256]{1,0:T(8,128)(2,1)S(1)}, u32[]{:S(2)}, u32[]{:S(2)}) collective-permute-start(bf16[384,256]{1,0:T(8,128)(2,1)} %copy-done.7), channel_id=1, source_target_pairs={{0,256},{128,384},{256,0},{384,128},{1,257},{129,385},{257,1},{385... | collective-permute-start | bytes 589832 | tf_op jit(solution)/shard_map/ppermute | solution.py:207
  144.2 34.4 %all-to-all-start.2 = ((bf16[4,192,768]{2,1,0:T(8,128)(2,1)}), bf16[4,192,768]{2,1,0:T(8,128)(2,1)S(1)}, u32[]{:S(2)}, u32[]{:S(2)}) async-start(bf16[4,192,768]{2,1,0:T(8,128)(2,1)} %backward.1), calls=%async_computation.2 | async-start | bytes 2359296 | tf_op jit(solution)/shard_map/all_to_all | solution.py:215
  147.9 24.0 %collective-permute-start.9 = (bf16[32,512]{1,0:T(8,128)(2,1)S(1)}, bf16[32,512]{1,0:T(8,128)(2,1)S(1)}, u32[]{:S(2)}, u32[]{:S(2)}) collective-permute-start(bf16[32,512]{1,0:T(8,128)(2,1)S(1)} %get-tuple-element.33), channel_id=1, source_target_pairs={{0,0},{32,256},{64,128},{96,384},{128,64},{160,320},{192,192},{224... | collective-permute-start | bytes 98312 | tf_op jit(solution)/shard_map/ppermute | solution.py:281
  159.4 19.2 %collective-permute-start.10 = (bf16[32,512]{1,0:T(8,128)(2,1)S(1)}, bf16[32,512]{1,0:T(8,128)(2,1)S(1)}, u32[]{:S(2)}, u32[]{:S(2)}) collective-permute-start(bf16[32,512]{1,0:T(8,128)(2,1)S(1)} %get-tuple-element.34), channel_id=1, source_target_pairs={{0,32},{32,288},{64,160},{96,416},{128,96},{160,352},{192,224},{22... | collective-permute-start | bytes 98312 | tf_op jit(solution)/shard_map/ppermute | solution.py:281
  199.4 10.4 %all-to-all-start.4 = ((bf16[4,32,512]{2,1,0:T(8,128)(2,1)}), bf16[4,32,512]{2,1,0:T(8,128)(2,1)S(1)}, u32[]{:S(2)}, u32[]{:S(2)}) async-start(bf16[4,32,512]{2,1,0:T(8,128)(2,1)} %quarter.1), calls=%async_computation.4 | async-start | bytes 262144 | tf_op jit(solution)/shard_map/all_to_all | solution.py:215

commit v6 on v2

--- a/solution.py
+++ b/solution.py
@@ -45,15 +45,20 @@
     return 2 * (b % 2) + b // 2
 
 
-def pack_kernel(ids, q_ref, k_ref, v_ref, out):
+def pack_kernel(ids, q_ref, k_ref, v_ref, out, sems):
+    copies = []
+    for j in range(4):
+        cols = pl.ds(256 * group_of(j), 256)
+        for n, ref in enumerate((q_ref, k_ref, v_ref)):
+            to = out.at[j, pl.ds(0, 192), pl.ds(256 * n, 256)]
+            copies.append(pltpu.make_async_copy(ref.at[:, cols], to, sems.at[3 * j + n]))
+            copies[-1].start()
     lane = lax.broadcasted_iota(jnp.int32, (8, 768), 1)
     block = jnp.where(lane < 384, ids[0], ids[1]).astype(F32).astype(BF16)
     for j in range(4):
-        cols = slice(256 * group_of(j), 256 * group_of(j) + 256)
-        out[j, 0:192, 0:256] = q_ref[:, cols]
-        out[j, 0:192, 256:512] = k_ref[:, cols]
-        out[j, 0:192, 512:768] = v_ref[:, cols]
         out[j, 192:200, :] = block
+    for copy in copies:
+        copy.wait()
 
 
 def unpack_kernel(home, dq, dk, dv):
@@ -216,7 +221,6 @@
     z = ("seq", "zh")
 
     grads = out_grad[0]
-    mate_grads = swap(grads, "seq", 1, 4)
 
     first = lax.ppermute(
         out_weight, z, nearest([d for d in places if d[0] // 2 != d[1] % 2], lambda i, j: i ^ 2)
@@ -224,18 +228,23 @@
     second = lax.ppermute(
         out_weight, z, nearest(places, lambda i, j: i ^ 1 if i // 2 == j % 2 else i ^ 3)
     )
-    packed = call(pack_kernel, arr((4, 200, 768)), 1, 3, "pack")(
-        block_ids, query[0], key[0], value[0]
-    )
-    packed, mate_grads, first, second = lax.optimization_barrier(
-        (packed, mate_grads, first, second)
-    )
+    packed = pl.pallas_call(
+        pack_kernel,
+        out_shape=arr((4, 200, 768)),
+        in_specs=[SMEM] + [pl.BlockSpec(memory_space=pl.ANY)] * 3,
+        out_specs=VMEM,
+        scratch_shapes=[pltpu.SemaphoreType.DMA((12,))],
+        compiler_params=pltpu.CompilerParams(vmem_limit_bytes=60 * 1024 * 1024),
+        cost_estimate=pl.CostEstimate(flops=1000, bytes_accessed=1000, transcendentals=0),
+        name="pack",
+    )(block_ids, query[0], key[0], value[0])
     rows = exchange(packed, "seq")
+    grads, first, second = lax.optimization_barrier((grads, first, second))
+    mate_grads = swap(grads, "seq", 1, 4)
     first = jnp.where((a >> 1) == half, out_weight, first)
     piece = jnp.concatenate([first, second], axis=0)
     pieces = [piece] + [swap(piece, "y", k, 4) for k in (1, 2, 3)]
     w_here = jnp.stack(pieces)
-    rows, w_here = lax.optimization_barrier((rows, w_here))
     w_there = swap(w_here, "c", 1, 2)
 
     g_near, g_send = call(
@@ -247,11 +256,10 @@
         forward_kernel, [arr((384, 256))] * 2 + [arr((768, 256), F32)], 1, 1, "forward", kv
     )(scalars(b), rows)
     o_there = swap(o_far, "seq", 2, 4)
-    o_there, _ = lax.optimization_barrier((o_there, g_send))
+    o_there, w_here = lax.optimization_barrier((o_there, w_here))
     keep, send = call(weight_kernel, [arr((4, 4, 2, 32, 512))] * 2, 1, 4, "weight")(
         scalars(core), o_near, o_there, grads, mate_grads
     )
-    send, g_far = lax.optimization_barrier((send, g_far))
     taken = swap(send, "c", 1, 2)
     back = call(
         backward_kernel,

time: 186 us -> 169 us (0.909)
  waiting for transfers between devices: 68.7 us -> 52.8 us
  local copies, waits for them, and re-layouts: 9.16 us -> 2.88 us
  Pallas kernels: 19.1 us -> 21.2 us
    all_to_all x4, waiting for transfers between devices: 28.4 us -> 7.77 us  [exchange(): return lax.all_to_all(value, axes, 0, 0, tiled=True)]
    ppermute x1, waiting for transfers between devices: 0.01 us -> 10.4 us  [shards(): lax.ppermute(own, z, turn).astype(F32)]
    ppermute x1, waiting for transfers between devices: 16 us -> 6.21 us  [shards(): lax.ppermute(other, z, turn2).astype(F32)]
    unnamed x28 -> x18, local copies, waits for them, and re-layouts: 9.06 us -> 2.78 us
    ppermute x1, waiting for transfers between devices: 5.6 us -> 10.6 us  [shards(): lax.ppermute(out_weight, z, nearest(places, lambda i, j: i ^ 1 if i // 2...]
    ppermute x1, starting transfers between devices: 5.02 us -> 9.07 us  [shards(): lax.ppermute(own, z, turn).astype(F32)]
    ppermute x1, starting transfers between devices: 4.83 us -> 1.92 us  [shards(): lax.ppermute(other, z, turn2).astype(F32)]
    ppermute x8, starting transfers between devices: 24.2 us -> 21.7 us  [swap(): return lax.ppermute(value, axis, [(i, i ^ mask) for i in range(n)])]
  transfers between devices with their start and end apart: 16 -> 16, of which waited for: 12 -> 8; matrix products, arithmetic and copies ran while one was open for 0% -> 2% of each run, Pallas kernels for 10% -> 8%
where the time goes in v6:
time: 169 us; the launch traced here: 168 us
  starting transfers between devices  68.2 us (40%)
  waiting for transfers between devices  52.8 us (31%)
  Pallas kernels  21.2 us (13%)
  blocking collectives  18.3 us (11%)
  other arithmetic  3.41 us (2%)
  local copies, waits for them, and re-layouts  2.88 us (2%)
    ppermute x8, starting transfers between devices, swap(): return lax.ppermute(value, axis, [(i, i ^ mask) for i in range(n)])  21.7 us
    all_to_all x4, starting transfers between devices, exchange(): return lax.all_to_all(value, axes, 0, 0, tiled=True)  20.9 us
    all_to_all x1, blocking collectives, exchange(): return lax.all_to_all(value, axes, 0, 0, tiled=True)  18.3 us
    ppermute x8, waiting for transfers between devices, swap(): return lax.ppermute(value, axis, [(i, i ^ mask) for i in range(n)])  17.8 us
    ppermute x1, waiting for transfers between devices, shards(): lax.ppermute(out_weight, z, nearest(places, lambda i, j: i ^ 1 if i // 2...  10.6 us
    ppermute x1, waiting for transfers between devices, shards(): lax.ppermute(own, z, turn).astype(F32)  10.4 us
    ppermute x1, starting transfers between devices, shards(): lax.ppermute(out_weight, z, nearest([d for d in places if d[0] // 2 != d[...  9.08 us
    ppermute x1, starting transfers between devices, shards(): lax.ppermute(own, z, turn).astype(F32)  9.07 us
  transfers between devices with their start and end apart: 16, of which 8 were waited for; matrix products, arithmetic and copies ran while one was open for 2% of the time, Pallas kernels for 8%

profile of v6, /device:TPU:128, one launch (start us, length us, event | category | flops | bytes accessed | tf_op | source)
XLA Modules:
  0.0 167.7 jit_solution(249406518015591398)
XLA Ops:
  0.6 3.2 %pack.1 = bf16[4,200,768]{2,1,0:T(8,128)(2,1)} custom-call(s32[2]{0:T(128)} %ids.1, bf16[192,1024]{1,0:T(8,128)(2,1)} %bitcast.24, bf16[192,1024]{1,0:T(8,128)(2,1)} %bitcast.25, bf16[192,1024]{1,0:T(8,128)(2,1)} %bitcast.26), custom_call_target="tpu_custom_call" | custom-call | flops 1000 | bytes 1000 | tf_op jit(solution)/shard_map/pack/pallas_call | solution.py:231
  3.8 0.0 copy-start.8
  3.8 0.0 copy-start
  3.8 6.0 %all-to-all-start = ((bf16[4,200,768]{2,1,0:T(8,128)(2,1)}), bf16[4,200,768]{2,1,0:T(8,128)(2,1)S(1)}, u32[]{:S(2)}, u32[]{:S(2)}) async-start(bf16[4,200,768]{2,1,0:T(8,128)(2,1)} %pack.1), calls=%async_computation | async-start | bytes 2457600 | tf_op jit(solution)/shard_map/all_to_all | solution.py:213
  9.9 9.1 %collective-permute-start.1 = (bf16[32,2048]{1,0:T(8,128)(2,1)S(1)}, bf16[32,2048]{1,0:T(8,128)(2,1)S(1)}, u32[]{:S(2)}, u32[]{:S(2)}) collective-permute-start(bf16[32,2048]{1,0:T(8,128)(2,1)S(1)} %copy-done.8), channel_id=1, source_target_pairs={{384,64},{0,320},{416,96},{32,352},{448,128},{64,384},{480,160},{9... | collective-permute-start | bytes 393224 | tf_op jit(solution)/shard_map/ppermute | solution.py:225
  19.0 5.5 %collective-permute-start.2 = (bf16[32,2048]{1,0:T(8,128)(2,1)S(1)}, bf16[32,2048]{1,0:T(8,128)(2,1)S(1)}, u32[]{:S(2)}, u32[]{:S(2)}) collective-permute-start(bf16[32,2048]{1,0:T(8,128)(2,1)S(1)} %copy-done.8), channel_id=1, source_target_pairs={{256,32},{384,288},{0,96},{128,352},{32,0},{160,256},{288,64},{416... | collective-permute-start | bytes 393224 | tf_op jit(solution)/shard_map/ppermute | solution.py:228
  24.4 0.0 collective-permute-done.1
  24.4 10.6 %collective-permute-done.2 = bf16[32,2048]{1,0:T(8,128)(2,1)S(1)} collective-permute-done((bf16[32,2048]{1,0:T(8,128)(2,1)S(1)}, bf16[32,2048]{1,0:T(8,128)(2,1)S(1)}, u32[]{:S(2)}, u32[]{:S(2)}) %collective-permute-start.2) | collective-permute-done | bytes 131104 | tf_op jit(solution)/shard_map/ppermute | solution.py:228
  35.0 1.9 %collective-permute-start.6 = (bf16[192,2048]{1,0:T(8,128)(2,1)S(1)}, bf16[192,2048]{1,0:T(8,128)(2,1)}, u32[]{:S(2)}, u32[]{:S(2)}) collective-permute-start(bf16[192,2048]{1,0:T(8,128)(2,1)S(1)} %bitcast.20), channel_id=1, source_target_pairs={{0,128},{128,0},{256,384},{384,256},{1,129},{129,1},{257,385},{385... | collective-permute-start | bytes 2359304 | tf_op jit(solution)/shard_map/ppermute | solution.py:205
  37.0 0.8 fusion
  37.7 4.2 %collective-permute-start.4 = (bf16[64,2048]{1,0:T(8,128)(2,1)S(1)}, bf16[64,2048]{1,0:T(8,128)(2,1)}, u32[]{:S(2)}, u32[]{:S(2)}) collective-permute-start(bf16[64,2048]{1,0:T(8,128)(2,1)S(1)} %get-tuple-element.41), channel_id=1, source_target_pairs={{0,16},{8,24},{16,0},{24,8},{1,17},{9,25},{17,1},{25,9},{2,18},{10... | collective-permute-start | bytes 786440 | tf_op jit(solution)/shard_map/ppermute | solution.py:205
  42.0 2.6 %collective-permute-start.3 = (bf16[64,2048]{1,0:T(8,128)(2,1)S(1)}, bf16[64,2048]{1,0:T(8,128)(2,1)}, u32[]{:S(2)}, u32[]{:S(2)}) collective-permute-start(bf16[64,2048]{1,0:T(8,128)(2,1)S(1)} %get-tuple-element.41), channel_id=1, source_target_pairs={{0,8},{8,0},{16,24},{24,16},{1,9},{9,1},{17,25},{25,17},{2,10},{10... | collective-permute-start | bytes 786440 | tf_op jit(solution)/shard_map/ppermute | solution.py:205
  44.6 3.0 %collective-permute-start.5 = (bf16[64,2048]{1,0:T(8,128)(2,1)S(1)}, bf16[64,2048]{1,0:T(8,128)(2,1)S(1)}, u32[]{:S(2)}, u32[]{:S(2)}) collective-permute-start(bf16[64,2048]{1,0:T(8,128)(2,1)S(1)} %get-tuple-element.41), channel_id=1, source_target_pairs={{0,24},{8,16},{16,8},{24,0},{1,25},{9,17},{17,9},{25,1},{2,26},{10... | collective-permute-start | bytes 786440 | tf_op jit(solution)/shard_map/ppermute | solution.py:205
  47.6 0.0 all-to-all-done.x_all
  47.6 0.0 copy-start.6
  47.6 4.0 %forward.1 = (bf16[384,256]{1,0:T(8,128)(2,1)S(1)}, bf16[384,256]{1,0:T(8,128)(2,1)S(1)}, f32[768,256]{1,0:T(8,128)S(1)}) custom-call(s32[1]{0:T(128)} %bitcast.1.where, bf16[4,200,768]{2,1,0:T(8,128)(2,1)S(1)} %all-to-all-done.x_all), custom_call_target="tpu_custom_call" | custom-call | flops 1000 | bytes 1000 | tf_op jit(solution)/shard_map/forward/pallas_call | solution.py:255
  51.6 0.9 copy-done.2
  52.5 3.8 %collective-permute-start = (bf16[384,256]{1,0:T(8,128)(2,1)S(1)}, bf16[384,256]{1,0:T(8,128)(2,1)S(1)}, u32[]{:S(2)}, u32[]{:S(2)}) collective-permute-start(bf16[384,256]{1,0:T(8,128)(2,1)S(1)} %get-tuple-element.23.o_far), channel_id=1, source_target_pairs={{0,256},{128,384},{256,0},{384,128},{1,257},{129,385},{257,1},{385... | collective-permute-start | bytes 589832 | tf_op jit(solution)/shard_map/ppermute | solution.py:205
  56.3 0.0 collective-permute-done.5
  56.3 0.0 copy-start.7
  56.3 0.7 copy-done.7
  57.0 1.2 pad_maximum_fusion.w_here
  58.3 7.0 %collective-permute-done.o_there = bf16[384,256]{1,0:T(8,128)(2,1)S(1)} collective-permute-done((bf16[384,256]{1,0:T(8,128)(2,1)S(1)}, bf16[384,256]{1,0:T(8,128)(2,1)S(1)}, u32[]{:S(2)}, u32[]{:S(2)}) %collective-permute-start) | collective-permute-done | bytes 196640 | tf_op jit(solution)/shard_map/ppermute | solution.py:205
  65.2 2.4 %weight.1 = (bf16[4,4,2,32,512]{4,3,2,1,0:T(8,128)(2,1)S(1)}, bf16[4,4,2,32,512]{4,3,2,1,0:T(8,128)(2,1)S(1)}) custom-call(s32[1]{0:T(128)} %bitcast.where, bf16[384,256]{1,0:T(8,128)(2,1)S(1)} %get-tuple-element.22.o_here.o_near, bf16[384,256]{1,0:T(8,128)(2,1)S(1)} %collective-permute-done.o_there, bf16[192,2048]{1,0:T(8,128)(2,1)S(1)} %bitcast.21, ...), custom_call_target="tpu_custom_call" | custom-call | flops 1000 | bytes 1000 | tf_op jit(solution)/shard_map/weight/pallas_call | solution.py:260
  67.7 1.9 %collective-permute-start.7 = (bf16[4,4,2,32,512]{4,3,2,1,0:T(8,128)(2,1)S(1)}, bf16[4,4,2,32,512]{4,3,2,1,0:T(8,128)(2,1)S(1)}, u32[]{:S(2)}, u32[]{:S(2)}) collective-permute-start(bf16[4,4,2,32,512]{4,3,2,1,0:T(8,128)(2,1)S(1)} %get-tuple-element.29), channel_id=1, source_target_pairs={{0,4},{4,0},{1,5},{5,1},{2,6},{6,2},{3,7},{7,3},{8,12},{12,8},{9,1... | collective-permute-start | bytes 3145736 | tf_op jit(solution)/shard_map/ppermute | solution.py:205
  69.6 2.4 %collective-permute-start.10 = (bf16[4,64,2048]{2,1,0:T(8,128)(2,1)S(1)}, bf16[4,64,2048]{2,1,0:T(8,128)(2,1)}, u32[]{:S(2)}, u32[]{:S(2)}) collective-permute-start(bf16[4,64,2048]{2,1,0:T(8,128)(2,1)S(1)} %pad_maximum_fusion.w_here), channel_id=1, source_target_pairs={{0,4},{4,0},{1,5},{5,1},{2,6},{6,2},{3,7},{7,3},{8,12},{12,8},{9,1... | collective-permute-start | bytes 3145736 | tf_op jit(solution)/shard_map/ppermute | solution.py:205
  72.0 0.2 collective-permute-done.7
  72.2 1.4 add_convert_fusion
  73.6 7.0 %all-to-all-start.1 = ((bf16[16,2,32,512]{3,2,1,0:T(8,128)(2,1)}), bf16[16,2,32,512]{3,2,1,0:T(8,128)(2,1)S(1)}, u32[]{:S(2)}, u32[]{:S(2)}) async-start(bf16[16,2,32,512]{3,2,1,0:T(8,128)(2,1)} %bitcast.23), calls=%async_computation.1 | async-start | bytes 2097152 | tf_op jit(solution)/shard_map/all_to_all | solution.py:213
  80.6 0.1 stack.53.where
  80.7 1.1 copy-done.1
  81.9 3.2 %project.1 = (bf16[384,256]{1,0:T(8,128)(2,1)S(1)}, bf16[384,256]{1,0:T(8,128)(2,1)S(1)}) custom-call(s32[6]{0:T(128)S(1)} %stack.53.where, bf16[192,2048]{1,0:T(8,128)(2,1)S(1)} %bitcast.22, bf16[192,2048]{1,0:T(8,128)(2,1)} %collective-permute-done.6.mate_ref, bf16[4,64,2048]{2,1,0:T(8,128)(2,1)S(1)} %pad_maximum_fusion.w_here, ...), custom_call_target="tpu_custom_call" | custom-call | flops 1000 | bytes 1000 | tf_op jit(solution)/shard_map/project/pallas_call | solution.py:250
  85.1 1.9 %collective-permute-start.11 = (bf16[384,256]{1,0:T(8,128)(2,1)S(1)}, bf16[384,256]{1,0:T(8,128)(2,1)S(1)}, u32[]{:S(2)}, u32[]{:S(2)}) collective-permute-start(bf16[384,256]{1,0:T(8,128)(2,1)S(1)} %get-tuple-element.33), channel_id=1, source_target_pairs={{0,256},{128,384},{256,0},{384,128},{1,257},{129,385},{257,1},{385... | collective-permute-start | bytes 589832 | tf_op jit(solution)/shard_map/ppermute | solution.py:205
  87.0 10.6 %collective-permute-done.11.g_far = bf16[384,256]{1,0:T(8,128)(2,1)S(1)} collective-permute-done((bf16[384,256]{1,0:T(8,128)(2,1)S(1)}, bf16[384,256]{1,0:T(8,128)(2,1)S(1)}, u32[]{:S(2)}, u32[]{:S(2)}) %collective-permute-start.11) | collective-permute-done | bytes 196640 | tf_op jit(solution)/shard_map/ppermute | solution.py:205
  97.7 5.7 %backward.1 = bf16[4,192,768]{2,1,0:T(8,128)(2,1)} custom-call(s32[1]{0:T(128)} %bitcast.1.where, bf16[4,200,768]{2,1,0:T(8,128)(2,1)S(1)} %all-to-all-done.x_all, bf16[384,256]{1,0:T(8,128)(2,1)S(1)} %get-tuple-element.32.g_near, bf16[384,256]{1,0:T(8,128)(2,1)S(1)} %collective-permute-done.11.g_far, bf16[384,256]{1,0:T(8,128)(2,1)S(1)} %get-tuple-element.22.o_here.o_near, ...), custom_call_target="tpu_custom_call" | custom-call | flops 1000 | bytes 1000 | tf_op jit(solution)/shard_map/backward/pallas_call | solution.py:264
  103.4 3.5 %all-to-all-start.2 = ((bf16[4,192,768]{2,1,0:T(8,128)(2,1)}), bf16[4,192,768]{2,1,0:T(8,128)(2,1)S(1)}, u32[]{:S(2)}, u32[]{:S(2)}) async-start(bf16[4,192,768]{2,1,0:T(8,128)(2,1)} %backward.1), calls=%async_computation.2 | async-start | bytes 2359296 | tf_op jit(solution)/shard_map/all_to_all | solution.py:213
  106.9 0.1 sum.1
  107.1 9.1 %collective-permute-start.8 = (bf16[32,512]{1,0:T(8,128)(2,1)S(1)}, bf16[32,512]{1,0:T(8,128)(2,1)S(1)}, u32[]{:S(2)}, u32[]{:S(2)}) collective-permute-start(bf16[32,512]{1,0:T(8,128)(2,1)S(1)} %get-tuple-element.30), channel_id=1, source_target_pairs={{0,0},{32,256},{64,128},{96,384},{128,64},{160,320},{192,192},{224... | collective-permute-start | bytes 98312 | tf_op jit(solution)/shard_map/ppermute | solution.py:278
  116.1 1.9 %collective-permute-start.9 = (bf16[32,512]{1,0:T(8,128)(2,1)S(1)}, bf16[32,512]{1,0:T(8,128)(2,1)S(1)}, u32[]{:S(2)}, u32[]{:S(2)}) collective-permute-start(bf16[32,512]{1,0:T(8,128)(2,1)S(1)} %get-tuple-element.31), channel_id=1, source_target_pairs={{0,32},{32,288},{64,160},{96,416},{128,96},{160,352},{192,224},{22... | collective-permute-start | bytes 98312 | tf_op jit(solution)/shard_map/ppermute | solution.py:278
  118.1 10.4 %collective-permute-done.8 = bf16[32,512]{1,0:T(8,128)(2,1)S(1)} collective-permute-done((bf16[32,512]{1,0:T(8,128)(2,1)S(1)}, bf16[32,512]{1,0:T(8,128)(2,1)S(1)}, u32[]{:S(2)}, u32[]{:S(2)}) %collective-permute-start.8) | collective-permute-done | bytes 32800 | tf_op jit(solution)/shard_map/ppermute | solution.py:278
  128.5 6.2 %collective-permute-done.9 = bf16[32,512]{1,0:T(8,128)(2,1)S(1)} collective-permute-done((bf16[32,512]{1,0:T(8,128)(2,1)S(1)}, bf16[32,512]{1,0:T(8,128)(2,1)S(1)}, u32[]{:S(2)}, u32[]{:S(2)}) %collective-permute-start.9) | collective-permute-done | bytes 32800 | tf_op jit(solution)/shard_map/ppermute | solution.py:278
  134.7 2.9 %all-to-all-done.2.home = bf16[4,192,768]{2,1,0:T(8,128)(2,1)S(1)} async-done(((bf16[4,192,768]{2,1,0:T(8,128)(2,1)}), bf16[4,192,768]{2,1,0:T(8,128)(2,1)S(1)}, u32[]{:S(2)}, u32[]{:S(2)}) %all-to-all-start.2) | async-done | bytes 1179680 | tf_op jit(solution)/shard_map/all_to_all | solution.py:213
  137.7 18.3 %all_to_all.25.parts = bf16[4,32,512]{2,1,0:T(8,128)(2,1)S(1)} all-to-all(bf16[4,32,512]{2,1,0:T(8,128)(2,1)S(1)} %broadcast_in_dim.18), channel_id=1, replica_groups=mesh['seq'=4,'zh'=4,'y'=4,'c'=2,'dp'=4] {'seq'}, dimensions={0} | all-to-all | bytes 262144 | tf_op jit(solution)/shard_map/all_to_all | solution.py:213
  155.9 0.7 quarter.1
  156.6 4.4 %all-to-all-start.4 = ((bf16[4,32,512]{2,1,0:T(8,128)(2,1)}), bf16[4,32,512]{2,1,0:T(8,128)(2,1)S(1)}, u32[]{:S(2)}, u32[]{:S(2)}) async-start(bf16[4,32,512]{2,1,0:T(8,128)(2,1)} %quarter.1), calls=%async_computation.4 | async-start | bytes 262144 | tf_op jit(solution)/shard_map/all_to_all | solution.py:213
  161.0 1.2 unpack.1
  162.2 4.8 %all-to-all-done.4.parts = bf16[4,32,512]{2,1,0:T(8,128)(2,1)S(1)} async-done(((bf16[4,32,512]{2,1,0:T(8,128)(2,1)}), bf16[4,32,512]{2,1,0:T(8,128)(2,1)S(1)}, u32[]{:S(2)}, u32[]{:S(2)}) %all-to-all-start.4) | async-done | bytes 131104 | tf_op jit(solution)/shard_map/all_to_all | solution.py:213
  167.0 0.7 finish.1
  (19 shorter events, 0.1 us)
Async XLA Ops:
  3.8 6.1 %copy-start.8 = (bf16[32,2048]{1,0:T(8,128)(2,1)S(1)}, bf16[32,2048]{1,0:T(8,128)(2,1)}, u32[]{:S(2)}) copy-start(bf16[32,2048]{1,0:T(8,128)(2,1)} %param.9) | copy-start | bytes 393220
  3.8 31.2 %copy-start = (bf16[1,192,2048]{2,1,0:T(8,128)(2,1)S(1)}, bf16[1,192,2048]{2,1,0:T(8,128)(2,1)}, u32[]{:S(2)}) copy-start(bf16[1,192,2048]{2,1,0:T(8,128)(2,1)} %param.10) | copy-start | bytes 2359300
  3.8 43.8 %all-to-all-start = ((bf16[4,200,768]{2,1,0:T(8,128)(2,1)}), bf16[4,200,768]{2,1,0:T(8,128)(2,1)S(1)}, u32[]{:S(2)}, u32[]{:S(2)}) async-start(bf16[4,200,768]{2,1,0:T(8,128)(2,1)} %pack.1), calls=%async_computation | async-start | bytes 2457600 | tf_op jit(solution)/shard_map/all_to_all | solution.py:213
  9.9 14.6 %collective-permute-start.1 = (bf16[32,2048]{1,0:T(8,128)(2,1)S(1)}, bf16[32,2048]{1,0:T(8,128)(2,1)S(1)}, u32[]{:S(2)}, u32[]{:S(2)}) collective-permute-start(bf16[32,2048]{1,0:T(8,128)(2,1)S(1)} %copy-done.8), channel_id=1, source_target_pairs={{384,64},{0,320},{416,96},{32,352},{448,128},{64,384},{480,160},{9... | collective-permute-start | bytes 393224 | tf_op jit(solution)/shard_map/ppermute | solution.py:225
  19.0 16.1 %collective-permute-start.2 = (bf16[32,2048]{1,0:T(8,128)(2,1)S(1)}, bf16[32,2048]{1,0:T(8,128)(2,1)S(1)}, u32[]{:S(2)}, u32[]{:S(2)}) collective-permute-start(bf16[32,2048]{1,0:T(8,128)(2,1)S(1)} %copy-done.8), channel_id=1, source_target_pairs={{256,32},{384,288},{0,96},{128,352},{32,0},{160,256},{288,64},{416... | collective-permute-start | bytes 393224 | tf_op jit(solution)/shard_map/ppermute | solution.py:228
  35.0 30.2 %collective-permute-start.6 = (bf16[192,2048]{1,0:T(8,128)(2,1)S(1)}, bf16[192,2048]{1,0:T(8,128)(2,1)}, u32[]{:S(2)}, u32[]{:S(2)}) collective-permute-start(bf16[192,2048]{1,0:T(8,128)(2,1)S(1)} %bitcast.20), channel_id=1, source_target_pairs={{0,128},{128,0},{256,384},{384,256},{1,129},{129,1},{257,385},{385... | collective-permute-start | bytes 2359304 | tf_op jit(solution)/shard_map/ppermute | solution.py:205
  37.7 18.6 %collective-permute-start.4 = (bf16[64,2048]{1,0:T(8,128)(2,1)S(1)}, bf16[64,2048]{1,0:T(8,128)(2,1)}, u32[]{:S(2)}, u32[]{:S(2)}) collective-permute-start(bf16[64,2048]{1,0:T(8,128)(2,1)S(1)} %get-tuple-element.41), channel_id=1, source_target_pairs={{0,16},{8,24},{16,0},{24,8},{1,17},{9,25},{17,1},{25,9},{2,18},{10... | collective-permute-start | bytes 786440 | tf_op jit(solution)/shard_map/ppermute | solution.py:205
  42.0 14.3 %collective-permute-start.3 = (bf16[64,2048]{1,0:T(8,128)(2,1)S(1)}, bf16[64,2048]{1,0:T(8,128)(2,1)}, u32[]{:S(2)}, u32[]{:S(2)}) collective-permute-start(bf16[64,2048]{1,0:T(8,128)(2,1)S(1)} %get-tuple-element.41), channel_id=1, source_target_pairs={{0,8},{8,0},{16,24},{24,16},{1,9},{9,1},{17,25},{25,17},{2,10},{10... | collective-permute-start | bytes 786440 | tf_op jit(solution)/shard_map/ppermute | solution.py:205
  44.6 11.8 %collective-permute-start.5 = (bf16[64,2048]{1,0:T(8,128)(2,1)S(1)}, bf16[64,2048]{1,0:T(8,128)(2,1)S(1)}, u32[]{:S(2)}, u32[]{:S(2)}) collective-permute-start(bf16[64,2048]{1,0:T(8,128)(2,1)S(1)} %get-tuple-element.41), channel_id=1, source_target_pairs={{0,24},{8,16},{16,8},{24,0},{1,25},{9,17},{17,9},{25,1},{2,26},{10... | collective-permute-start | bytes 786440 | tf_op jit(solution)/shard_map/ppermute | solution.py:205
  47.6 9.5 %copy-start.6 = (bf16[1,64,2048]{2,1,0:T(8,128)(2,1)S(1)}, bf16[1,64,2048]{2,1,0:T(8,128)(2,1)}, u32[]{:S(2)}) copy-start(bf16[1,64,2048]{2,1,0:T(8,128)(2,1)} %get-tuple-element.40) | copy-start | bytes 786436
  51.6 0.9 copy-start.2
  52.5 15.2 %copy-start.4 = (bf16[384,256]{1,0:T(8,128)(2,1)}, bf16[384,256]{1,0:T(8,128)(2,1)S(1)}, u32[]{:S(2)}) copy-start(bf16[384,256]{1,0:T(8,128)(2,1)S(1)} %get-tuple-element.23.o_far) | copy-start | bytes 589828
  52.5 12.7 %collective-permute-start = (bf16[384,256]{1,0:T(8,128)(2,1)S(1)}, bf16[384,256]{1,0:T(8,128)(2,1)S(1)}, u32[]{:S(2)}, u32[]{:S(2)}) collective-permute-start(bf16[384,256]{1,0:T(8,128)(2,1)S(1)} %get-tuple-element.23.o_far), channel_id=1, source_target_pairs={{0,256},{128,384},{256,0},{384,128},{1,257},{129,385},{257,1},{385... | collective-permute-start | bytes 589832 | tf_op jit(solution)/shard_map/ppermute | solution.py:205
  56.3 0.7 copy-start.7
  67.7 4.6 %collective-permute-start.7 = (bf16[4,4,2,32,512]{4,3,2,1,0:T(8,128)(2,1)S(1)}, bf16[4,4,2,32,512]{4,3,2,1,0:T(8,128)(2,1)S(1)}, u32[]{:S(2)}, u32[]{:S(2)}) collective-permute-start(bf16[4,4,2,32,512]{4,3,2,1,0:T(8,128)(2,1)S(1)} %get-tuple-element.29), channel_id=1, source_target_pairs={{0,4},{4,0},{1,5},{5,1},{2,6},{6,2},{3,7},{7,3},{8,12},{12,8},{9,1... | collective-permute-start | bytes 3145736 | tf_op jit(solution)/shard_map/ppermute | solution.py:205
  69.6 11.1 %collective-permute-start.10 = (bf16[4,64,2048]{2,1,0:T(8,128)(2,1)S(1)}, bf16[4,64,2048]{2,1,0:T(8,128)(2,1)}, u32[]{:S(2)}, u32[]{:S(2)}) collective-permute-start(bf16[4,64,2048]{2,1,0:T(8,128)(2,1)S(1)} %pad_maximum_fusion.w_here), channel_id=1, source_target_pairs={{0,4},{4,0},{1,5},{5,1},{2,6},{6,2},{3,7},{7,3},{8,12},{12,8},{9,1... | collective-permute-start | bytes 3145736 | tf_op jit(solution)/shard_map/ppermute | solution.py:205
  73.6 29.8 %all-to-all-start.1 = ((bf16[16,2,32,512]{3,2,1,0:T(8,128)(2,1)}), bf16[16,2,32,512]{3,2,1,0:T(8,128)(2,1)S(1)}, u32[]{:S(2)}, u32[]{:S(2)}) async-start(bf16[16,2,32,512]{3,2,1,0:T(8,128)(2,1)} %bitcast.23), calls=%async_computation.1 | async-start | bytes 2097152 | tf_op jit(solution)/shard_map/all_to_all | solution.py:213
  80.7 1.1 copy-start.1
  81.8 15.8 %copy-start.3 = (f32[768,256]{1,0:T(8,128)S(1)}, f32[768,256]{1,0:T(8,128)}, u32[]{:S(2)}) copy-start(f32[768,256]{1,0:T(8,128)} %copy-done.2) | copy-start | bytes 2359300
  81.8 15.8 %copy-start.5 = (bf16[384,256]{1,0:T(8,128)(2,1)S(1)}, bf16[384,256]{1,0:T(8,128)(2,1)}, u32[]{:S(2)}) copy-start(bf16[384,256]{1,0:T(8,128)(2,1)} %copy-done.4) | copy-start | bytes 589828
  85.1 12.6 %collective-permute-start.11 = (bf16[384,256]{1,0:T(8,128)(2,1)S(1)}, bf16[384,256]{1,0:T(8,128)(2,1)S(1)}, u32[]{:S(2)}, u32[]{:S(2)}) collective-permute-start(bf16[384,256]{1,0:T(8,128)(2,1)S(1)} %get-tuple-element.33), channel_id=1, source_target_pairs={{0,256},{128,384},{256,0},{384,128},{1,257},{129,385},{257,1},{385... | collective-permute-start | bytes 589832 | tf_op jit(solution)/shard_map/ppermute | solution.py:205
  103.4 34.2 %all-to-all-start.2 = ((bf16[4,192,768]{2,1,0:T(8,128)(2,1)}), bf16[4,192,768]{2,1,0:T(8,128)(2,1)S(1)}, u32[]{:S(2)}, u32[]{:S(2)}) async-start(bf16[4,192,768]{2,1,0:T(8,128)(2,1)} %backward.1), calls=%async_computation.2 | async-start | bytes 2359296 | tf_op jit(solution)/shard_map/all_to_all | solution.py:213
  107.1 21.4 %collective-permute-start.8 = (bf16[32,512]{1,0:T(8,128)(2,1)S(1)}, bf16[32,512]{1,0:T(8,128)(2,1)S(1)}, u32[]{:S(2)}, u32[]{:S(2)}) collective-permute-start(bf16[32,512]{1,0:T(8,128)(2,1)S(1)} %get-tuple-element.30), channel_id=1, source_target_pairs={{0,0},{32,256},{64,128},{96,384},{128,64},{160,320},{192,192},{224... | collective-permute-start | bytes 98312 | tf_op jit(solution)/shard_map/ppermute | solution.py:278
  116.1 18.5 %collective-permute-start.9 = (bf16[32,512]{1,0:T(8,128)(2,1)S(1)}, bf16[32,512]{1,0:T(8,128)(2,1)S(1)}, u32[]{:S(2)}, u32[]{:S(2)}) collective-permute-start(bf16[32,512]{1,0:T(8,128)(2,1)S(1)} %get-tuple-element.31), channel_id=1, source_target_pairs={{0,32},{32,288},{64,160},{96,416},{128,96},{160,352},{192,224},{22... | collective-permute-start | bytes 98312 | tf_op jit(solution)/shard_map/ppermute | solution.py:278
  156.6 10.4 %all-to-all-start.4 = ((bf16[4,32,512]{2,1,0:T(8,128)(2,1)}), bf16[4,32,512]{2,1,0:T(8,128)(2,1)S(1)}, u32[]{:S(2)}, u32[]{:S(2)}) async-start(bf16[4,32,512]{2,1,0:T(8,128)(2,1)} %quarter.1), calls=%async_computation.4 | async-start | bytes 262144 | tf_op jit(solution)/shard_map/all_to_all | solution.py:213

commit v7 on v6

--- a/solution.py
+++ b/solution.py
@@ -239,7 +239,6 @@
         name="pack",
     )(block_ids, query[0], key[0], value[0])
     rows = exchange(packed, "seq")
-    grads, first, second = lax.optimization_barrier((grads, first, second))
     mate_grads = swap(grads, "seq", 1, 4)
     first = jnp.where((a >> 1) == half, out_weight, first)
     piece = jnp.concatenate([first, second], axis=0)

time: 169 us -> 164 us (0.970)
  the two profiles are of different devices: /device:TPU:128 before, /device:TPU:8 now
where the time goes in v7:
time: 164 us; the launch traced here: 163 us
  starting transfers between devices  82.3 us (50%)
  waiting for transfers between devices  38.4 us (23%)
  Pallas kernels  21.2 us (13%)
  blocking collectives  14 us (9%)
  other arithmetic  3.41 us (2%)
  local copies, waits for them, and re-layouts  2.87 us (2%)
    ppermute x8, starting transfers between devices, swap(): return lax.ppermute(value, axis, [(i, i ^ mask) for i in range(n)])  28.3 us
    all_to_all x4, starting transfers between devices, exchange(): return lax.all_to_all(value, axes, 0, 0, tiled=True)  26.7 us
    ppermute x1, waiting for transfers between devices, shards(): lax.ppermute(other, z, turn2).astype(F32)  19.8 us
    all_to_all x1, blocking collectives, exchange(): return lax.all_to_all(value, axes, 0, 0, tiled=True)  14 us
    ppermute x1, starting transfers between devices, shards(): lax.ppermute(out_weight, z, nearest([d for d in places if d[0] // 2 != d[...  13.9 us
    ppermute x1, starting transfers between devices, shards(): lax.ppermute(other, z, turn2).astype(F32)  9.65 us
    ppermute x8, waiting for transfers between devices, swap(): return lax.ppermute(value, axis, [(i, i ^ mask) for i in range(n)])  7.23 us
    pallas_call x1, Pallas kernels, shards(): call(backward_kernel, arr((4, 192, 768)), 1, 6, 'backward', kv + [pltpu.V...  5.72 us
  transfers between devices with their start and end apart: 16, of which 7 were waited for; matrix products, arithmetic and copies ran while one was open for 2% of the time, Pallas kernels for 9%

profile of v7, /device:TPU:8, one launch (start us, length us, event | category | flops | bytes accessed | tf_op | source)
XLA Modules:
  0.0 163.1 jit_solution(17533083762946147926)
XLA Ops:
  0.6 3.2 %pack.1 = bf16[4,200,768]{2,1,0:T(8,128)(2,1)} custom-call(s32[2]{0:T(128)} %ids.1, bf16[192,1024]{1,0:T(8,128)(2,1)} %bitcast.24, bf16[192,1024]{1,0:T(8,128)(2,1)} %bitcast.25, bf16[192,1024]{1,0:T(8,128)(2,1)} %bitcast.26), custom_call_target="tpu_custom_call" | custom-call | flops 1000 | bytes 1000 | tf_op jit(solution)/shard_map/pack/pallas_call | solution.py:231
  3.8 0.0 copy-start.8
  3.8 0.0 copy-start
  3.8 6.0 %all-to-all-start = ((bf16[4,200,768]{2,1,0:T(8,128)(2,1)}), bf16[4,200,768]{2,1,0:T(8,128)(2,1)S(1)}, u32[]{:S(2)}, u32[]{:S(2)}) async-start(bf16[4,200,768]{2,1,0:T(8,128)(2,1)} %pack.1), calls=%async_computation | async-start | bytes 2457600 | tf_op jit(solution)/shard_map/all_to_all | solution.py:213
  9.9 13.9 %collective-permute-start.1 = (bf16[32,2048]{1,0:T(8,128)(2,1)S(1)}, bf16[32,2048]{1,0:T(8,128)(2,1)S(1)}, u32[]{:S(2)}, u32[]{:S(2)}) collective-permute-start(bf16[32,2048]{1,0:T(8,128)(2,1)S(1)} %copy-done.8), channel_id=1, source_target_pairs={{384,64},{0,320},{416,96},{32,352},{448,128},{64,384},{480,160},{9... | collective-permute-start | bytes 393224 | tf_op jit(solution)/shard_map/ppermute | solution.py:225
  23.8 3.0 %collective-permute-start.2 = (bf16[32,2048]{1,0:T(8,128)(2,1)S(1)}, bf16[32,2048]{1,0:T(8,128)(2,1)S(1)}, u32[]{:S(2)}, u32[]{:S(2)}) collective-permute-start(bf16[32,2048]{1,0:T(8,128)(2,1)S(1)} %copy-done.8), channel_id=1, source_target_pairs={{256,32},{384,288},{0,96},{128,352},{32,0},{160,256},{288,64},{416... | collective-permute-start | bytes 393224 | tf_op jit(solution)/shard_map/ppermute | solution.py:228
  26.8 1.9 %collective-permute-start.6 = (bf16[192,2048]{1,0:T(8,128)(2,1)S(1)}, bf16[192,2048]{1,0:T(8,128)(2,1)}, u32[]{:S(2)}, u32[]{:S(2)}) collective-permute-start(bf16[192,2048]{1,0:T(8,128)(2,1)S(1)} %bitcast.20), channel_id=1, source_target_pairs={{0,128},{128,0},{256,384},{384,256},{1,129},{129,1},{257,385},{385... | collective-permute-start | bytes 2359304 | tf_op jit(solution)/shard_map/ppermute | solution.py:205
  28.8 2.7 %collective-permute-done.1 = bf16[32,2048]{1,0:T(8,128)(2,1)S(1)} collective-permute-done((bf16[32,2048]{1,0:T(8,128)(2,1)S(1)}, bf16[32,2048]{1,0:T(8,128)(2,1)S(1)}, u32[]{:S(2)}, u32[]{:S(2)}) %collective-permute-start.1) | collective-permute-done | bytes 131104 | tf_op jit(solution)/shard_map/ppermute | solution.py:225
  31.4 3.9 %collective-permute-done.2 = bf16[32,2048]{1,0:T(8,128)(2,1)S(1)} collective-permute-done((bf16[32,2048]{1,0:T(8,128)(2,1)S(1)}, bf16[32,2048]{1,0:T(8,128)(2,1)S(1)}, u32[]{:S(2)}, u32[]{:S(2)}) %collective-permute-start.2) | collective-permute-done | bytes 131104 | tf_op jit(solution)/shard_map/ppermute | solution.py:228
  35.3 0.8 fusion
  36.1 4.2 %collective-permute-start.4 = (bf16[64,2048]{1,0:T(8,128)(2,1)S(1)}, bf16[64,2048]{1,0:T(8,128)(2,1)}, u32[]{:S(2)}, u32[]{:S(2)}) collective-permute-start(bf16[64,2048]{1,0:T(8,128)(2,1)S(1)} %get-tuple-element.35), channel_id=1, source_target_pairs={{0,16},{8,24},{16,0},{24,8},{1,17},{9,25},{17,1},{25,9},{2,18},{10... | collective-permute-start | bytes 786440 | tf_op jit(solution)/shard_map/ppermute | solution.py:205
  40.3 3.3 %collective-permute-start.3 = (bf16[64,2048]{1,0:T(8,128)(2,1)S(1)}, bf16[64,2048]{1,0:T(8,128)(2,1)}, u32[]{:S(2)}, u32[]{:S(2)}) collective-permute-start(bf16[64,2048]{1,0:T(8,128)(2,1)S(1)} %get-tuple-element.35), channel_id=1, source_target_pairs={{0,8},{8,0},{16,24},{24,16},{1,9},{9,1},{17,25},{25,17},{2,10},{10... | collective-permute-start | bytes 786440 | tf_op jit(solution)/shard_map/ppermute | solution.py:205
  43.6 2.4 %collective-permute-start.5 = (bf16[64,2048]{1,0:T(8,128)(2,1)S(1)}, bf16[64,2048]{1,0:T(8,128)(2,1)S(1)}, u32[]{:S(2)}, u32[]{:S(2)}) collective-permute-start(bf16[64,2048]{1,0:T(8,128)(2,1)S(1)} %get-tuple-element.35), channel_id=1, source_target_pairs={{0,24},{8,16},{16,8},{24,0},{1,25},{9,17},{17,9},{25,1},{2,26},{10... | collective-permute-start | bytes 786440 | tf_op jit(solution)/shard_map/ppermute | solution.py:205
  45.9 0.0 all-to-all-done.x_all
  45.9 0.0 copy-start.6
  46.0 4.0 %forward.1 = (bf16[384,256]{1,0:T(8,128)(2,1)S(1)}, bf16[384,256]{1,0:T(8,128)(2,1)S(1)}, f32[768,256]{1,0:T(8,128)S(1)}) custom-call(s32[1]{0:T(128)} %bitcast.1.where, bf16[4,200,768]{2,1,0:T(8,128)(2,1)S(1)} %all-to-all-done.x_all), custom_call_target="tpu_custom_call" | custom-call | flops 1000 | bytes 1000 | tf_op jit(solution)/shard_map/forward/pallas_call | solution.py:254
  50.0 0.9 copy-done.2
  50.9 6.9 %collective-permute-start = (bf16[384,256]{1,0:T(8,128)(2,1)S(1)}, bf16[384,256]{1,0:T(8,128)(2,1)S(1)}, u32[]{:S(2)}, u32[]{:S(2)}) collective-permute-start(bf16[384,256]{1,0:T(8,128)(2,1)S(1)} %get-tuple-element.20.o_far), channel_id=1, source_target_pairs={{0,256},{128,384},{256,0},{384,128},{1,257},{129,385},{257,1},{385... | collective-permute-start | bytes 589832 | tf_op jit(solution)/shard_map/ppermute | solution.py:205
  57.8 0.0 collective-permute-done.4
  57.9 0.0 copy-start.7
  57.9 0.7 copy-done.7
  58.6 1.2 pad_maximum_fusion.w_here
  59.8 2.4 %collective-permute-done.o_there = bf16[384,256]{1,0:T(8,128)(2,1)S(1)} collective-permute-done((bf16[384,256]{1,0:T(8,128)(2,1)S(1)}, bf16[384,256]{1,0:T(8,128)(2,1)S(1)}, u32[]{:S(2)}, u32[]{:S(2)}) %collective-permute-start) | collective-permute-done | bytes 196640 | tf_op jit(solution)/shard_map/ppermute | solution.py:205
  62.2 0.0 collective-permute-done.6.mate_ref
  62.2 2.4 %weight.1 = (bf16[4,4,2,32,512]{4,3,2,1,0:T(8,128)(2,1)S(1)}, bf16[4,4,2,32,512]{4,3,2,1,0:T(8,128)(2,1)S(1)}) custom-call(s32[1]{0:T(128)} %bitcast.where, bf16[384,256]{1,0:T(8,128)(2,1)S(1)} %get-tuple-element.19.o_here.o_near, bf16[384,256]{1,0:T(8,128)(2,1)S(1)} %collective-permute-done.o_there, bf16[192,2048]{1,0:T(8,128)(2,1)S(1)} %bitcast.21, ...), custom_call_target="tpu_custom_call" | custom-call | flops 1000 | bytes 1000 | tf_op jit(solution)/shard_map/weight/pallas_call | solution.py:259
  64.7 1.9 %collective-permute-start.7 = (bf16[4,4,2,32,512]{4,3,2,1,0:T(8,128)(2,1)S(1)}, bf16[4,4,2,32,512]{4,3,2,1,0:T(8,128)(2,1)S(1)}, u32[]{:S(2)}, u32[]{:S(2)}) collective-permute-start(bf16[4,4,2,32,512]{4,3,2,1,0:T(8,128)(2,1)S(1)} %get-tuple-element.23), channel_id=1, source_target_pairs={{0,4},{4,0},{1,5},{5,1},{2,6},{6,2},{3,7},{7,3},{8,12},{12,8},{9,1... | collective-permute-start | bytes 3145736 | tf_op jit(solution)/shard_map/ppermute | solution.py:205
  66.6 2.4 %collective-permute-start.10 = (bf16[4,64,2048]{2,1,0:T(8,128)(2,1)S(1)}, bf16[4,64,2048]{2,1,0:T(8,128)(2,1)}, u32[]{:S(2)}, u32[]{:S(2)}) collective-permute-start(bf16[4,64,2048]{2,1,0:T(8,128)(2,1)S(1)} %pad_maximum_fusion.w_here), channel_id=1, source_target_pairs={{0,4},{4,0},{1,5},{5,1},{2,6},{6,2},{3,7},{7,3},{8,12},{12,8},{9,1... | collective-permute-start | bytes 3145736 | tf_op jit(solution)/shard_map/ppermute | solution.py:205
  69.0 0.2 collective-permute-done.7
  69.2 1.4 add_convert_fusion
  70.6 7.4 %all-to-all-start.1 = ((bf16[16,2,32,512]{3,2,1,0:T(8,128)(2,1)}), bf16[16,2,32,512]{3,2,1,0:T(8,128)(2,1)S(1)}, u32[]{:S(2)}, u32[]{:S(2)}) async-start(bf16[16,2,32,512]{3,2,1,0:T(8,128)(2,1)} %bitcast.23), calls=%async_computation.1 | async-start | bytes 2097152 | tf_op jit(solution)/shard_map/all_to_all | solution.py:213
  78.0 0.1 stack.53.where
  78.1 0.0 collective-permute-done.10.w_there
  78.1 1.1 copy-done.1
  79.2 3.2 %project.1 = (bf16[384,256]{1,0:T(8,128)(2,1)S(1)}, bf16[384,256]{1,0:T(8,128)(2,1)S(1)}) custom-call(s32[6]{0:T(128)S(1)} %stack.53.where, bf16[192,2048]{1,0:T(8,128)(2,1)S(1)} %bitcast.22, bf16[192,2048]{1,0:T(8,128)(2,1)} %collective-permute-done.6.mate_ref, bf16[4,64,2048]{2,1,0:T(8,128)(2,1)S(1)} %pad_maximum_fusion.w_here, ...), custom_call_target="tpu_custom_call" | custom-call | flops 1000 | bytes 1000 | tf_op jit(solution)/shard_map/project/pallas_call | solution.py:249
  82.5 5.3 %collective-permute-start.11 = (bf16[384,256]{1,0:T(8,128)(2,1)S(1)}, bf16[384,256]{1,0:T(8,128)(2,1)S(1)}, u32[]{:S(2)}, u32[]{:S(2)}) collective-permute-start(bf16[384,256]{1,0:T(8,128)(2,1)S(1)} %get-tuple-element.27), channel_id=1, source_target_pairs={{0,256},{128,384},{256,0},{384,128},{1,257},{129,385},{257,1},{385... | collective-permute-start | bytes 589832 | tf_op jit(solution)/shard_map/ppermute | solution.py:205
  87.8 4.6 %collective-permute-done.11.g_far = bf16[384,256]{1,0:T(8,128)(2,1)S(1)} collective-permute-done((bf16[384,256]{1,0:T(8,128)(2,1)S(1)}, bf16[384,256]{1,0:T(8,128)(2,1)S(1)}, u32[]{:S(2)}, u32[]{:S(2)}) %collective-permute-start.11) | collective-permute-done | bytes 196640 | tf_op jit(solution)/shard_map/ppermute | solution.py:205
  92.4 5.7 %backward.1 = bf16[4,192,768]{2,1,0:T(8,128)(2,1)} custom-call(s32[1]{0:T(128)} %bitcast.1.where, bf16[4,200,768]{2,1,0:T(8,128)(2,1)S(1)} %all-to-all-done.x_all, bf16[384,256]{1,0:T(8,128)(2,1)S(1)} %get-tuple-element.26.g_near, bf16[384,256]{1,0:T(8,128)(2,1)S(1)} %collective-permute-done.11.g_far, bf16[384,256]{1,0:T(8,128)(2,1)S(1)} %get-tuple-element.19.o_here.o_near, ...), custom_call_target="tpu_custom_call" | custom-call | flops 1000 | bytes 1000 | tf_op jit(solution)/shard_map/backward/pallas_call | solution.py:263
  98.2 9.0 %all-to-all-start.2 = ((bf16[4,192,768]{2,1,0:T(8,128)(2,1)}), bf16[4,192,768]{2,1,0:T(8,128)(2,1)S(1)}, u32[]{:S(2)}, u32[]{:S(2)}) async-start(bf16[4,192,768]{2,1,0:T(8,128)(2,1)} %backward.1), calls=%async_computation.2 | async-start | bytes 2359296 | tf_op jit(solution)/shard_map/all_to_all | solution.py:213
  107.2 0.1 sum.1
  107.3 0.7 collective-permute-start.8
  108.0 9.6 %collective-permute-start.9 = (bf16[32,512]{1,0:T(8,128)(2,1)S(1)}, bf16[32,512]{1,0:T(8,128)(2,1)S(1)}, u32[]{:S(2)}, u32[]{:S(2)}) collective-permute-start(bf16[32,512]{1,0:T(8,128)(2,1)S(1)} %get-tuple-element.25), channel_id=1, source_target_pairs={{0,32},{32,288},{64,160},{96,416},{128,96},{160,352},{192,224},{22... | collective-permute-start | bytes 98312 | tf_op jit(solution)/shard_map/ppermute | solution.py:277
  117.6 19.8 %collective-permute-done.9 = bf16[32,512]{1,0:T(8,128)(2,1)S(1)} collective-permute-done((bf16[32,512]{1,0:T(8,128)(2,1)S(1)}, bf16[32,512]{1,0:T(8,128)(2,1)S(1)}, u32[]{:S(2)}, u32[]{:S(2)}) %collective-permute-start.9) | collective-permute-done | bytes 32800 | tf_op jit(solution)/shard_map/ppermute | solution.py:277
  137.5 14.0 %all_to_all.25.parts = bf16[4,32,512]{2,1,0:T(8,128)(2,1)S(1)} all-to-all(bf16[4,32,512]{2,1,0:T(8,128)(2,1)S(1)} %broadcast_in_dim.18), channel_id=1, replica_groups=mesh['seq'=4,'zh'=4,'y'=4,'c'=2,'dp'=4] {'seq'}, dimensions={0} | all-to-all | bytes 262144 | tf_op jit(solution)/shard_map/all_to_all | solution.py:213
  151.5 0.7 quarter.1
  152.2 4.3 %all-to-all-start.4 = ((bf16[4,32,512]{2,1,0:T(8,128)(2,1)}), bf16[4,32,512]{2,1,0:T(8,128)(2,1)S(1)}, u32[]{:S(2)}, u32[]{:S(2)}) async-start(bf16[4,32,512]{2,1,0:T(8,128)(2,1)} %quarter.1), calls=%async_computation.4 | async-start | bytes 262144 | tf_op jit(solution)/shard_map/all_to_all | solution.py:213
  156.4 1.2 unpack.1
  157.6 4.8 %all-to-all-done.4.parts = bf16[4,32,512]{2,1,0:T(8,128)(2,1)S(1)} async-done(((bf16[4,32,512]{2,1,0:T(8,128)(2,1)}), bf16[4,32,512]{2,1,0:T(8,128)(2,1)S(1)}, u32[]{:S(2)}, u32[]{:S(2)}) %all-to-all-start.4) | async-done | bytes 131104 | tf_op jit(solution)/shard_map/all_to_all | solution.py:213
  162.4 0.7 finish.1
  (19 shorter events, 0.1 us)
Async XLA Ops:
  3.8 6.1 %copy-start.8 = (bf16[32,2048]{1,0:T(8,128)(2,1)S(1)}, bf16[32,2048]{1,0:T(8,128)(2,1)}, u32[]{:S(2)}) copy-start(bf16[32,2048]{1,0:T(8,128)(2,1)} %param.9) | copy-start | bytes 393220
  3.8 23.0 %copy-start = (bf16[1,192,2048]{2,1,0:T(8,128)(2,1)S(1)}, bf16[1,192,2048]{2,1,0:T(8,128)(2,1)}, u32[]{:S(2)}) copy-start(bf16[1,192,2048]{2,1,0:T(8,128)(2,1)} %param.10) | copy-start | bytes 2359300
  3.8 42.1 %all-to-all-start = ((bf16[4,200,768]{2,1,0:T(8,128)(2,1)}), bf16[4,200,768]{2,1,0:T(8,128)(2,1)S(1)}, u32[]{:S(2)}, u32[]{:S(2)}) async-start(bf16[4,200,768]{2,1,0:T(8,128)(2,1)} %pack.1), calls=%async_computation | async-start | bytes 2457600 | tf_op jit(solution)/shard_map/all_to_all | solution.py:213
  9.9 21.5 %collective-permute-start.1 = (bf16[32,2048]{1,0:T(8,128)(2,1)S(1)}, bf16[32,2048]{1,0:T(8,128)(2,1)S(1)}, u32[]{:S(2)}, u32[]{:S(2)}) collective-permute-start(bf16[32,2048]{1,0:T(8,128)(2,1)S(1)} %copy-done.8), channel_id=1, source_target_pairs={{384,64},{0,320},{416,96},{32,352},{448,128},{64,384},{480,160},{9... | collective-permute-start | bytes 393224 | tf_op jit(solution)/shard_map/ppermute | solution.py:225
  23.8 11.6 %collective-permute-start.2 = (bf16[32,2048]{1,0:T(8,128)(2,1)S(1)}, bf16[32,2048]{1,0:T(8,128)(2,1)S(1)}, u32[]{:S(2)}, u32[]{:S(2)}) collective-permute-start(bf16[32,2048]{1,0:T(8,128)(2,1)S(1)} %copy-done.8), channel_id=1, source_target_pairs={{256,32},{384,288},{0,96},{128,352},{32,0},{160,256},{288,64},{416... | collective-permute-start | bytes 393224 | tf_op jit(solution)/shard_map/ppermute | solution.py:228
  26.8 35.4 %collective-permute-start.6 = (bf16[192,2048]{1,0:T(8,128)(2,1)S(1)}, bf16[192,2048]{1,0:T(8,128)(2,1)}, u32[]{:S(2)}, u32[]{:S(2)}) collective-permute-start(bf16[192,2048]{1,0:T(8,128)(2,1)S(1)} %bitcast.20), channel_id=1, source_target_pairs={{0,128},{128,0},{256,384},{384,256},{1,129},{129,1},{257,385},{385... | collective-permute-start | bytes 2359304 | tf_op jit(solution)/shard_map/ppermute | solution.py:205
  36.1 21.7 %collective-permute-start.4 = (bf16[64,2048]{1,0:T(8,128)(2,1)S(1)}, bf16[64,2048]{1,0:T(8,128)(2,1)}, u32[]{:S(2)}, u32[]{:S(2)}) collective-permute-start(bf16[64,2048]{1,0:T(8,128)(2,1)S(1)} %get-tuple-element.35), channel_id=1, source_target_pairs={{0,16},{8,24},{16,0},{24,8},{1,17},{9,25},{17,1},{25,9},{2,18},{10... | collective-permute-start | bytes 786440 | tf_op jit(solution)/shard_map/ppermute | solution.py:205
  40.3 17.6 %collective-permute-start.3 = (bf16[64,2048]{1,0:T(8,128)(2,1)S(1)}, bf16[64,2048]{1,0:T(8,128)(2,1)}, u32[]{:S(2)}, u32[]{:S(2)}) collective-permute-start(bf16[64,2048]{1,0:T(8,128)(2,1)S(1)} %get-tuple-element.35), channel_id=1, source_target_pairs={{0,8},{8,0},{16,24},{24,16},{1,9},{9,1},{17,25},{25,17},{2,10},{10... | collective-permute-start | bytes 786440 | tf_op jit(solution)/shard_map/ppermute | solution.py:205
  43.6 14.3 %collective-permute-start.5 = (bf16[64,2048]{1,0:T(8,128)(2,1)S(1)}, bf16[64,2048]{1,0:T(8,128)(2,1)S(1)}, u32[]{:S(2)}, u32[]{:S(2)}) collective-permute-start(bf16[64,2048]{1,0:T(8,128)(2,1)S(1)} %get-tuple-element.35), channel_id=1, source_target_pairs={{0,24},{8,16},{16,8},{24,0},{1,25},{9,17},{17,9},{25,1},{2,26},{10... | collective-permute-start | bytes 786440 | tf_op jit(solution)/shard_map/ppermute | solution.py:205
  45.9 12.6 %copy-start.6 = (bf16[1,64,2048]{2,1,0:T(8,128)(2,1)S(1)}, bf16[1,64,2048]{2,1,0:T(8,128)(2,1)}, u32[]{:S(2)}) copy-start(bf16[1,64,2048]{2,1,0:T(8,128)(2,1)} %get-tuple-element.34) | copy-start | bytes 786436
  50.0 0.9 copy-start.2
  50.9 13.7 %copy-start.4 = (bf16[384,256]{1,0:T(8,128)(2,1)}, bf16[384,256]{1,0:T(8,128)(2,1)S(1)}, u32[]{:S(2)}) copy-start(bf16[384,256]{1,0:T(8,128)(2,1)S(1)} %get-tuple-element.20.o_far) | copy-start | bytes 589828
  50.9 11.3 %collective-permute-start = (bf16[384,256]{1,0:T(8,128)(2,1)S(1)}, bf16[384,256]{1,0:T(8,128)(2,1)S(1)}, u32[]{:S(2)}, u32[]{:S(2)}) collective-permute-start(bf16[384,256]{1,0:T(8,128)(2,1)S(1)} %get-tuple-element.20.o_far), channel_id=1, source_target_pairs={{0,256},{128,384},{256,0},{384,128},{1,257},{129,385},{257,1},{385... | collective-permute-start | bytes 589832 | tf_op jit(solution)/shard_map/ppermute | solution.py:205
  57.9 0.7 copy-start.7
  64.7 4.6 %collective-permute-start.7 = (bf16[4,4,2,32,512]{4,3,2,1,0:T(8,128)(2,1)S(1)}, bf16[4,4,2,32,512]{4,3,2,1,0:T(8,128)(2,1)S(1)}, u32[]{:S(2)}, u32[]{:S(2)}) collective-permute-start(bf16[4,4,2,32,512]{4,3,2,1,0:T(8,128)(2,1)S(1)} %get-tuple-element.23), channel_id=1, source_target_pairs={{0,4},{4,0},{1,5},{5,1},{2,6},{6,2},{3,7},{7,3},{8,12},{12,8},{9,1... | collective-permute-start | bytes 3145736 | tf_op jit(solution)/shard_map/ppermute | solution.py:205
  66.6 11.5 %collective-permute-start.10 = (bf16[4,64,2048]{2,1,0:T(8,128)(2,1)S(1)}, bf16[4,64,2048]{2,1,0:T(8,128)(2,1)}, u32[]{:S(2)}, u32[]{:S(2)}) collective-permute-start(bf16[4,64,2048]{2,1,0:T(8,128)(2,1)S(1)} %pad_maximum_fusion.w_here), channel_id=1, source_target_pairs={{0,4},{4,0},{1,5},{5,1},{2,6},{6,2},{3,7},{7,3},{8,12},{12,8},{9,1... | collective-permute-start | bytes 3145736 | tf_op jit(solution)/shard_map/ppermute | solution.py:205
  70.6 27.6 %all-to-all-start.1 = ((bf16[16,2,32,512]{3,2,1,0:T(8,128)(2,1)}), bf16[16,2,32,512]{3,2,1,0:T(8,128)(2,1)S(1)}, u32[]{:S(2)}, u32[]{:S(2)}) async-start(bf16[16,2,32,512]{3,2,1,0:T(8,128)(2,1)} %bitcast.23), calls=%async_computation.1 | async-start | bytes 2097152 | tf_op jit(solution)/shard_map/all_to_all | solution.py:213
  78.1 1.1 copy-start.1
  79.2 13.2 %copy-start.3 = (f32[768,256]{1,0:T(8,128)S(1)}, f32[768,256]{1,0:T(8,128)}, u32[]{:S(2)}) copy-start(f32[768,256]{1,0:T(8,128)} %copy-done.2) | copy-start | bytes 2359300
  79.2 13.2 %copy-start.5 = (bf16[384,256]{1,0:T(8,128)(2,1)S(1)}, bf16[384,256]{1,0:T(8,128)(2,1)}, u32[]{:S(2)}) copy-start(bf16[384,256]{1,0:T(8,128)(2,1)} %copy-done.4) | copy-start | bytes 589828
  82.5 10.0 %collective-permute-start.11 = (bf16[384,256]{1,0:T(8,128)(2,1)S(1)}, bf16[384,256]{1,0:T(8,128)(2,1)S(1)}, u32[]{:S(2)}, u32[]{:S(2)}) collective-permute-start(bf16[384,256]{1,0:T(8,128)(2,1)S(1)} %get-tuple-element.27), channel_id=1, source_target_pairs={{0,256},{128,384},{256,0},{384,128},{1,257},{129,385},{257,1},{385... | collective-permute-start | bytes 589832 | tf_op jit(solution)/shard_map/ppermute | solution.py:205
  98.2 39.3 %all-to-all-start.2 = ((bf16[4,192,768]{2,1,0:T(8,128)(2,1)}), bf16[4,192,768]{2,1,0:T(8,128)(2,1)S(1)}, u32[]{:S(2)}, u32[]{:S(2)}) async-start(bf16[4,192,768]{2,1,0:T(8,128)(2,1)} %backward.1), calls=%async_computation.2 | async-start | bytes 2359296 | tf_op jit(solution)/shard_map/all_to_all | solution.py:213
  107.3 10.3 %collective-permute-start.8 = (bf16[32,512]{1,0:T(8,128)(2,1)S(1)}, bf16[32,512]{1,0:T(8,128)(2,1)S(1)}, u32[]{:S(2)}, u32[]{:S(2)}) collective-permute-start(bf16[32,512]{1,0:T(8,128)(2,1)S(1)} %get-tuple-element.24), channel_id=1, source_target_pairs={{0,0},{32,256},{64,128},{96,384},{128,64},{160,320},{192,192},{224... | collective-permute-start | bytes 98312 | tf_op jit(solution)/shard_map/ppermute | solution.py:277
  108.0 29.5 %collective-permute-start.9 = (bf16[32,512]{1,0:T(8,128)(2,1)S(1)}, bf16[32,512]{1,0:T(8,128)(2,1)S(1)}, u32[]{:S(2)}, u32[]{:S(2)}) collective-permute-start(bf16[32,512]{1,0:T(8,128)(2,1)S(1)} %get-tuple-element.25), channel_id=1, source_target_pairs={{0,32},{32,288},{64,160},{96,416},{128,96},{160,352},{192,224},{22... | collective-permute-start | bytes 98312 | tf_op jit(solution)/shard_map/ppermute | solution.py:277
  152.2 10.2 %all-to-all-start.4 = ((bf16[4,32,512]{2,1,0:T(8,128)(2,1)}), bf16[4,32,512]{2,1,0:T(8,128)(2,1)S(1)}, u32[]{:S(2)}, u32[]{:S(2)}) async-start(bf16[4,32,512]{2,1,0:T(8,128)(2,1)} %quarter.1), calls=%async_computation.4 | async-start | bytes 262144 | tf_op jit(solution)/shard_map/all_to_all | solution.py:213

commit v8 on v7

--- a/solution.py
+++ b/solution.py
@@ -1,3 +1,4 @@
+import functools
 import itertools
 import math
 
@@ -101,14 +102,14 @@
     return jnp.where(at < 96, first * 96 + at, second * 96 + (at - 96))
 
 
-def forward_kernel(where, x_all, near, far, lse_ref, k_all, v_all):
+def forward_kernel(first, where, x_all, out, lse_ref, k_all, v_all):
     xs = [x_all.at[where[0] ^ i] for i in range(4)]
     for i, x in enumerate(xs):
         k_all[192 * i : 192 * i + 192] = x[0:192, 256:512]
         v_all[192 * i : 192 * i + 192] = x[0:192, 512:768]
     key_pos = jnp.concatenate([positions(x, (1, 192), 1) for x in xs], axis=1)
-    for i, x in enumerate(xs):
-        rows = slice(192 * i, 192 * i + 192)
+    for i in (first, first + 1):
+        x = xs[i]
         here = slice(192 * (i % 2), 192 * (i % 2) + 192)
         allowed = key_pos <= positions(x, (192, 1), 0)
         for h in range(2):
@@ -119,13 +120,12 @@
             e = jnp.exp(s - top)
             total = jnp.sum(e, axis=1, keepdims=True)
             p = (e * (1.0 / total)).astype(BF16)
-            out = near if i < 2 else far
             out[here, cols] = dot(p, v_all[:, cols], NN).astype(BF16)
-            lse_ref[rows, cols] = jnp.broadcast_to(top + jnp.log(total), (192, HD))
+            lse_ref[here, cols] = jnp.broadcast_to(top + jnp.log(total), (192, HD))
 
 
 def backward_kernel(
-    where, x_all, g_near, g_far, o_near, o_far, lse_ref, home, k_all, v_all, dk, dv
+    where, x_all, g_near, g_far, o_near, o_far, lse_near, lse_far, home, k_all, v_all, dk, dv
 ):
     xs = [x_all.at[where[0] ^ i] for i in range(4)]
     outs = [home.at[where[0] ^ i] for i in range(4)]
@@ -134,7 +134,7 @@
         v_all[192 * i : 192 * i + 192] = x[0:192, 512:768]
     key_pos = jnp.concatenate([positions(x, (1, 192), 1) for x in xs], axis=1)
     for i, x in enumerate(xs):
-        rows = slice(192 * i, 192 * i + 192)
+        lse_ref = lse_near if i < 2 else lse_far
         here = slice(192 * (i % 2), 192 * (i % 2) + 192)
         grads, attended = (g_near, o_near) if i < 2 else (g_far, o_far)
         allowed = key_pos <= positions(x, (192, 1), 0)
@@ -143,7 +143,7 @@
             q = x[0:192, cols]
             g = grads[here, cols]
             s = dot(q, k_all[:, cols], NT) * SCALE
-            p = jnp.exp(jnp.where(allowed, s, -jnp.inf) - lse_ref[rows, HD * h : HD * h + 1])
+            p = jnp.exp(jnp.where(allowed, s, -jnp.inf) - lse_ref[here, HD * h : HD * h + 1])
             delta = jnp.sum(g.astype(F32) * attended[here, cols].astype(F32), axis=1, keepdims=True)
             dp = dot(g, v_all[:, cols], NT)
             ds = (p * (dp - delta)).astype(BF16)
@@ -251,9 +251,13 @@
     )(scalars((a & 1) ^ pair, core, *(y ^ k for k in range(4))), grads, mate_grads, w_here, w_there)
     g_far = swap(g_send, "seq", 2, 4)
     kv = [pltpu.VMEM((768, 256), BF16)] * 2
-    o_near, o_far, lse = call(
-        forward_kernel, [arr((384, 256))] * 2 + [arr((768, 256), F32)], 1, 1, "forward", kv
-    )(scalars(b), rows)
+    halves = [arr((384, 256)), arr((384, 256), F32)]
+    o_far, lse_far = call(functools.partial(forward_kernel, 2), halves, 1, 1, "far", kv)(
+        scalars(b), rows
+    )
+    o_near, lse_near = call(functools.partial(forward_kernel, 0), halves, 1, 1, "near", kv)(
+        scalars(b), rows
+    )
     o_there = swap(o_far, "seq", 2, 4)
     o_there, w_here = lax.optimization_barrier((o_there, w_here))
     keep, send = call(weight_kernel, [arr((4, 4, 2, 32, 512))] * 2, 1, 4, "weight")(
@@ -264,10 +268,10 @@
         backward_kernel,
         arr((4, 192, 768)),
         1,
-        6,
+        7,
         "backward",
         kv + [pltpu.VMEM((768, 256), F32)] * 2,
-    )(scalars(b), rows, g_near, g_far, o_near, o_far, lse)
+    )(scalars(b), rows, g_near, g_far, o_near, o_far, lse_near, lse_far)
     home = exchange(back, "seq")
     both = (keep.astype(F32) + taken.astype(F32)).astype(BF16).reshape(16, 2, 32, 512)
     parts = exchange(both, ("y", "dp"))

time: 164 us -> 163 us (level)
  the two profiles are of different devices: /device:TPU:8 before, /device:TPU:128 now
where the time goes in v8:
time: 163 us; the launch traced here: 162 us
  starting transfers between devices  63.5 us (39%)
  waiting for transfers between devices  54.4 us (33%)
  Pallas kernels  21.4 us (13%)
  blocking collectives  15.9 us (10%)
  other arithmetic  3.38 us (2%)
  local copies, waits for them, and re-layouts  2.71 us (2%)
    ppermute x8, starting transfers between devices, swap(): return lax.ppermute(value, axis, [(i, i ^ mask) for i in range(n)])  23.3 us
    all_to_all x4, starting transfers between devices, exchange(): return lax.all_to_all(value, axes, 0, 0, tiled=True)  19.7 us
    all_to_all x1, blocking collectives, exchange(): return lax.all_to_all(value, axes, 0, 0, tiled=True)  15.9 us
    ppermute x8, waiting for transfers between devices, swap(): return lax.ppermute(value, axis, [(i, i ^ mask) for i in range(n)])  14.6 us
    all_to_all x4, waiting for transfers between devices, exchange(): return lax.all_to_all(value, axes, 0, 0, tiled=True)  11.8 us
    ppermute x1, waiting for transfers between devices, shards(): lax.ppermute(out_weight, z, nearest(places, lambda i, j: i ^ 1 if i // 2...  10.7 us
    ppermute x1, waiting for transfers between devices, shards(): lax.ppermute(own, z, turn).astype(F32)  10.4 us
    ppermute x1, starting transfers between devices, shards(): lax.ppermute(out_weight, z, nearest([d for d in places if d[0] // 2 != d[...  9.08 us
  transfers between devices with their start and end apart: 16, of which 10 were waited for; matrix products, arithmetic and copies ran while one was open for 2% of the time, Pallas kernels for 9%

profile of v8, /device:TPU:128, one launch (start us, length us, event | category | flops | bytes accessed | tf_op | source)
XLA Modules:
  0.0 162.3 jit_solution(14710840528403938159)
XLA Ops:
  0.6 3.2 %pack.1 = bf16[4,200,768]{2,1,0:T(8,128)(2,1)} custom-call(s32[2]{0:T(128)} %ids.1, bf16[192,1024]{1,0:T(8,128)(2,1)} %bitcast.24, bf16[192,1024]{1,0:T(8,128)(2,1)} %bitcast.25, bf16[192,1024]{1,0:T(8,128)(2,1)} %bitcast.26), custom_call_target="tpu_custom_call" | custom-call | flops 1000 | bytes 1000 | tf_op jit(solution)/shard_map/pack/pallas_call | solution.py:231
  3.8 0.0 copy-start
  3.8 6.0 %all-to-all-start = ((bf16[4,200,768]{2,1,0:T(8,128)(2,1)}), bf16[4,200,768]{2,1,0:T(8,128)(2,1)S(1)}, u32[]{:S(2)}, u32[]{:S(2)}) async-start(bf16[4,200,768]{2,1,0:T(8,128)(2,1)} %pack.1), calls=%async_computation | async-start | bytes 2457600 | tf_op jit(solution)/shard_map/all_to_all | solution.py:213
  9.9 9.1 %collective-permute-start.1 = (bf16[32,2048]{1,0:T(8,128)(2,1)S(1)}, bf16[32,2048]{1,0:T(8,128)(2,1)S(1)}, u32[]{:S(2)}, u32[]{:S(2)}) collective-permute-start(bf16[32,2048]{1,0:T(8,128)(2,1)S(1)} %copy-done.10), channel_id=1, source_target_pairs={{384,64},{0,320},{416,96},{32,352},{448,128},{64,384},{480,160},{9... | collective-permute-start | bytes 393224 | tf_op jit(solution)/shard_map/ppermute | solution.py:225
  19.0 5.5 %collective-permute-start.2 = (bf16[32,2048]{1,0:T(8,128)(2,1)S(1)}, bf16[32,2048]{1,0:T(8,128)(2,1)S(1)}, u32[]{:S(2)}, u32[]{:S(2)}) collective-permute-start(bf16[32,2048]{1,0:T(8,128)(2,1)S(1)} %copy-done.10), channel_id=1, source_target_pairs={{256,32},{384,288},{0,96},{128,352},{32,0},{160,256},{288,64},{416... | collective-permute-start | bytes 393224 | tf_op jit(solution)/shard_map/ppermute | solution.py:228
  24.4 1.9 %collective-permute-start.6 = (bf16[192,2048]{1,0:T(8,128)(2,1)S(1)}, bf16[192,2048]{1,0:T(8,128)(2,1)}, u32[]{:S(2)}, u32[]{:S(2)}) collective-permute-start(bf16[192,2048]{1,0:T(8,128)(2,1)S(1)} %bitcast.20), channel_id=1, source_target_pairs={{0,128},{128,0},{256,384},{384,256},{1,129},{129,1},{257,385},{385... | collective-permute-start | bytes 2359304 | tf_op jit(solution)/shard_map/ppermute | solution.py:205
  26.4 10.7 %collective-permute-done.2 = bf16[32,2048]{1,0:T(8,128)(2,1)S(1)} collective-permute-done((bf16[32,2048]{1,0:T(8,128)(2,1)S(1)}, bf16[32,2048]{1,0:T(8,128)(2,1)S(1)}, u32[]{:S(2)}, u32[]{:S(2)}) %collective-permute-start.2) | collective-permute-done | bytes 131104 | tf_op jit(solution)/shard_map/ppermute | solution.py:228
  37.1 0.8 fusion
  37.8 2.2 %collective-permute-start.4 = (bf16[64,2048]{1,0:T(8,128)(2,1)S(1)}, bf16[64,2048]{1,0:T(8,128)(2,1)}, u32[]{:S(2)}, u32[]{:S(2)}) collective-permute-start(bf16[64,2048]{1,0:T(8,128)(2,1)S(1)} %get-tuple-element.37), channel_id=1, source_target_pairs={{0,16},{8,24},{16,0},{24,8},{1,17},{9,25},{17,1},{25,9},{2,18},{10... | collective-permute-start | bytes 786440 | tf_op jit(solution)/shard_map/ppermute | solution.py:205
  40.0 2.6 %collective-permute-start.3 = (bf16[64,2048]{1,0:T(8,128)(2,1)S(1)}, bf16[64,2048]{1,0:T(8,128)(2,1)}, u32[]{:S(2)}, u32[]{:S(2)}) collective-permute-start(bf16[64,2048]{1,0:T(8,128)(2,1)S(1)} %get-tuple-element.37), channel_id=1, source_target_pairs={{0,8},{8,0},{16,24},{24,16},{1,9},{9,1},{17,25},{25,17},{2,10},{10... | collective-permute-start | bytes 786440 | tf_op jit(solution)/shard_map/ppermute | solution.py:205
  42.6 5.0 %collective-permute-start.5 = (bf16[64,2048]{1,0:T(8,128)(2,1)S(1)}, bf16[64,2048]{1,0:T(8,128)(2,1)S(1)}, u32[]{:S(2)}, u32[]{:S(2)}) collective-permute-start(bf16[64,2048]{1,0:T(8,128)(2,1)S(1)} %get-tuple-element.37), channel_id=1, source_target_pairs={{0,24},{8,16},{16,8},{24,0},{1,25},{9,17},{17,9},{25,1},{2,26},{10... | collective-permute-start | bytes 786440 | tf_op jit(solution)/shard_map/ppermute | solution.py:205
  47.7 0.0 copy-start.8
  47.7 2.1 %far.1 = (bf16[384,256]{1,0:T(8,128)(2,1)S(1)}, f32[384,256]{1,0:T(8,128)S(1)}) custom-call(s32[1]{0:T(128)} %bitcast.1.where, bf16[4,200,768]{2,1,0:T(8,128)(2,1)S(1)} %all-to-all-done.x_all), custom_call_target="tpu_custom_call" | custom-call | flops 1000 | bytes 1000 | tf_op jit(solution)/shard_map/far/pallas_call | solution.py:255
  49.8 0.0 copy-start.2
  49.8 1.9 %collective-permute-start = (bf16[384,256]{1,0:T(8,128)(2,1)S(1)}, bf16[384,256]{1,0:T(8,128)(2,1)S(1)}, u32[]{:S(2)}, u32[]{:S(2)}) collective-permute-start(bf16[384,256]{1,0:T(8,128)(2,1)S(1)} %get-tuple-element.21.o_far), channel_id=1, source_target_pairs={{0,256},{128,384},{256,0},{384,128},{1,257},{129,385},{257,1},{385... | collective-permute-start | bytes 589832 | tf_op jit(solution)/shard_map/ppermute | solution.py:205
  51.8 0.9 collective-permute-done.3
  52.7 2.0 %collective-permute-done.5 = bf16[64,2048]{1,0:T(8,128)(2,1)S(1)} collective-permute-done((bf16[64,2048]{1,0:T(8,128)(2,1)S(1)}, bf16[64,2048]{1,0:T(8,128)(2,1)S(1)}, u32[]{:S(2)}, u32[]{:S(2)}) %collective-permute-start.5) | collective-permute-done | bytes 262176 | tf_op jit(solution)/shard_map/ppermute | solution.py:205
  54.7 0.7 copy-done.9
  55.4 1.2 pad_maximum_fusion.w_here
  56.7 2.1 %near.1 = (bf16[384,256]{1,0:T(8,128)(2,1)S(1)}, f32[384,256]{1,0:T(8,128)S(1)}) custom-call(s32[1]{0:T(128)} %bitcast.1.where, bf16[4,200,768]{2,1,0:T(8,128)(2,1)S(1)} %all-to-all-done.x_all), custom_call_target="tpu_custom_call" | custom-call | flops 1000 | bytes 1000 | tf_op jit(solution)/shard_map/near/pallas_call | solution.py:258
  58.8 0.0 copy-start.4
  58.8 0.7 copy-done.4
  59.6 2.3 %collective-permute-done.o_there = bf16[384,256]{1,0:T(8,128)(2,1)S(1)} collective-permute-done((bf16[384,256]{1,0:T(8,128)(2,1)S(1)}, bf16[384,256]{1,0:T(8,128)(2,1)S(1)}, u32[]{:S(2)}, u32[]{:S(2)}) %collective-permute-start) | collective-permute-done | bytes 196640 | tf_op jit(solution)/shard_map/ppermute | solution.py:205
  61.9 2.4 %weight.1 = (bf16[4,4,2,32,512]{4,3,2,1,0:T(8,128)(2,1)S(1)}, bf16[4,4,2,32,512]{4,3,2,1,0:T(8,128)(2,1)S(1)}) custom-call(s32[1]{0:T(128)} %bitcast.where, bf16[384,256]{1,0:T(8,128)(2,1)S(1)} %get-tuple-element.20.o_here.o_near, bf16[384,256]{1,0:T(8,128)(2,1)S(1)} %collective-permute-done.o_there, bf16[192,2048]{1,0:T(8,128)(2,1)S(1)} %bitcast.21, ...), custom_call_target="tpu_custom_call" | custom-call | flops 1000 | bytes 1000 | tf_op jit(solution)/shard_map/weight/pallas_call | solution.py:263
  64.3 1.9 %collective-permute-start.7 = (bf16[4,4,2,32,512]{4,3,2,1,0:T(8,128)(2,1)S(1)}, bf16[4,4,2,32,512]{4,3,2,1,0:T(8,128)(2,1)S(1)}, u32[]{:S(2)}, u32[]{:S(2)}) collective-permute-start(bf16[4,4,2,32,512]{4,3,2,1,0:T(8,128)(2,1)S(1)} %get-tuple-element.24), channel_id=1, source_target_pairs={{0,4},{4,0},{1,5},{5,1},{2,6},{6,2},{3,7},{7,3},{8,12},{12,8},{9,1... | collective-permute-start | bytes 3145736 | tf_op jit(solution)/shard_map/ppermute | solution.py:205
  66.3 2.4 %collective-permute-start.10 = (bf16[4,64,2048]{2,1,0:T(8,128)(2,1)S(1)}, bf16[4,64,2048]{2,1,0:T(8,128)(2,1)}, u32[]{:S(2)}, u32[]{:S(2)}) collective-permute-start(bf16[4,64,2048]{2,1,0:T(8,128)(2,1)S(1)} %pad_maximum_fusion.w_here), channel_id=1, source_target_pairs={{0,4},{4,0},{1,5},{5,1},{2,6},{6,2},{3,7},{7,3},{8,12},{12,8},{9,1... | collective-permute-start | bytes 3145736 | tf_op jit(solution)/shard_map/ppermute | solution.py:205
  68.7 0.2 collective-permute-done.7
  68.9 1.4 add_convert_fusion
  70.3 4.5 %all-to-all-start.1 = ((bf16[16,2,32,512]{3,2,1,0:T(8,128)(2,1)}), bf16[16,2,32,512]{3,2,1,0:T(8,128)(2,1)S(1)}, u32[]{:S(2)}, u32[]{:S(2)}) async-start(bf16[16,2,32,512]{3,2,1,0:T(8,128)(2,1)} %bitcast.23), calls=%async_computation.1 | async-start | bytes 2097152 | tf_op jit(solution)/shard_map/all_to_all | solution.py:213
  74.8 0.1 stack.54.where
  74.9 1.1 copy-done.1
  76.0 3.2 %project.1 = (bf16[384,256]{1,0:T(8,128)(2,1)S(1)}, bf16[384,256]{1,0:T(8,128)(2,1)S(1)}) custom-call(s32[6]{0:T(128)S(1)} %stack.54.where, bf16[192,2048]{1,0:T(8,128)(2,1)S(1)} %bitcast.22, bf16[192,2048]{1,0:T(8,128)(2,1)} %collective-permute-done.6.mate_ref, bf16[4,64,2048]{2,1,0:T(8,128)(2,1)S(1)} %pad_maximum_fusion.w_here, ...), custom_call_target="tpu_custom_call" | custom-call | flops 1000 | bytes 1000 | tf_op jit(solution)/shard_map/project/pallas_call | solution.py:249
  79.2 5.3 %collective-permute-start.11 = (bf16[384,256]{1,0:T(8,128)(2,1)S(1)}, bf16[384,256]{1,0:T(8,128)(2,1)S(1)}, u32[]{:S(2)}, u32[]{:S(2)}) collective-permute-start(bf16[384,256]{1,0:T(8,128)(2,1)S(1)} %get-tuple-element.28), channel_id=1, source_target_pairs={{0,256},{128,384},{256,0},{384,128},{1,257},{129,385},{257,1},{385... | collective-permute-start | bytes 589832 | tf_op jit(solution)/shard_map/ppermute | solution.py:205
  84.6 9.1 %collective-permute-done.11.g_far = bf16[384,256]{1,0:T(8,128)(2,1)S(1)} collective-permute-done((bf16[384,256]{1,0:T(8,128)(2,1)S(1)}, bf16[384,256]{1,0:T(8,128)(2,1)S(1)}, u32[]{:S(2)}, u32[]{:S(2)}) %collective-permute-start.11) | collective-permute-done | bytes 196640 | tf_op jit(solution)/shard_map/ppermute | solution.py:205
  93.7 5.7 %backward.1 = bf16[4,192,768]{2,1,0:T(8,128)(2,1)} custom-call(s32[1]{0:T(128)} %bitcast.1.where, bf16[4,200,768]{2,1,0:T(8,128)(2,1)S(1)} %all-to-all-done.x_all, bf16[384,256]{1,0:T(8,128)(2,1)S(1)} %get-tuple-element.27.g_near, bf16[384,256]{1,0:T(8,128)(2,1)S(1)} %collective-permute-done.11.g_far, bf16[384,256]{1,0:T(8,128)(2,1)S(1)} %get-tuple-element.20.o_here.o_near, ...), custom_call_target="tpu_custom_call" | custom-call | flops 1000 | bytes 1000 | tf_op jit(solution)/shard_map/backward/pallas_call | solution.py:267
  99.4 4.8 %all-to-all-start.2 = ((bf16[4,192,768]{2,1,0:T(8,128)(2,1)}), bf16[4,192,768]{2,1,0:T(8,128)(2,1)S(1)}, u32[]{:S(2)}, u32[]{:S(2)}) async-start(bf16[4,192,768]{2,1,0:T(8,128)(2,1)} %backward.1), calls=%async_computation.2 | async-start | bytes 2359296 | tf_op jit(solution)/shard_map/all_to_all | solution.py:213
  104.2 0.1 sum.1
  104.4 4.1 %collective-permute-start.8 = (bf16[32,512]{1,0:T(8,128)(2,1)S(1)}, bf16[32,512]{1,0:T(8,128)(2,1)S(1)}, u32[]{:S(2)}, u32[]{:S(2)}) collective-permute-start(bf16[32,512]{1,0:T(8,128)(2,1)S(1)} %get-tuple-element.25), channel_id=1, source_target_pairs={{0,0},{32,256},{64,128},{96,384},{128,64},{160,320},{192,192},{224... | collective-permute-start | bytes 98312 | tf_op jit(solution)/shard_map/ppermute | solution.py:281
  108.4 1.9 %collective-permute-start.9 = (bf16[32,512]{1,0:T(8,128)(2,1)S(1)}, bf16[32,512]{1,0:T(8,128)(2,1)S(1)}, u32[]{:S(2)}, u32[]{:S(2)}) collective-permute-start(bf16[32,512]{1,0:T(8,128)(2,1)S(1)} %get-tuple-element.26), channel_id=1, source_target_pairs={{0,32},{32,288},{64,160},{96,416},{128,96},{160,352},{192,224},{22... | collective-permute-start | bytes 98312 | tf_op jit(solution)/shard_map/ppermute | solution.py:281
  110.4 10.4 %collective-permute-done.8 = bf16[32,512]{1,0:T(8,128)(2,1)S(1)} collective-permute-done((bf16[32,512]{1,0:T(8,128)(2,1)S(1)}, bf16[32,512]{1,0:T(8,128)(2,1)S(1)}, u32[]{:S(2)}, u32[]{:S(2)}) %collective-permute-start.8) | collective-permute-done | bytes 32800 | tf_op jit(solution)/shard_map/ppermute | solution.py:281
  120.8 6.9 %collective-permute-done.9 = bf16[32,512]{1,0:T(8,128)(2,1)S(1)} collective-permute-done((bf16[32,512]{1,0:T(8,128)(2,1)S(1)}, bf16[32,512]{1,0:T(8,128)(2,1)S(1)}, u32[]{:S(2)}, u32[]{:S(2)}) %collective-permute-start.9) | collective-permute-done | bytes 32800 | tf_op jit(solution)/shard_map/ppermute | solution.py:281
  127.8 7.0 %all-to-all-done.2.home = bf16[4,192,768]{2,1,0:T(8,128)(2,1)S(1)} async-done(((bf16[4,192,768]{2,1,0:T(8,128)(2,1)}), bf16[4,192,768]{2,1,0:T(8,128)(2,1)S(1)}, u32[]{:S(2)}, u32[]{:S(2)}) %all-to-all-start.2) | async-done | bytes 1179680 | tf_op jit(solution)/shard_map/all_to_all | solution.py:213
  134.7 15.9 %all_to_all.25.parts = bf16[4,32,512]{2,1,0:T(8,128)(2,1)S(1)} all-to-all(bf16[4,32,512]{2,1,0:T(8,128)(2,1)S(1)} %broadcast_in_dim.18), channel_id=1, replica_groups=mesh['seq'=4,'zh'=4,'y'=4,'c'=2,'dp'=4] {'seq'}, dimensions={0} | all-to-all | bytes 262144 | tf_op jit(solution)/shard_map/all_to_all | solution.py:213
  150.6 0.7 quarter.1
  151.3 4.4 %all-to-all-start.4 = ((bf16[4,32,512]{2,1,0:T(8,128)(2,1)}), bf16[4,32,512]{2,1,0:T(8,128)(2,1)S(1)}, u32[]{:S(2)}, u32[]{:S(2)}) async-start(bf16[4,32,512]{2,1,0:T(8,128)(2,1)} %quarter.1), calls=%async_computation.4 | async-start | bytes 262144 | tf_op jit(solution)/shard_map/all_to_all | solution.py:213
  155.7 1.2 unpack.1
  156.8 4.8 %all-to-all-done.4.parts = bf16[4,32,512]{2,1,0:T(8,128)(2,1)S(1)} async-done(((bf16[4,32,512]{2,1,0:T(8,128)(2,1)}), bf16[4,32,512]{2,1,0:T(8,128)(2,1)S(1)}, u32[]{:S(2)}, u32[]{:S(2)}) %all-to-all-start.4) | async-done | bytes 131104 | tf_op jit(solution)/shard_map/all_to_all | solution.py:213
  161.6 0.7 finish.1
  (24 shorter events, 0.1 us)
Async XLA Ops:
  3.8 6.1 %copy-start.10 = (bf16[32,2048]{1,0:T(8,128)(2,1)S(1)}, bf16[32,2048]{1,0:T(8,128)(2,1)}, u32[]{:S(2)}) copy-start(bf16[32,2048]{1,0:T(8,128)(2,1)} %param.9) | copy-start | bytes 393220
  3.8 20.6 %copy-start = (bf16[1,192,2048]{2,1,0:T(8,128)(2,1)S(1)}, bf16[1,192,2048]{2,1,0:T(8,128)(2,1)}, u32[]{:S(2)}) copy-start(bf16[1,192,2048]{2,1,0:T(8,128)(2,1)} %param.10) | copy-start | bytes 2359300
  3.8 43.8 %all-to-all-start = ((bf16[4,200,768]{2,1,0:T(8,128)(2,1)}), bf16[4,200,768]{2,1,0:T(8,128)(2,1)S(1)}, u32[]{:S(2)}, u32[]{:S(2)}) async-start(bf16[4,200,768]{2,1,0:T(8,128)(2,1)} %pack.1), calls=%async_computation | async-start | bytes 2457600 | tf_op jit(solution)/shard_map/all_to_all | solution.py:213
  9.9 16.5 %collective-permute-start.1 = (bf16[32,2048]{1,0:T(8,128)(2,1)S(1)}, bf16[32,2048]{1,0:T(8,128)(2,1)S(1)}, u32[]{:S(2)}, u32[]{:S(2)}) collective-permute-start(bf16[32,2048]{1,0:T(8,128)(2,1)S(1)} %copy-done.10), channel_id=1, source_target_pairs={{384,64},{0,320},{416,96},{32,352},{448,128},{64,384},{480,160},{9... | collective-permute-start | bytes 393224 | tf_op jit(solution)/shard_map/ppermute | solution.py:225
  19.0 18.1 %collective-permute-start.2 = (bf16[32,2048]{1,0:T(8,128)(2,1)S(1)}, bf16[32,2048]{1,0:T(8,128)(2,1)S(1)}, u32[]{:S(2)}, u32[]{:S(2)}) collective-permute-start(bf16[32,2048]{1,0:T(8,128)(2,1)S(1)} %copy-done.10), channel_id=1, source_target_pairs={{256,32},{384,288},{0,96},{128,352},{32,0},{160,256},{288,64},{416... | collective-permute-start | bytes 393224 | tf_op jit(solution)/shard_map/ppermute | solution.py:228
  24.4 37.5 %collective-permute-start.6 = (bf16[192,2048]{1,0:T(8,128)(2,1)S(1)}, bf16[192,2048]{1,0:T(8,128)(2,1)}, u32[]{:S(2)}, u32[]{:S(2)}) collective-permute-start(bf16[192,2048]{1,0:T(8,128)(2,1)S(1)} %bitcast.20), channel_id=1, source_target_pairs={{0,128},{128,0},{256,384},{384,256},{1,129},{129,1},{257,385},{385... | collective-permute-start | bytes 2359304 | tf_op jit(solution)/shard_map/ppermute | solution.py:205
  37.8 14.0 %collective-permute-start.4 = (bf16[64,2048]{1,0:T(8,128)(2,1)S(1)}, bf16[64,2048]{1,0:T(8,128)(2,1)}, u32[]{:S(2)}, u32[]{:S(2)}) collective-permute-start(bf16[64,2048]{1,0:T(8,128)(2,1)S(1)} %get-tuple-element.37), channel_id=1, source_target_pairs={{0,16},{8,24},{16,0},{24,8},{1,17},{9,25},{17,1},{25,9},{2,18},{10... | collective-permute-start | bytes 786440 | tf_op jit(solution)/shard_map/ppermute | solution.py:205
  40.0 12.7 %collective-permute-start.3 = (bf16[64,2048]{1,0:T(8,128)(2,1)S(1)}, bf16[64,2048]{1,0:T(8,128)(2,1)}, u32[]{:S(2)}, u32[]{:S(2)}) collective-permute-start(bf16[64,2048]{1,0:T(8,128)(2,1)S(1)} %get-tuple-element.37), channel_id=1, source_target_pairs={{0,8},{8,0},{16,24},{24,16},{1,9},{9,1},{17,25},{25,17},{2,10},{10... | collective-permute-start | bytes 786440 | tf_op jit(solution)/shard_map/ppermute | solution.py:205
  42.6 12.1 %collective-permute-start.5 = (bf16[64,2048]{1,0:T(8,128)(2,1)S(1)}, bf16[64,2048]{1,0:T(8,128)(2,1)S(1)}, u32[]{:S(2)}, u32[]{:S(2)}) collective-permute-start(bf16[64,2048]{1,0:T(8,128)(2,1)S(1)} %get-tuple-element.37), channel_id=1, source_target_pairs={{0,24},{8,16},{16,8},{24,0},{1,25},{9,17},{17,9},{25,1},{2,26},{10... | collective-permute-start | bytes 786440 | tf_op jit(solution)/shard_map/ppermute | solution.py:205
  47.7 7.8 %copy-start.8 = (bf16[1,64,2048]{2,1,0:T(8,128)(2,1)S(1)}, bf16[1,64,2048]{2,1,0:T(8,128)(2,1)}, u32[]{:S(2)}) copy-start(bf16[1,64,2048]{2,1,0:T(8,128)(2,1)} %get-tuple-element.36) | copy-start | bytes 786436
  49.8 9.0 %copy-start.2 = (f32[384,256]{1,0:T(8,128)}, f32[384,256]{1,0:T(8,128)S(1)}, u32[]{:S(2)}) copy-start(f32[384,256]{1,0:T(8,128)S(1)} %get-tuple-element.30.lse_far) | copy-start | bytes 1179652
  49.8 9.0 %copy-start.6 = (bf16[384,256]{1,0:T(8,128)(2,1)}, bf16[384,256]{1,0:T(8,128)(2,1)S(1)}, u32[]{:S(2)}) copy-start(bf16[384,256]{1,0:T(8,128)(2,1)S(1)} %get-tuple-element.21.o_far) | copy-start | bytes 589828
  49.8 12.1 %collective-permute-start = (bf16[384,256]{1,0:T(8,128)(2,1)S(1)}, bf16[384,256]{1,0:T(8,128)(2,1)S(1)}, u32[]{:S(2)}, u32[]{:S(2)}) collective-permute-start(bf16[384,256]{1,0:T(8,128)(2,1)S(1)} %get-tuple-element.21.o_far), channel_id=1, source_target_pairs={{0,256},{128,384},{256,0},{384,128},{1,257},{129,385},{257,1},{385... | collective-permute-start | bytes 589832 | tf_op jit(solution)/shard_map/ppermute | solution.py:205
  54.7 0.7 copy-start.9
  58.8 0.7 copy-start.4
  64.3 4.6 %collective-permute-start.7 = (bf16[4,4,2,32,512]{4,3,2,1,0:T(8,128)(2,1)S(1)}, bf16[4,4,2,32,512]{4,3,2,1,0:T(8,128)(2,1)S(1)}, u32[]{:S(2)}, u32[]{:S(2)}) collective-permute-start(bf16[4,4,2,32,512]{4,3,2,1,0:T(8,128)(2,1)S(1)} %get-tuple-element.24), channel_id=1, source_target_pairs={{0,4},{4,0},{1,5},{5,1},{2,6},{6,2},{3,7},{7,3},{8,12},{12,8},{9,1... | collective-permute-start | bytes 3145736 | tf_op jit(solution)/shard_map/ppermute | solution.py:205
  66.3 8.6 %collective-permute-start.10 = (bf16[4,64,2048]{2,1,0:T(8,128)(2,1)S(1)}, bf16[4,64,2048]{2,1,0:T(8,128)(2,1)}, u32[]{:S(2)}, u32[]{:S(2)}) collective-permute-start(bf16[4,64,2048]{2,1,0:T(8,128)(2,1)S(1)} %pad_maximum_fusion.w_here), channel_id=1, source_target_pairs={{0,4},{4,0},{1,5},{5,1},{2,6},{6,2},{3,7},{7,3},{8,12},{12,8},{9,1... | collective-permute-start | bytes 3145736 | tf_op jit(solution)/shard_map/ppermute | solution.py:205
  70.3 29.2 %all-to-all-start.1 = ((bf16[16,2,32,512]{3,2,1,0:T(8,128)(2,1)}), bf16[16,2,32,512]{3,2,1,0:T(8,128)(2,1)S(1)}, u32[]{:S(2)}, u32[]{:S(2)}) async-start(bf16[16,2,32,512]{3,2,1,0:T(8,128)(2,1)} %bitcast.23), calls=%async_computation.1 | async-start | bytes 2097152 | tf_op jit(solution)/shard_map/all_to_all | solution.py:213
  74.9 1.1 copy-start.1
  76.0 17.7 %copy-start.3 = (f32[384,256]{1,0:T(8,128)S(1)}, f32[384,256]{1,0:T(8,128)}, u32[]{:S(2)}) copy-start(f32[384,256]{1,0:T(8,128)} %copy-done.2) | copy-start | bytes 1179652
  76.0 17.7 %copy-start.5 = (f32[384,256]{1,0:T(8,128)S(1)}, f32[384,256]{1,0:T(8,128)}, u32[]{:S(2)}) copy-start(f32[384,256]{1,0:T(8,128)} %copy-done.4) | copy-start | bytes 1179652
  76.0 17.7 %copy-start.7 = (bf16[384,256]{1,0:T(8,128)(2,1)S(1)}, bf16[384,256]{1,0:T(8,128)(2,1)}, u32[]{:S(2)}) copy-start(bf16[384,256]{1,0:T(8,128)(2,1)} %copy-done.6) | copy-start | bytes 589828
  79.2 14.5 %collective-permute-start.11 = (bf16[384,256]{1,0:T(8,128)(2,1)S(1)}, bf16[384,256]{1,0:T(8,128)(2,1)S(1)}, u32[]{:S(2)}, u32[]{:S(2)}) collective-permute-start(bf16[384,256]{1,0:T(8,128)(2,1)S(1)} %get-tuple-element.28), channel_id=1, source_target_pairs={{0,256},{128,384},{256,0},{384,128},{1,257},{129,385},{257,1},{385... | collective-permute-start | bytes 589832 | tf_op jit(solution)/shard_map/ppermute | solution.py:205
  99.4 35.3 %all-to-all-start.2 = ((bf16[4,192,768]{2,1,0:T(8,128)(2,1)}), bf16[4,192,768]{2,1,0:T(8,128)(2,1)S(1)}, u32[]{:S(2)}, u32[]{:S(2)}) async-start(bf16[4,192,768]{2,1,0:T(8,128)(2,1)} %backward.1), calls=%async_computation.2 | async-start | bytes 2359296 | tf_op jit(solution)/shard_map/all_to_all | solution.py:213
  104.4 16.4 %collective-permute-start.8 = (bf16[32,512]{1,0:T(8,128)(2,1)S(1)}, bf16[32,512]{1,0:T(8,128)(2,1)S(1)}, u32[]{:S(2)}, u32[]{:S(2)}) collective-permute-start(bf16[32,512]{1,0:T(8,128)(2,1)S(1)} %get-tuple-element.25), channel_id=1, source_target_pairs={{0,0},{32,256},{64,128},{96,384},{128,64},{160,320},{192,192},{224... | collective-permute-start | bytes 98312 | tf_op jit(solution)/shard_map/ppermute | solution.py:281
  108.4 19.3 %collective-permute-start.9 = (bf16[32,512]{1,0:T(8,128)(2,1)S(1)}, bf16[32,512]{1,0:T(8,128)(2,1)S(1)}, u32[]{:S(2)}, u32[]{:S(2)}) collective-permute-start(bf16[32,512]{1,0:T(8,128)(2,1)S(1)} %get-tuple-element.26), channel_id=1, source_target_pairs={{0,32},{32,288},{64,160},{96,416},{128,96},{160,352},{192,224},{22... | collective-permute-start | bytes 98312 | tf_op jit(solution)/shard_map/ppermute | solution.py:281
  151.3 10.4 %all-to-all-start.4 = ((bf16[4,32,512]{2,1,0:T(8,128)(2,1)}), bf16[4,32,512]{2,1,0:T(8,128)(2,1)S(1)}, u32[]{:S(2)}, u32[]{:S(2)}) async-start(bf16[4,32,512]{2,1,0:T(8,128)(2,1)} %quarter.1), calls=%async_computation.4 | async-start | bytes 262144 | tf_op jit(solution)/shard_map/all_to_all | solution.py:213

commit v9 on v8

--- a/solution.py
+++ b/solution.py
@@ -32,7 +32,7 @@
         in_specs=[SMEM] * n_scalar + [VMEM] * n_vector,
         out_specs=jax.tree.map(lambda _: VMEM, outs),
         scratch_shapes=list(scratch),
-        compiler_params=pltpu.CompilerParams(vmem_limit_bytes=40 * 1024 * 1024),
+        compiler_params=pltpu.CompilerParams(vmem_limit_bytes=56 * 1024 * 1024),
         cost_estimate=pl.CostEstimate(flops=1000, bytes_accessed=1000, transcendentals=0),
         name=name,
     )

time: 163 us -> 175 us (1.074)
  the two profiles are of different devices: /device:TPU:128 before, /device:TPU:8 now
where the time goes in v9:
time: 175 us; the launch traced here: 174 us
  starting transfers between devices  80.9 us (46%)
  Pallas kernels  35.3 us (20%)
  waiting for transfers between devices  34.4 us (20%)
  blocking collectives  12.3 us (7%)
  local copies, waits for them, and re-layouts  4.99 us (3%)
  other arithmetic  4.81 us (3%)
    all_to_all x4, starting transfers between devices, exchange(): return lax.all_to_all(value, axes, 0, 0, tiled=True)  27.1 us
    ppermute x8, starting transfers between devices, swap(): return lax.ppermute(value, axis, [(i, i ^ mask) for i in range(n)])  26.6 us
    ppermute x1, waiting for transfers between devices, shards(): lax.ppermute(other, z, turn2).astype(F32)  17.9 us
    ppermute x1, starting transfers between devices, shards(): lax.ppermute(out_weight, z, nearest([d for d in places if d[0] // 2 != d[...  13.9 us
    all_to_all x1, blocking collectives, exchange(): return lax.all_to_all(value, axes, 0, 0, tiled=True)  12.3 us
    ppermute x1, starting transfers between devices, shards(): lax.ppermute(other, z, turn2).astype(F32)  8.9 us
    pallas_call x1, Pallas kernels, shards(): call(backward_kernel, arr((4, 192, 768)), 1, 7, 'backward', kv + [pltpu.V...  7.53 us
    ppermute x8, waiting for transfers between devices, swap(): return lax.ppermute(value, axis, [(i, i ^ mask) for i in range(n)])  6.22 us
  transfers between devices with their start and end apart: 16, of which 6 were waited for; matrix products, arithmetic and copies ran while one was open for 3% of the time, Pallas kernels for 14%

profile of v9, /device:TPU:8, one launch (start us, length us, event | category | flops | bytes accessed | tf_op | source)
XLA Modules:
  0.0 173.7 jit_solution(2621085539662864567)
XLA Ops:
  0.6 3.2 %pack.1 = bf16[4,200,768]{2,1,0:T(8,128)(2,1)} custom-call(s32[2]{0:T(128)} %ids.1, bf16[192,1024]{1,0:T(8,128)(2,1)} %bitcast.23, bf16[192,1024]{1,0:T(8,128)(2,1)} %bitcast.24, bf16[192,1024]{1,0:T(8,128)(2,1)} %bitcast.25), custom_call_target="tpu_custom_call" | custom-call | flops 1000 | bytes 1000 | tf_op jit(solution)/shard_map/pack/pallas_call | solution.py:231
  3.8 0.0 copy-start.10
  3.8 0.0 copy-start.4
  3.8 6.0 %all-to-all-start = ((bf16[4,200,768]{2,1,0:T(8,128)(2,1)}), bf16[4,200,768]{2,1,0:T(8,128)(2,1)S(1)}, u32[]{:S(2)}, u32[]{:S(2)}) async-start(bf16[4,200,768]{2,1,0:T(8,128)(2,1)} %pack.1), calls=%async_computation | async-start | bytes 2457600 | tf_op jit(solution)/shard_map/all_to_all | solution.py:213
  9.9 13.9 %collective-permute-start.1 = (bf16[32,2048]{1,0:T(8,128)(2,1)S(1)}, bf16[32,2048]{1,0:T(8,128)(2,1)S(1)}, u32[]{:S(2)}, u32[]{:S(2)}) collective-permute-start(bf16[32,2048]{1,0:T(8,128)(2,1)S(1)} %copy-done.10), channel_id=1, source_target_pairs={{384,64},{0,320},{416,96},{32,352},{448,128},{64,384},{480,160},{9... | collective-permute-start | bytes 393224 | tf_op jit(solution)/shard_map/ppermute | solution.py:225
  23.8 3.0 %collective-permute-start.2 = (bf16[32,2048]{1,0:T(8,128)(2,1)S(1)}, bf16[32,2048]{1,0:T(8,128)(2,1)}, u32[]{:S(2)}, u32[]{:S(2)}) collective-permute-start(bf16[32,2048]{1,0:T(8,128)(2,1)S(1)} %copy-done.10), channel_id=1, source_target_pairs={{256,32},{384,288},{0,96},{128,352},{32,0},{160,256},{288,64},{416... | collective-permute-start | bytes 393224 | tf_op jit(solution)/shard_map/ppermute | solution.py:228
  26.8 1.9 %collective-permute-start.6 = (bf16[192,2048]{1,0:T(8,128)(2,1)S(1)}, bf16[192,2048]{1,0:T(8,128)(2,1)S(1)}, u32[]{:S(2)}, u32[]{:S(2)}) collective-permute-start(bf16[192,2048]{1,0:T(8,128)(2,1)S(1)} %bitcast.22), channel_id=1, source_target_pairs={{0,128},{128,0},{256,384},{384,256},{1,129},{129,1},{257,385},{385... | collective-permute-start | bytes 2359304 | tf_op jit(solution)/shard_map/ppermute | solution.py:205
  28.8 2.7 %collective-permute-done.1 = bf16[32,2048]{1,0:T(8,128)(2,1)S(1)} collective-permute-done((bf16[32,2048]{1,0:T(8,128)(2,1)S(1)}, bf16[32,2048]{1,0:T(8,128)(2,1)S(1)}, u32[]{:S(2)}, u32[]{:S(2)}) %collective-permute-start.1) | collective-permute-done | bytes 131104 | tf_op jit(solution)/shard_map/ppermute | solution.py:225
  31.4 4.0 %collective-permute-done.2 = bf16[32,2048]{1,0:T(8,128)(2,1)} collective-permute-done((bf16[32,2048]{1,0:T(8,128)(2,1)S(1)}, bf16[32,2048]{1,0:T(8,128)(2,1)}, u32[]{:S(2)}, u32[]{:S(2)}) %collective-permute-start.2) | collective-permute-done | bytes 131104 | tf_op jit(solution)/shard_map/ppermute | solution.py:228
  35.5 1.0 fusion
  36.4 4.2 %collective-permute-start.4 = (bf16[64,2048]{1,0:T(8,128)(2,1)S(1)}, bf16[64,2048]{1,0:T(8,128)(2,1)}, u32[]{:S(2)}, u32[]{:S(2)}) collective-permute-start(bf16[64,2048]{1,0:T(8,128)(2,1)S(1)} %get-tuple-element.37), channel_id=1, source_target_pairs={{0,16},{8,24},{16,0},{24,8},{1,17},{9,25},{17,1},{25,9},{2,18},{10... | collective-permute-start | bytes 786440 | tf_op jit(solution)/shard_map/ppermute | solution.py:205
  40.6 3.3 %collective-permute-start.3 = (bf16[64,2048]{1,0:T(8,128)(2,1)S(1)}, bf16[64,2048]{1,0:T(8,128)(2,1)}, u32[]{:S(2)}, u32[]{:S(2)}) collective-permute-start(bf16[64,2048]{1,0:T(8,128)(2,1)S(1)} %get-tuple-element.37), channel_id=1, source_target_pairs={{0,8},{8,0},{16,24},{24,16},{1,9},{9,1},{17,25},{25,17},{2,10},{10... | collective-permute-start | bytes 786440 | tf_op jit(solution)/shard_map/ppermute | solution.py:205
  43.9 2.4 %collective-permute-start.5 = (bf16[64,2048]{1,0:T(8,128)(2,1)S(1)}, bf16[64,2048]{1,0:T(8,128)(2,1)}, u32[]{:S(2)}, u32[]{:S(2)}) collective-permute-start(bf16[64,2048]{1,0:T(8,128)(2,1)S(1)} %get-tuple-element.37), channel_id=1, source_target_pairs={{0,24},{8,16},{16,8},{24,0},{1,25},{9,17},{17,9},{25,1},{2,26},{10... | collective-permute-start | bytes 786440 | tf_op jit(solution)/shard_map/ppermute | solution.py:205
  46.3 1.0 copy-done
  47.3 4.1 %far.1 = (bf16[384,256]{1,0:T(8,128)(2,1)}, f32[384,256]{1,0:T(8,128)}) custom-call(s32[1]{0:T(128)} %bitcast.1.where, bf16[4,200,768]{2,1,0:T(8,128)(2,1)} %copy-done), custom_call_target="tpu_custom_call" | custom-call | flops 1000 | bytes 1000 | tf_op jit(solution)/shard_map/far/pallas_call | solution.py:255
  51.4 6.9 %collective-permute-start = (bf16[384,256]{1,0:T(8,128)(2,1)}, bf16[384,256]{1,0:T(8,128)(2,1)S(1)}, u32[]{:S(2)}, u32[]{:S(2)}) collective-permute-start(bf16[384,256]{1,0:T(8,128)(2,1)} %get-tuple-element.21.o_far), channel_id=1, source_target_pairs={{0,256},{128,384},{256,0},{384,128},{1,257},{129,385},{257,1},{385... | collective-permute-start | bytes 589832 | tf_op jit(solution)/shard_map/ppermute | solution.py:205
  58.4 0.0 collective-permute-done.4
  58.4 0.0 collective-permute-done.3
  58.4 1.2 pad_maximum_fusion.w_here
  59.7 4.5 %near.1 = (bf16[384,256]{1,0:T(8,128)(2,1)}, f32[384,256]{1,0:T(8,128)}) custom-call(s32[1]{0:T(128)} %bitcast.1.where, bf16[4,200,768]{2,1,0:T(8,128)(2,1)} %copy-done), custom_call_target="tpu_custom_call" | custom-call | flops 1000 | bytes 1000 | tf_op jit(solution)/shard_map/near/pallas_call | solution.py:258
  64.2 0.0 collective-permute-done.o_there
  64.2 0.7 copy-done.9
  64.8 0.3 copy-done.5
  65.1 4.2 %weight.1 = (bf16[4,4,2,32,512]{4,3,2,1,0:T(8,128)(2,1)}, bf16[4,4,2,32,512]{4,3,2,1,0:T(8,128)(2,1)}) custom-call(s32[1]{0:T(128)} %bitcast.where, bf16[384,256]{1,0:T(8,128)(2,1)} %get-tuple-element.20.o_here.o_near, bf16[384,256]{1,0:T(8,128)(2,1)} %copy-done.9, bf16[192,2048]{1,0:T(8,128)(2,1)} %bitcast.20, bf16[192,2048]{1,0:T(8,128)(2,1)} %copy-done.5), custom_call_target="tpu_custom_call" | custom-call | flops 1000 | bytes 1000 | tf_op jit(solution)/shard_map/weight/pallas_call | solution.py:263
  69.3 1.9 %collective-permute-start.7 = (bf16[4,4,2,32,512]{4,3,2,1,0:T(8,128)(2,1)}, bf16[4,4,2,32,512]{4,3,2,1,0:T(8,128)(2,1)S(1)}, u32[]{:S(2)}, u32[]{:S(2)}) collective-permute-start(bf16[4,4,2,32,512]{4,3,2,1,0:T(8,128)(2,1)} %get-tuple-element.24), channel_id=1, source_target_pairs={{0,4},{4,0},{1,5},{5,1},{2,6},{6,2},{3,7},{7,3},{8,12},{12,8},{9,1... | collective-permute-start | bytes 3145736 | tf_op jit(solution)/shard_map/ppermute | solution.py:205
  71.2 2.4 %collective-permute-start.10 = (bf16[4,64,2048]{2,1,0:T(8,128)(2,1)S(1)}, bf16[4,64,2048]{2,1,0:T(8,128)(2,1)S(1)}, u32[]{:S(2)}, u32[]{:S(2)}) collective-permute-start(bf16[4,64,2048]{2,1,0:T(8,128)(2,1)S(1)} %pad_maximum_fusion.w_here), channel_id=1, source_target_pairs={{0,4},{4,0},{1,5},{5,1},{2,6},{6,2},{3,7},{7,3},{8,12},{12,8},{9,1... | collective-permute-start | bytes 3145736 | tf_op jit(solution)/shard_map/ppermute | solution.py:205
  73.7 0.4 collective-permute-done.7
  74.1 2.6 %add_convert_fusion = bf16[4,4,2,32,512]{4,3,2,1,0:T(8,128)(2,1)} fusion(bf16[4,4,2,32,512]{4,3,2,1,0:T(8,128)(2,1)S(1)} %collective-permute-done.7, bf16[4,4,2,32,512]{4,3,2,1,0:T(8,128)(2,1)} %get-tuple-element.23), kind=kLoop, calls=%fused_computation | loop fusion | flops 2097152 | bytes 3145728 | tf_op jit(solution)/shard_map/convert_element_type | solution.py:276
  76.7 7.4 %all-to-all-start.1 = ((bf16[16,2,32,512]{3,2,1,0:T(8,128)(2,1)}), bf16[16,2,32,512]{3,2,1,0:T(8,128)(2,1)S(1)}, u32[]{:S(2)}, u32[]{:S(2)}) async-start(bf16[16,2,32,512]{3,2,1,0:T(8,128)(2,1)} %bitcast.10), calls=%async_computation.1 | async-start | bytes 2097152 | tf_op jit(solution)/shard_map/all_to_all | solution.py:213
  84.1 0.7 stack.54.where
  84.7 1.0 copy-done.6
  85.7 4.4 %project.1 = (bf16[384,256]{1,0:T(8,128)(2,1)}, bf16[384,256]{1,0:T(8,128)(2,1)}) custom-call(s32[6]{0:T(128)} %stack.54.where, bf16[192,2048]{1,0:T(8,128)(2,1)} %bitcast.21, bf16[192,2048]{1,0:T(8,128)(2,1)} %copy-done.5, bf16[4,64,2048]{2,1,0:T(8,128)(2,1)} %copy-done.3, bf16[4,64,2048]{2,1,0:T(8,128)(2,1)} %copy-done.6), custom_call_target="tpu_custom_call" | custom-call | flops 1000 | bytes 1000 | tf_op jit(solution)/shard_map/project/pallas_call | solution.py:249
  90.1 3.6 %collective-permute-start.11 = (bf16[384,256]{1,0:T(8,128)(2,1)}, bf16[384,256]{1,0:T(8,128)(2,1)S(1)}, u32[]{:S(2)}, u32[]{:S(2)}) collective-permute-start(bf16[384,256]{1,0:T(8,128)(2,1)} %get-tuple-element.28), channel_id=1, source_target_pairs={{0,256},{128,384},{256,0},{384,128},{1,257},{129,385},{257,1},{385... | collective-permute-start | bytes 589832 | tf_op jit(solution)/shard_map/ppermute | solution.py:205
  93.7 5.8 %collective-permute-done.11.g_far = bf16[384,256]{1,0:T(8,128)(2,1)S(1)} collective-permute-done((bf16[384,256]{1,0:T(8,128)(2,1)}, bf16[384,256]{1,0:T(8,128)(2,1)S(1)}, u32[]{:S(2)}, u32[]{:S(2)}) %collective-permute-start.11) | collective-permute-done | bytes 196640 | tf_op jit(solution)/shard_map/ppermute | solution.py:205
  99.5 0.7 copy-done.8
  100.1 7.5 %backward.1 = bf16[4,192,768]{2,1,0:T(8,128)(2,1)} custom-call(s32[1]{0:T(128)} %bitcast.1.where, bf16[4,200,768]{2,1,0:T(8,128)(2,1)} %copy-done, bf16[384,256]{1,0:T(8,128)(2,1)} %get-tuple-element.27.g_near, bf16[384,256]{1,0:T(8,128)(2,1)} %copy-done.8, bf16[384,256]{1,0:T(8,128)(2,1)} %get-tuple-element.20.o_here.o_near, ...), custom_call_target="tpu_custom_call" | custom-call | flops 1000 | bytes 1000 | tf_op jit(solution)/shard_map/backward/pallas_call | solution.py:267
  107.7 9.5 %all-to-all-start.2 = ((bf16[4,192,768]{2,1,0:T(8,128)(2,1)}), bf16[4,192,768]{2,1,0:T(8,128)(2,1)S(1)}, u32[]{:S(2)}, u32[]{:S(2)}) async-start(bf16[4,192,768]{2,1,0:T(8,128)(2,1)} %backward.1), calls=%async_computation.2 | async-start | bytes 2359296 | tf_op jit(solution)/shard_map/all_to_all | solution.py:213
  117.1 2.0 %sum.1 = (bf16[32,512]{1,0:T(8,128)(2,1)}, bf16[32,512]{1,0:T(8,128)(2,1)}) custom-call(bf16[16,2,32,512]{3,2,1,0:T(8,128)(2,1)} %copy-done.2), custom_call_target="tpu_custom_call" | custom-call | flops 1000 | bytes 1000 | tf_op jit(solution)/shard_map/sum/pallas_call | solution.py:278
  119.1 1.4 collective-permute-start.8
  120.5 8.9 %collective-permute-start.9 = (bf16[32,512]{1,0:T(8,128)(2,1)}, bf16[32,512]{1,0:T(8,128)(2,1)S(1)}, u32[]{:S(2)}, u32[]{:S(2)}) collective-permute-start(bf16[32,512]{1,0:T(8,128)(2,1)} %get-tuple-element.26), channel_id=1, source_target_pairs={{0,32},{32,288},{64,160},{96,416},{128,96},{160,352},{192,224},{22... | collective-permute-start | bytes 98312 | tf_op jit(solution)/shard_map/ppermute | solution.py:281
  129.4 17.9 %collective-permute-done.9 = bf16[32,512]{1,0:T(8,128)(2,1)S(1)} collective-permute-done((bf16[32,512]{1,0:T(8,128)(2,1)}, bf16[32,512]{1,0:T(8,128)(2,1)S(1)}, u32[]{:S(2)}, u32[]{:S(2)}) %collective-permute-start.9) | collective-permute-done | bytes 32800 | tf_op jit(solution)/shard_map/ppermute | solution.py:281
  147.4 12.3 %all_to_all.25.parts = bf16[4,32,512]{2,1,0:T(8,128)(2,1)} all-to-all(bf16[4,32,512]{2,1,0:T(8,128)(2,1)S(1)} %broadcast_in_dim.18), channel_id=1, replica_groups=mesh['seq'=4,'zh'=4,'y'=4,'c'=2,'dp'=4] {'seq'}, dimensions={0} | all-to-all | bytes 262144 | tf_op jit(solution)/shard_map/all_to_all | solution.py:213
  159.7 1.6 quarter.1
  161.3 4.2 %all-to-all-start.4 = ((bf16[4,32,512]{2,1,0:T(8,128)(2,1)}), bf16[4,32,512]{2,1,0:T(8,128)(2,1)S(1)}, u32[]{:S(2)}, u32[]{:S(2)}) async-start(bf16[4,32,512]{2,1,0:T(8,128)(2,1)} %quarter.1), calls=%async_computation.4 | async-start | bytes 262144 | tf_op jit(solution)/shard_map/all_to_all | solution.py:213
  165.5 2.3 %unpack.1 = (bf16[192,1024]{1,0:T(8,128)(2,1)}, bf16[192,1024]{1,0:T(8,128)(2,1)}, bf16[192,1024]{1,0:T(8,128)(2,1)}) custom-call(bf16[4,192,768]{2,1,0:T(8,128)(2,1)} %copy-done.1), custom_call_target="tpu_custom_call" | custom-call | flops 1000 | bytes 1000 | tf_op jit(solution)/shard_map/unpack/pallas_call | solution.py:286
  167.8 3.7 %all-to-all-done.4.parts = bf16[4,32,512]{2,1,0:T(8,128)(2,1)S(1)} async-done(((bf16[4,32,512]{2,1,0:T(8,128)(2,1)}), bf16[4,32,512]{2,1,0:T(8,128)(2,1)S(1)}, u32[]{:S(2)}, u32[]{:S(2)}) %all-to-all-start.4) | async-done | bytes 131104 | tf_op jit(solution)/shard_map/all_to_all | solution.py:213
  171.5 0.6 copy-done.7
  172.1 1.6 finish.1
  (24 shorter events, 0.1 us)
Async XLA Ops:
  3.8 6.1 %copy-start.10 = (bf16[32,2048]{1,0:T(8,128)(2,1)S(1)}, bf16[32,2048]{1,0:T(8,128)(2,1)}, u32[]{:S(2)}) copy-start(bf16[32,2048]{1,0:T(8,128)(2,1)} %param.9) | copy-start | bytes 393220
  3.8 23.0 %copy-start.4 = (bf16[1,192,2048]{2,1,0:T(8,128)(2,1)S(1)}, bf16[1,192,2048]{2,1,0:T(8,128)(2,1)}, u32[]{:S(2)}) copy-start(bf16[1,192,2048]{2,1,0:T(8,128)(2,1)} %param.10) | copy-start | bytes 2359300
  3.8 42.4 %all-to-all-start = ((bf16[4,200,768]{2,1,0:T(8,128)(2,1)}), bf16[4,200,768]{2,1,0:T(8,128)(2,1)S(1)}, u32[]{:S(2)}, u32[]{:S(2)}) async-start(bf16[4,200,768]{2,1,0:T(8,128)(2,1)} %pack.1), calls=%async_computation | async-start | bytes 2457600 | tf_op jit(solution)/shard_map/all_to_all | solution.py:213
  9.9 21.5 %collective-permute-start.1 = (bf16[32,2048]{1,0:T(8,128)(2,1)S(1)}, bf16[32,2048]{1,0:T(8,128)(2,1)S(1)}, u32[]{:S(2)}, u32[]{:S(2)}) collective-permute-start(bf16[32,2048]{1,0:T(8,128)(2,1)S(1)} %copy-done.10), channel_id=1, source_target_pairs={{384,64},{0,320},{416,96},{32,352},{448,128},{64,384},{480,160},{9... | collective-permute-start | bytes 393224 | tf_op jit(solution)/shard_map/ppermute | solution.py:225
  23.8 11.7 %collective-permute-start.2 = (bf16[32,2048]{1,0:T(8,128)(2,1)S(1)}, bf16[32,2048]{1,0:T(8,128)(2,1)}, u32[]{:S(2)}, u32[]{:S(2)}) collective-permute-start(bf16[32,2048]{1,0:T(8,128)(2,1)S(1)} %copy-done.10), channel_id=1, source_target_pairs={{256,32},{384,288},{0,96},{128,352},{32,0},{160,256},{288,64},{416... | collective-permute-start | bytes 393224 | tf_op jit(solution)/shard_map/ppermute | solution.py:228
  26.8 37.3 %collective-permute-start.6 = (bf16[192,2048]{1,0:T(8,128)(2,1)S(1)}, bf16[192,2048]{1,0:T(8,128)(2,1)S(1)}, u32[]{:S(2)}, u32[]{:S(2)}) collective-permute-start(bf16[192,2048]{1,0:T(8,128)(2,1)S(1)} %bitcast.22), channel_id=1, source_target_pairs={{0,128},{128,0},{256,384},{384,256},{1,129},{129,1},{257,385},{385... | collective-permute-start | bytes 2359304 | tf_op jit(solution)/shard_map/ppermute | solution.py:205
  36.4 22.0 %collective-permute-start.4 = (bf16[64,2048]{1,0:T(8,128)(2,1)S(1)}, bf16[64,2048]{1,0:T(8,128)(2,1)}, u32[]{:S(2)}, u32[]{:S(2)}) collective-permute-start(bf16[64,2048]{1,0:T(8,128)(2,1)S(1)} %get-tuple-element.37), channel_id=1, source_target_pairs={{0,16},{8,24},{16,0},{24,8},{1,17},{9,25},{17,1},{25,9},{2,18},{10... | collective-permute-start | bytes 786440 | tf_op jit(solution)/shard_map/ppermute | solution.py:205
  40.6 17.8 %collective-permute-start.3 = (bf16[64,2048]{1,0:T(8,128)(2,1)S(1)}, bf16[64,2048]{1,0:T(8,128)(2,1)}, u32[]{:S(2)}, u32[]{:S(2)}) collective-permute-start(bf16[64,2048]{1,0:T(8,128)(2,1)S(1)} %get-tuple-element.37), channel_id=1, source_target_pairs={{0,8},{8,0},{16,24},{24,16},{1,9},{9,1},{17,25},{25,17},{2,10},{10... | collective-permute-start | bytes 786440 | tf_op jit(solution)/shard_map/ppermute | solution.py:205
  43.9 14.5 %collective-permute-start.5 = (bf16[64,2048]{1,0:T(8,128)(2,1)S(1)}, bf16[64,2048]{1,0:T(8,128)(2,1)}, u32[]{:S(2)}, u32[]{:S(2)}) collective-permute-start(bf16[64,2048]{1,0:T(8,128)(2,1)S(1)} %get-tuple-element.37), channel_id=1, source_target_pairs={{0,24},{8,16},{16,8},{24,0},{1,25},{9,17},{17,9},{25,1},{2,26},{10... | collective-permute-start | bytes 786440 | tf_op jit(solution)/shard_map/ppermute | solution.py:205
  46.3 1.1 copy-start
  51.4 12.7 %collective-permute-start = (bf16[384,256]{1,0:T(8,128)(2,1)}, bf16[384,256]{1,0:T(8,128)(2,1)S(1)}, u32[]{:S(2)}, u32[]{:S(2)}) collective-permute-start(bf16[384,256]{1,0:T(8,128)(2,1)} %get-tuple-element.21.o_far), channel_id=1, source_target_pairs={{0,256},{128,384},{256,0},{384,128},{1,257},{129,385},{257,1},{385... | collective-permute-start | bytes 589832 | tf_op jit(solution)/shard_map/ppermute | solution.py:205
  59.7 11.6 %copy-start.3 = (bf16[4,64,2048]{2,1,0:T(8,128)(2,1)}, bf16[4,64,2048]{2,1,0:T(8,128)(2,1)S(1)}, u32[]{:S(2)}) copy-start(bf16[4,64,2048]{2,1,0:T(8,128)(2,1)S(1)} %pad_maximum_fusion.w_here) | copy-start | bytes 3145732
  64.2 0.7 copy-start.9
  64.2 0.9 copy-start.5
  69.3 4.8 %collective-permute-start.7 = (bf16[4,4,2,32,512]{4,3,2,1,0:T(8,128)(2,1)}, bf16[4,4,2,32,512]{4,3,2,1,0:T(8,128)(2,1)S(1)}, u32[]{:S(2)}, u32[]{:S(2)}) collective-permute-start(bf16[4,4,2,32,512]{4,3,2,1,0:T(8,128)(2,1)} %get-tuple-element.24), channel_id=1, source_target_pairs={{0,4},{4,0},{1,5},{5,1},{2,6},{6,2},{3,7},{7,3},{8,12},{12,8},{9,1... | collective-permute-start | bytes 3145736 | tf_op jit(solution)/shard_map/ppermute | solution.py:205
  71.2 13.5 %collective-permute-start.10 = (bf16[4,64,2048]{2,1,0:T(8,128)(2,1)S(1)}, bf16[4,64,2048]{2,1,0:T(8,128)(2,1)S(1)}, u32[]{:S(2)}, u32[]{:S(2)}) collective-permute-start(bf16[4,64,2048]{2,1,0:T(8,128)(2,1)S(1)} %pad_maximum_fusion.w_here), channel_id=1, source_target_pairs={{0,4},{4,0},{1,5},{5,1},{2,6},{6,2},{3,7},{7,3},{8,12},{12,8},{9,1... | collective-permute-start | bytes 3145736 | tf_op jit(solution)/shard_map/ppermute | solution.py:205
  76.7 31.0 %all-to-all-start.1 = ((bf16[16,2,32,512]{3,2,1,0:T(8,128)(2,1)}), bf16[16,2,32,512]{3,2,1,0:T(8,128)(2,1)S(1)}, u32[]{:S(2)}, u32[]{:S(2)}) async-start(bf16[16,2,32,512]{3,2,1,0:T(8,128)(2,1)} %bitcast.10), calls=%async_computation.1 | async-start | bytes 2097152 | tf_op jit(solution)/shard_map/all_to_all | solution.py:213
  84.7 1.0 copy-start.6
  90.1 9.4 %collective-permute-start.11 = (bf16[384,256]{1,0:T(8,128)(2,1)}, bf16[384,256]{1,0:T(8,128)(2,1)S(1)}, u32[]{:S(2)}, u32[]{:S(2)}) collective-permute-start(bf16[384,256]{1,0:T(8,128)(2,1)} %get-tuple-element.28), channel_id=1, source_target_pairs={{0,256},{128,384},{256,0},{384,128},{1,257},{129,385},{257,1},{385... | collective-permute-start | bytes 589832 | tf_op jit(solution)/shard_map/ppermute | solution.py:205
  99.5 0.7 copy-start.8
  107.7 9.5 %copy-start.2 = (bf16[16,2,32,512]{3,2,1,0:T(8,128)(2,1)}, bf16[16,2,32,512]{3,2,1,0:T(8,128)(2,1)S(1)}, u32[]{:S(2)}) copy-start(bf16[16,2,32,512]{3,2,1,0:T(8,128)(2,1)S(1)} %all-to-all-done.1.parts) | copy-start | bytes 3145732
  107.7 39.7 %all-to-all-start.2 = ((bf16[4,192,768]{2,1,0:T(8,128)(2,1)}), bf16[4,192,768]{2,1,0:T(8,128)(2,1)S(1)}, u32[]{:S(2)}, u32[]{:S(2)}) async-start(bf16[4,192,768]{2,1,0:T(8,128)(2,1)} %backward.1), calls=%async_computation.2 | async-start | bytes 2359296 | tf_op jit(solution)/shard_map/all_to_all | solution.py:213
  119.1 10.3 %collective-permute-start.8 = (bf16[32,512]{1,0:T(8,128)(2,1)}, bf16[32,512]{1,0:T(8,128)(2,1)S(1)}, u32[]{:S(2)}, u32[]{:S(2)}) collective-permute-start(bf16[32,512]{1,0:T(8,128)(2,1)} %get-tuple-element.25), channel_id=1, source_target_pairs={{0,0},{32,256},{64,128},{96,384},{128,64},{160,320},{192,192},{224... | collective-permute-start | bytes 98312 | tf_op jit(solution)/shard_map/ppermute | solution.py:281
  120.5 26.8 %collective-permute-start.9 = (bf16[32,512]{1,0:T(8,128)(2,1)}, bf16[32,512]{1,0:T(8,128)(2,1)S(1)}, u32[]{:S(2)}, u32[]{:S(2)}) collective-permute-start(bf16[32,512]{1,0:T(8,128)(2,1)} %get-tuple-element.26), channel_id=1, source_target_pairs={{0,32},{32,288},{64,160},{96,416},{128,96},{160,352},{192,224},{22... | collective-permute-start | bytes 98312 | tf_op jit(solution)/shard_map/ppermute | solution.py:281
  147.3 18.2 %copy-start.1 = (bf16[4,192,768]{2,1,0:T(8,128)(2,1)}, bf16[4,192,768]{2,1,0:T(8,128)(2,1)S(1)}, u32[]{:S(2)}) copy-start(bf16[4,192,768]{2,1,0:T(8,128)(2,1)S(1)} %all-to-all-done.2.home) | copy-start | bytes 3538948
  161.3 10.2 %all-to-all-start.4 = ((bf16[4,32,512]{2,1,0:T(8,128)(2,1)}), bf16[4,32,512]{2,1,0:T(8,128)(2,1)S(1)}, u32[]{:S(2)}, u32[]{:S(2)}) async-start(bf16[4,32,512]{2,1,0:T(8,128)(2,1)} %quarter.1), calls=%async_computation.4 | async-start | bytes 262144 | tf_op jit(solution)/shard_map/all_to_all | solution.py:213
  171.5 0.6 copy-start.7
